TPU v7x, 32 devices: a whole 2x2x4 slice. The times are simulated.
32 devices in a mesh: grp: 2 (over y), frm: 4 (over z), row: 4 (over x, core).
Axes of the slice: x: 2, y: 2, z: 4, core: 2. Of those that a mesh axis runs over, the one named last changes fastest.
Arguments:
- hidden_in: bfloat16 [512, 16, 2240], P('row', ('grp', 'frm')), parts along dimension 1, may hold values from -6 to 6
- norm_gain: float32 [2240], replicated, may hold values from 0.1 to 1.9
- query_key_value_weight: bfloat16 [2240, 3, 2240], P(None, None, 'row'), may hold values from -0.125 to 0.125
- head_gain: float32 [2240], P('row'), may hold values from 0.1 to 1.9
- output_matrix: bfloat16 [2240, 2240], P('row'), may hold values from -0.125 to 0.125
- block_end: int32 [16], P(('grp', 'frm')), parts along dimension 0, may hold values from 0 to 7, as said below
Outputs:
- mixed_out: bfloat16 [512, 16, 2240], P('row', ('grp', 'frm')), parts along dimension 1
There are 2 independent parts, one for each index of `grp`. A program takes and returns all parts, laid end to end along the dimension named above; an argument that names none is the same for every part. Nothing has to cross between parts.
Inputs may be any that keep to these rules, and one draw needn't show every extreme that they name: `block_end`: entries never fall from one frame to the next; each entry is at least its frame's index, and frames with equal entries form a block of consecutive frames; a block never holds frames of two different runs of 2 frames (f // 2 differs), and the last frame of every such run ends a block.
All inputs are finite; a program needn't handle non-finite values.
Results may differ from a plain program's by a relative error of at most 0.015.
Values may be sent and summed in bfloat16 or wider, within the bound.
No kernel may reach another device: no remote copies, remote signals or barrier semaphores. Data moves between devices by JAX's collectives and lax.ppermute only.
A program may use at most 64 MiB of HBM per device.

v0:
```python
import jax
import jax.numpy as jnp
from jax import lax
from jax.experimental import pallas as pl
from jax.experimental.pallas import tpu as pltpu
from jax.sharding import PartitionSpec as P


HD = 112
EPS = 1e-06
F32 = jnp.float32
BF16 = jnp.bfloat16


def cost(flops, nbytes):
    return pl.CostEstimate(flops=int(flops), bytes_accessed=int(nbytes), transcendentals=0)


def params(mib=48):
    return pltpu.CompilerParams(vmem_limit_bytes=mib << 20)


def dot(a, b):
    return jnp.dot(a, b, preferred_element_type=F32)


def dot_nt(a, b):
    return lax.dot_general(a, b, (((1,), (1,)), ((), ())), preferred_element_type=F32)


VMEM = pl.BlockSpec(memory_space=pltpu.VMEM)


def scaled(x_ref, gain_ref):
    x = x_ref[...].astype(F32)
    mean = jnp.mean(x * x, axis=0, keepdims=True)
    return (x * lax.rsqrt(mean + EPS) * gain_ref[...]).astype(BF16)


def project(blocks, where, gain, weights, states=None, frames=1, first=0, last=False):
    n = len(blocks)
    here, per_frame = len(where), len(where[0])
    features, lanes = blocks[0].shape[-2:]
    group = weights.shape[0] // 3
    heads = group // HD
    width = per_frame * lanes
    total = here * width
    begin = group if last else 0

    def kernel(*refs):
        x_refs, rest = refs[:n], refs[n:]
        gain_ref, w_ref, rest = rest[0], rest[1], rest[2:]
        if states is not None:
            old, rest = rest[0], rest[1:]
        state, second, normed, part = rest[0], rest[1], rest[-2], rest[-1]
        if last:
            normed = rest[2]
        for f in range(here):
            for b, (k, i) in enumerate(where[f]):
                block = x_refs[k] if i is None else x_refs[k].at[i]
                at = f * width + b * lanes
                normed[:, at : at + lanes] = scaled(block, gain_ref)
        part[...] = jnp.dot(w_ref[begin:, :], normed[...], preferred_element_type=F32).astype(BF16)
        keys, values = group - begin, 2 * group - begin
        for f in range(here):
            cols = slice(f * width, (f + 1) * width)
            for h in range(heads):
                k = jnp.maximum(part[keys + h * HD : keys + (h + 1) * HD, cols], 0.0)
                v = part[values + h * HD : values + (h + 1) * HD, cols]
                rows = slice(h * HD, (h + 1) * HD)
                add = dot_nt(v, k)
                state[first + f, rows, :] = add if states is None else old[first + f, rows, :] + add
        if states is not None:
            for f in range(frames):
                if not first <= f < first + here:
                    state[f] = old[f]
        if last:
            own = state[0]
            for f in range(1, frames):
                own = own + state[f]
            second[...] = own.astype(BF16)
        else:
            for f in range(here):
                second[f] = jnp.maximum(part[:group, f * width : (f + 1) * width], 0.0)

    out_shape = [jax.ShapeDtypeStruct((frames, group, HD), F32)]
    scratch = [pltpu.VMEM((3 * group - begin, total), BF16)]
    if last:
        out_shape.append(jax.ShapeDtypeStruct((group, HD), BF16))
        out_shape.append(jax.ShapeDtypeStruct((features, total), BF16))
    else:
        out_shape.append(jax.ShapeDtypeStruct((here, group, width), BF16))
        scratch = [pltpu.VMEM((features, total), BF16)] + scratch
    given = [*blocks, gain, weights] + ([] if states is None else [states])
    return pl.pallas_call(
        kernel,
        in_specs=[VMEM] * len(given),
        out_specs=[VMEM] * len(out_shape),
        out_shape=out_shape,
        scratch_shapes=scratch,
        compiler_params=params(),
        cost_estimate=cost(2 * (3 * group - begin) * features * total, 2 * features * total),
        name="project",
    )(*given)


def query(normed, weights):
    features, total = normed.shape
    group = weights.shape[0] // 3

    def kernel(x_ref, w_ref, q_ref):
        q_ref[0] = jnp.maximum(dot(w_ref[:group, :], x_ref[...]), 0.0).astype(BF16)

    return pl.pallas_call(
        kernel,
        in_specs=[VMEM] * 2,
        out_specs=VMEM,
        out_shape=jax.ShapeDtypeStruct((1, group, total), BF16),
        compiler_params=params(),
        cost_estimate=cost(2 * group * features * total, 2 * features * total),
        name="query",
    )(normed, weights)


def attend(end, states, priors, head_gain, queries, lanes):
    frames, group, _ = states.shape
    heads = group // HD
    n_prior, n_q = len(priors), len(queries)
    places, slabs = [], 0
    seen = {}
    for k, (array, where, first) in enumerate(queries):
        for f, i in where.items():
            for b in range(array.shape[-1] // lanes):
                places.append((k, f, i, b, first + b))
                seen[first + b] = True
    slabs = len(seen)

    def kernel(end_ref, state_ref, gain_ref, *rest):
        prior_refs, q_refs = rest[:n_prior], rest[n_prior : n_prior + n_q]
        outs = rest[n_prior + n_q :]
        prior = jnp.zeros((group, HD), F32)
        for p in prior_refs:
            prior = prior + p[...].astype(F32)
        block = []
        for f in range(frames):
            total = prior
            for g in range(frames):
                seen_by = (end_ref[g] <= end_ref[f]).astype(F32)
                total = total + seen_by * state_ref[g]
            block.append(total.astype(BF16))
        for k, f, i, b, slab in places:
            for h in range(heads):
                rows = slice(h * HD, (h + 1) * HD)
                a = dot(block[f][rows], q_refs[k][i, rows, b * lanes : (b + 1) * lanes])
                mean = jnp.mean(a * a, axis=0, keepdims=True)
                outs[slab][f, rows, :] = (a * lax.rsqrt(mean + EPS) * gain_ref[rows]).astype(BF16)

    return pl.pallas_call(
        kernel,
        in_specs=[pl.BlockSpec(memory_space=pltpu.SMEM)]
        + [pl.BlockSpec(memory_space=pltpu.VMEM)] * (2 + n_prior + n_q),
        out_specs=[pl.BlockSpec(memory_space=pltpu.VMEM)] * slabs,
        out_shape=[jax.ShapeDtypeStruct((frames, group, lanes), BF16)] * slabs,
        compiler_params=params(),
        cost_estimate=cost(2 * group * HD * frames * slabs * lanes, 4 * group * frames * slabs * lanes),
        name="attend",
    )(end, states, head_gain, *priors, *[a for a, _, _ in queries])


def turn(pieces):
    n = len(pieces)
    group, width = pieces[0].shape

    def kernel(*refs):
        for k in range(n):
            refs[n][:, k * group : (k + 1) * group] = refs[k][...].T

    return pl.pallas_call(
        kernel,
        in_specs=[VMEM] * n,
        out_specs=VMEM,
        out_shape=jax.ShapeDtypeStruct((width, n * group), BF16),
        compiler_params=params(),
        cost_estimate=cost(0, 4 * n * group * width),
        name="turn",
    )(*pieces)


def mix(weights, heads_out, start, stop, dtype):
    n = len(heads_out)
    frames, group, lanes = heads_out[0].shape

    def kernel(w_ref, *refs):
        out, both = refs[n], refs[n + 1]
        for k in range(n):
            for f in range(frames):
                both[k * group : (k + 1) * group, f * lanes : (f + 1) * lanes] = refs[k][f]
        total = dot(w_ref[start:stop, :], both[...])
        for f in range(frames):
            out[f] = total[:, f * lanes : (f + 1) * lanes].astype(dtype)

    return pl.pallas_call(
        kernel,
        in_specs=[VMEM] * (1 + n),
        out_specs=VMEM,
        out_shape=jax.ShapeDtypeStruct((frames, stop - start, lanes), dtype),
        scratch_shapes=[pltpu.VMEM((n * group, frames * lanes), BF16)],
        compiler_params=params(),
        cost_estimate=cost(2 * n * (stop - start) * group * frames * lanes, 2 * n * (stop - start) * group),
        name="mix",
    )(weights, *heads_out)


def finish(buffer, own, arrived, start, whole_shape):
    n = len(arrived)
    frames, rows, lanes = arrived[0].shape

    def kernel(*refs):
        own_ref, got, out, staged, sem = refs[0], refs[1 : 1 + n], refs[-3], refs[-2], refs[-1]
        copies = []
        for f in range(frames):
            total = own_ref[f, start : start + rows, :]
            for g in got:
                total = total + g[f].astype(F32)
            staged[f] = total.astype(BF16)
            copies.append(pltpu.make_async_copy(staged.at[f], out.at[f, pl.ds(start, rows), :], sem.at[f]))
            copies[-1].start()
        for c in copies:
            c.wait()

    given = [own, *arrived] + ([] if buffer is None else [buffer])
    return pl.pallas_call(
        kernel,
        in_specs=[VMEM] * (1 + n) + ([] if buffer is None else [pl.BlockSpec(memory_space=pl.ANY)]),
        out_specs=pl.BlockSpec(memory_space=pl.ANY),
        out_shape=jax.ShapeDtypeStruct(whole_shape, BF16),
        scratch_shapes=[pltpu.VMEM((frames, rows, lanes), BF16), pltpu.SemaphoreType.DMA((frames,))],
        input_output_aliases={} if buffer is None else {1 + n: 0},
        compiler_params=params(),
        cost_estimate=cost(0, 8 * frames * rows * lanes),
        name="finish",
    )(*given)


CUTS = (0.0, 0.25, 0.75, 1.0)


def per_device(n_row, n_frm, hidden_in, norm_gain, qkv_weight, head_gain, output_matrix, block_end):
    def swap(v, k):
        return lax.ppermute(v, "row", [(i, i ^ k) for i in range(n_row)])

    def shift(v, s):
        return lax.ppermute(v, "frm", [(i, i + s) for i in range(n_frm - s)])

    lanes, frames, features = hidden_in.shape
    tokens = jnp.transpose(hidden_in, (1, 2, 0))
    weights = jnp.transpose(qkv_weight, (1, 2, 0)).reshape(-1, features)
    gain = norm_gain.reshape(features, 1)
    out_gain = head_gain.reshape(-1, 1)

    pairs = n_row // 2
    crossed = {}
    for f in range(frames):
        for k in range(1, pairs):
            crossed[k, f] = swap(tokens[f], 2 * k)
    sibling = swap(tokens, 1)
    passed = {key: swap(v, 1) for key, v in crossed.items()}

    where = [[(0, f), (1, f)] for f in range(frames)]
    states, near_q = project([tokens, sibling], where, gain, weights, None, frames)
    turned = turn([output_matrix, swap(output_matrix, 1)])
    states, turned = lax.optimization_barrier((states, turned))
    queries = []
    for f in range(frames):
        for k in range(1, pairs):
            last = f == frames - 1 and k == pairs - 1
            blocks = [crossed[k, f], passed[k, f]]
            out = project(blocks, [[(0, None), (1, None)]], gain, weights, states, frames, f, last)
            states = out[0]
            if last:
                own_sum, normed = out[1:]
            else:
                queries.append((out[1], {f: 0}, 2 * k))
    if n_frm <= 4:
        priors = [shift(own_sum, s) for s in range(1, n_frm)]
    else:
        total, s = shift(own_sum.astype(F32), 1), 1
        while s < n_frm:
            total, s = total + shift(total, s), 2 * s
        priors = [total]
    queries.append((query(normed, weights), {frames - 1: 0}, n_row - 2))
    queries.append((near_q, {f: f for f in range(frames)}, 0))
    heads_out = attend(block_end, states, priors, out_gain, queries, lanes)

    got = {}
    for k in list(range(1, pairs)) + [0]:
        got[k] = swap(heads_out[2 * k + 1], 1)
    width = output_matrix.shape[1]
    cuts = [int(c * width) // 16 * 16 for c in CUTS]
    spans = list(zip(cuts[:-1], cuts[1:]))
    arrived = []
    for i, (start, stop) in enumerate(spans):
        arrived.append([])
        for k in range(1, pairs):
            part = mix(turned, (heads_out[2 * k], got[k]), start, stop, BF16)
            arrived[i].append(swap(part, 2 * k))
    own = mix(turned, (heads_out[0], got[0]), 0, width, F32)
    out = None
    for (start, stop), parts in zip(spans, arrived):
        out = finish(out, own, parts, start, (frames, width, lanes))
    return jnp.transpose(out, (2, 0, 1))


def solution(mesh):
    placed = (
        P("row", ("grp", "frm"), None),
        P(),
        P(None, None, "row"),
        P("row"),
        P("row", None),
        P(("grp", "frm")),
    )

    def body(*args):
        return per_device(mesh.shape["row"], mesh.shape["frm"], *args)

    return jax.shard_map(
        body, mesh=mesh, in_specs=placed, out_specs=P("row", ("grp", "frm"), None), check_vma=False
    )
```

profile of v0, /device:TPU:0, one launch (start us, length us, event | category | flops | bytes accessed | tf_op | source)
XLA Modules:
  0.0 105.5 jit_solution(11496979935513682322)
XLA Ops:
  0.0 0.5 collective-permute-start.1
  0.5 0.0 copy-start.3
  0.5 0.1 collective-permute-start
  0.6 1.3 %slice_bitcast_fusion = (bf16[2240,128]{1,0:T(8,128)(2,1)S(1)}, bf16[2240,128]{1,0:T(8,128)(2,1)S(1)}) fusion(bf16[2,2240,128]{2,1,0:T(8,128)(2,1)} %bitcast.12), kind=kLoop, calls=%fused_computation | loop fusion | bytes 2293760 | tf_op jit(solution)/shard_map/squeeze | solution.py:265
  1.9 0.0 copy-start.1
  1.9 3.0 %collective-permute-start.4 = (bf16[2240,128]{1,0:T(8,128)(2,1)S(1)}, bf16[2240,128]{1,0:T(8,128)(2,1)S(1)}, u32[]{:S(2)}, u32[]{:S(2)}) collective-permute-start(bf16[2240,128]{1,0:T(8,128)(2,1)S(1)} %get-tuple-element.31), channel_id=1, source_target_pairs={{0,2},{1,3},{2,0},{3,1},{4,6},{5,7},{6,4},{7,5},{8,10},{9,11},{10,... | collective-permute-start | bytes 1720328 | tf_op jit(solution)/shard_map/ppermute | solution.py:250
  4.9 0.1 collective-permute-start.2
  4.9 13.8 %collective-permute-done.4.refs_0_ = bf16[2240,128]{1,0:T(8,128)(2,1)S(1)} collective-permute-done((bf16[2240,128]{1,0:T(8,128)(2,1)S(1)}, bf16[2240,128]{1,0:T(8,128)(2,1)S(1)}, u32[]{:S(2)}, u32[]{:S(2)}) %collective-permute-start.4) | collective-permute-done | bytes 573472 | tf_op jit(solution)/shard_map/ppermute | solution.py:250
  18.7 0.0 collective-permute-start.5
  18.7 11.7 %collective-permute-done.2.refs_0_ = bf16[2240,128]{1,0:T(8,128)(2,1)S(1)} collective-permute-done((bf16[2240,128]{1,0:T(8,128)(2,1)S(1)}, bf16[2240,128]{1,0:T(8,128)(2,1)S(1)}, u32[]{:S(2)}, u32[]{:S(2)}) %collective-permute-start.2) | collective-permute-done | bytes 573472 | tf_op jit(solution)/shard_map/ppermute | solution.py:250
  30.4 0.0 collective-permute-start.3
  30.4 0.0 copy-done.3
  30.4 0.3 reshape.12.refs_2_
  30.7 0.0 collective-permute-done.refs_1_
  30.7 0.0 copy-done.1
  30.7 0.0 copy-start
  30.8 8.5 %project.3 = (f32[2,560,112]{2,1,0:T(8,128)S(1)}, bf16[2,560,256]{2,1,0:T(8,128)(2,1)S(1)}) custom-call(bf16[2,2240,128]{2,1,0:T(8,128)(2,1)S(1)} %bitcast.13, bf16[2,2240,128]{2,1,0:T(8,128)(2,1)S(1)} %collective-permute-done.refs_1_, f32[2240,1]{1,0:T(8,128)S(1)} %reshape.12.refs_2_, bf16[1680,2240]{1,0:T(8,128)(2,1)} %bitcast.14), custom_call_target="tpu_custom_call" | custom-call | flops 3853516800 | bytes 2293760 | tf_op jit(solution)/shard_map/project/pallas_call | solution.py:95
  39.2 0.0 collective-permute-done.1.refs_1_
  39.3 0.0 copy-done
  39.3 4.8 %turn.1.w_ref = bf16[2240,1120]{1,0:T(8,128)(2,1)} custom-call(bf16[560,2240]{1,0:T(8,128)(2,1)S(1)} %copy-done, bf16[560,2240]{1,0:T(8,128)(2,1)S(1)} %collective-permute-done.1.refs_1_), custom_call_target="tpu_custom_call" | custom-call | bytes 10035200 | tf_op jit(solution)/shard_map/turn/pallas_call | solution.py:178
  44.1 0.0 collective-permute-done.5.refs_1_
  44.1 6.1 %project.4 = (f32[2,560,112]{2,1,0:T(8,128)S(1)}, bf16[1,560,256]{2,1,0:T(8,128)(2,1)S(1)}) custom-call(bf16[2240,128]{1,0:T(8,128)(2,1)S(1)} %collective-permute-done.4.refs_0_, bf16[2240,128]{1,0:T(8,128)(2,1)S(1)} %collective-permute-done.5.refs_1_, f32[2240,1]{1,0:T(8,128)S(1)} %reshape.12.refs_2_, bf16[1680,2240]{1,0:T(8,128)(2,1)} %bitcast.15, ...), custom_call_target="tpu_custom_call" | custom-call | flops 1926758400 | bytes 1146880 | tf_op jit(solution)/shard_map/project/pallas_call | solution.py:95
  50.1 0.0 collective-permute-done.3.refs_1_
  50.1 0.0 copy-start.4
  50.1 0.0 slice-start
  50.1 5.8 %project.5 = (f32[2,560,112]{2,1,0:T(8,128)S(1)}, bf16[560,112]{1,0:T(8,128)(2,1)S(1)}, bf16[2240,256]{1,0:T(8,128)(2,1)S(1)}) custom-call(bf16[2240,128]{1,0:T(8,128)(2,1)S(1)} %collective-permute-done.2.refs_0_, bf16[2240,128]{1,0:T(8,128)(2,1)S(1)} %collective-permute-done.3.refs_1_, f32[2240,1]{1,0:T(8,128)S(1)} %reshape.12.refs_2_, ...), custom_call_target="tpu_custom_call" | custom-call | flops 1284505600 | bytes 1146880 | tf_op jit(solution)/shard_map/project/pallas_call | solution.py:95
  55.9 3.7 %collective-permute-start.6 = (bf16[560,112]{1,0:T(8,128)(2,1)S(1)}, bf16[560,112]{1,0:T(8,128)(2,1)S(1)}, u32[]{:S(2)}, u32[]{:S(2)}) collective-permute-start(bf16[560,112]{1,0:T(8,128)(2,1)S(1)} %get-tuple-element.23), channel_id=1, source_target_pairs={{0,4},{4,8},{8,12},{1,5},{5,9},{9,13},{2,6},{6,10},{10,14},{3,7},{... | collective-permute-start | bytes 376328 | tf_op jit(solution)/shard_map/ppermute | solution.py:253
  59.7 4.5 %collective-permute-start.7 = (bf16[560,112]{1,0:T(8,128)(2,1)S(1)}, bf16[560,112]{1,0:T(8,128)(2,1)S(1)}, u32[]{:S(2)}, u32[]{:S(2)}) collective-permute-start(bf16[560,112]{1,0:T(8,128)(2,1)S(1)} %get-tuple-element.23), channel_id=1, source_target_pairs={{0,8},{4,12},{1,9},{5,13},{2,10},{6,14},{3,11},{7,15},{16,24},{20,... | collective-permute-start | bytes 376328 | tf_op jit(solution)/shard_map/ppermute | solution.py:253
  64.2 1.3 %collective-permute-start.8 = (bf16[560,112]{1,0:T(8,128)(2,1)S(1)}, bf16[560,112]{1,0:T(8,128)(2,1)S(1)}, u32[]{:S(2)}, u32[]{:S(2)}) collective-permute-start(bf16[560,112]{1,0:T(8,128)(2,1)S(1)} %get-tuple-element.23), channel_id=1, source_target_pairs={{0,12},{1,13},{2,14},{3,15},{16,28},{17,29},{18,30},{19,31}} | collective-permute-start | bytes 376328 | tf_op jit(solution)/shard_map/ppermute | solution.py:253
  65.5 0.0 copy-done.4
  65.5 0.1 reshape.13.gain_ref
  65.6 0.0 copy-start.2
  65.6 0.0 slice-start.1
  65.6 4.1 %query.1.rest_4_ = bf16[1,560,256]{2,1,0:T(8,128)(2,1)S(1)} custom-call(bf16[2240,256]{1,0:T(8,128)(2,1)S(1)} %get-tuple-element.25.x_ref, bf16[1680,2240]{1,0:T(8,128)(2,1)} %bitcast.17), custom_call_target="tpu_custom_call" | custom-call | flops 642252800 | bytes 1146880 | tf_op jit(solution)/shard_map/query/pallas_call | solution.py:114
  69.8 0.0 collective-permute-done.6.rest_0_
  69.8 0.0 collective-permute-done.7.rest_1_
  69.8 0.9 collective-permute-done.8.rest_2_
  70.7 0.0 copy-done.2
  70.7 1.5 %attend.1 = (bf16[2,560,128]{2,1,0:T(8,128)(2,1)S(1)}, bf16[2,560,128]{2,1,0:T(8,128)(2,1)S(1)}, bf16[2,560,128]{2,1,0:T(8,128)(2,1)S(1)}, bf16[2,560,128]{2,1,0:T(8,128)(2,1)S(1)}) custom-call(s32[2]{0:T(128)S(1)} %copy-done.2, f32[2,560,112]{2,1,0:T(8,128)S(1)} %get-tuple-element.22.state_ref, f32[560,1]{1,0:T(8,128)S(1)} %reshape.13.gain_ref, ...), custom_call_target="tpu_custom_call" | custom-call | flops 128450560 | bytes 2293760 | tf_op jit(solution)/shard_map/attend/pallas_call | solution.py:158
  72.1 0.1 collective-permute-start.10
  72.2 1.6 %collective-permute-done.10.refs_1_ = bf16[2,560,128]{2,1,0:T(8,128)(2,1)S(1)} collective-permute-done((bf16[2,560,128]{2,1,0:T(8,128)(2,1)S(1)}, bf16[2,560,128]{2,1,0:T(8,128)(2,1)S(1)}, u32[]{:S(2)}, u32[]{:S(2)}) %collective-permute-start.10) | collective-permute-done | bytes 286752 | tf_op jit(solution)/shard_map/ppermute | solution.py:250
  73.8 3.4 %mix.6 = bf16[2,1120,128]{2,1,0:T(8,128)(2,1)S(1)} custom-call(bf16[2240,1120]{1,0:T(8,128)(2,1)} %turn.1.w_ref, bf16[2,560,128]{2,1,0:T(8,128)(2,1)S(1)} %get-tuple-element.29.refs_0_, bf16[2,560,128]{2,1,0:T(8,128)(2,1)S(1)} %collective-permute-done.10.refs_1_), custom_call_target="tpu_custom_call" | custom-call | flops 642252800 | bytes 2508800 | tf_op jit(solution)/shard_map/mix/pallas_call | solution.py:202
  77.2 1.6 %collective-permute-start.12 = (bf16[2,1120,128]{2,1,0:T(8,128)(2,1)S(1)}, bf16[2,1120,128]{2,1,0:T(8,128)(2,1)S(1)}, u32[]{:S(2)}, u32[]{:S(2)}) collective-permute-start(bf16[2,1120,128]{2,1,0:T(8,128)(2,1)S(1)} %mix.6), channel_id=1, source_target_pairs={{0,2},{1,3},{2,0},{3,1},{4,6},{5,7},{6,4},{7,5},{8,10},{9,11},{10,... | collective-permute-start | bytes 1720328 | tf_op jit(solution)/shard_map/ppermute | solution.py:250
  78.8 0.0 collective-permute-start.9
  78.8 0.0 slice-done
  78.8 0.0 slice-done.1
  78.8 0.6 mix.7
  79.4 0.6 collective-permute-start.13
  80.0 0.6 mix.5
  80.6 1.6 %collective-permute-start.11 = (bf16[2,560,128]{2,1,0:T(8,128)(2,1)S(1)}, bf16[2,560,128]{2,1,0:T(8,128)(2,1)S(1)}, u32[]{:S(2)}, u32[]{:S(2)}) collective-permute-start(bf16[2,560,128]{2,1,0:T(8,128)(2,1)S(1)} %mix.5), channel_id=1, source_target_pairs={{0,2},{1,3},{2,0},{3,1},{4,6},{5,7},{6,4},{7,5},{8,10},{9,11},{10,... | collective-permute-start | bytes 860168 | tf_op jit(solution)/shard_map/ppermute | solution.py:250
  82.2 0.0 collective-permute-done.9.refs_1_
  82.2 4.2 %mix.4.refs_0_ = f32[2,2240,128]{2,1,0:T(8,128)S(1)} custom-call(bf16[2240,1120]{1,0:T(8,128)(2,1)} %turn.1.w_ref, bf16[2,560,128]{2,1,0:T(8,128)(2,1)S(1)} %get-tuple-element.27.refs_0_, bf16[2,560,128]{2,1,0:T(8,128)(2,1)S(1)} %collective-permute-done.9.refs_1_), custom_call_target="tpu_custom_call" | custom-call | flops 1284505600 | bytes 5017600 | tf_op jit(solution)/shard_map/mix/pallas_call | solution.py:202
  86.4 12.9 %collective-permute-done.13.refs_1_ = bf16[2,560,128]{2,1,0:T(8,128)(2,1)S(1)} collective-permute-done((bf16[2,560,128]{2,1,0:T(8,128)(2,1)S(1)}, bf16[2,560,128]{2,1,0:T(8,128)(2,1)S(1)}, u32[]{:S(2)}, u32[]{:S(2)}) %collective-permute-start.13) | collective-permute-done | bytes 286752 | tf_op jit(solution)/shard_map/ppermute | solution.py:250
  99.3 0.7 finish.3.refs_2_
  100.1 0.0 collective-permute-done.12.refs_1_
  100.1 0.9 finish.4.refs_2_
  100.9 3.7 %collective-permute-done.11.refs_1_ = bf16[2,560,128]{2,1,0:T(8,128)(2,1)S(1)} collective-permute-done((bf16[2,560,128]{2,1,0:T(8,128)(2,1)S(1)}, bf16[2,560,128]{2,1,0:T(8,128)(2,1)S(1)}, u32[]{:S(2)}, u32[]{:S(2)}) %collective-permute-start.11) | collective-permute-done | bytes 286752 | tf_op jit(solution)/shard_map/ppermute | solution.py:250
  104.6 0.7 finish.5
  (1 shorter events, 0.0 us)
Async XLA Ops:
  0.0 39.3 %collective-permute-start.1 = (bf16[560,2240]{1,0:T(8,128)(2,1)}, bf16[560,2240]{1,0:T(8,128)(2,1)S(1)}, u32[]{:S(2)}, u32[]{:S(2)}) collective-permute-start(bf16[560,2240]{1,0:T(8,128)(2,1)} %refs_0_.1), channel_id=1, source_target_pairs={{0,1},{1,0},{2,3},{3,2},{4,5},{5,4},{6,7},{7,6},{8,9},{9,8},{10,11... | collective-permute-start | bytes 7526408 | tf_op jit(solution)/shard_map/ppermute | solution.py:250
  0.5 29.9 %copy-start.3 = (f32[2240]{0:T(1024)S(1)}, f32[2240]{0:T(1024)}, u32[]{:S(2)}) copy-start(f32[2240]{0:T(1024)} %param.7) | copy-start | bytes 26884
  0.5 30.2 %collective-permute-start = (bf16[2,2240,128]{2,1,0:T(8,128)(2,1)}, bf16[2,2240,128]{2,1,0:T(8,128)(2,1)S(1)}, u32[]{:S(2)}, u32[]{:S(2)}) collective-permute-start(bf16[2,2240,128]{2,1,0:T(8,128)(2,1)} %bitcast.11), channel_id=1, source_target_pairs={{0,1},{1,0},{2,3},{3,2},{4,5},{5,4},{6,7},{7,6},{8,9},{9,8},{10,11... | collective-permute-start | bytes 3440648 | tf_op jit(solution)/shard_map/ppermute | solution.py:250
  1.9 28.9 %copy-start.1 = (bf16[128,2,2240]{0,2,1:T(8,128)(2,1)S(1)}, bf16[128,2,2240]{0,2,1:T(8,128)(2,1)}, u32[]{:S(2)}) copy-start(bf16[128,2,2240]{0,2,1:T(8,128)(2,1)} %param.6) | copy-start | bytes 3440644
  1.9 16.8 %collective-permute-start.4 = (bf16[2240,128]{1,0:T(8,128)(2,1)S(1)}, bf16[2240,128]{1,0:T(8,128)(2,1)S(1)}, u32[]{:S(2)}, u32[]{:S(2)}) collective-permute-start(bf16[2240,128]{1,0:T(8,128)(2,1)S(1)} %get-tuple-element.31), channel_id=1, source_target_pairs={{0,2},{1,3},{2,0},{3,1},{4,6},{5,7},{6,4},{7,5},{8,10},{9,11},{10,... | collective-permute-start | bytes 1720328 | tf_op jit(solution)/shard_map/ppermute | solution.py:250
  4.9 25.5 %collective-permute-start.2 = (bf16[2240,128]{1,0:T(8,128)(2,1)S(1)}, bf16[2240,128]{1,0:T(8,128)(2,1)S(1)}, u32[]{:S(2)}, u32[]{:S(2)}) collective-permute-start(bf16[2240,128]{1,0:T(8,128)(2,1)S(1)} %get-tuple-element.32), channel_id=1, source_target_pairs={{0,2},{1,3},{2,0},{3,1},{4,6},{5,7},{6,4},{7,5},{8,10},{9,11},{10,... | collective-permute-start | bytes 1720328 | tf_op jit(solution)/shard_map/ppermute | solution.py:250
  18.7 25.4 %collective-permute-start.5 = (bf16[2240,128]{1,0:T(8,128)(2,1)S(1)}, bf16[2240,128]{1,0:T(8,128)(2,1)S(1)}, u32[]{:S(2)}, u32[]{:S(2)}) collective-permute-start(bf16[2240,128]{1,0:T(8,128)(2,1)S(1)} %collective-permute-done.4.refs_0_), channel_id=1, source_target_pairs={{0,1},{1,0},{2,3},{3,2},{4,5},{5,4},{6,7},{7,6},{8,9},{9,8},{10,11... | collective-permute-start | bytes 1720328 | tf_op jit(solution)/shard_map/ppermute | solution.py:250
  30.4 19.8 %collective-permute-start.3 = (bf16[2240,128]{1,0:T(8,128)(2,1)S(1)}, bf16[2240,128]{1,0:T(8,128)(2,1)S(1)}, u32[]{:S(2)}, u32[]{:S(2)}) collective-permute-start(bf16[2240,128]{1,0:T(8,128)(2,1)S(1)} %collective-permute-done.2.refs_0_), channel_id=1, source_target_pairs={{0,1},{1,0},{2,3},{3,2},{4,5},{5,4},{6,7},{7,6},{8,9},{9,8},{10,11... | collective-permute-start | bytes 1720328 | tf_op jit(solution)/shard_map/ppermute | solution.py:250
  30.7 8.5 %copy-start = (bf16[560,2240]{1,0:T(8,128)(2,1)S(1)}, bf16[560,2240]{1,0:T(8,128)(2,1)}, u32[]{:S(2)}) copy-start(bf16[560,2240]{1,0:T(8,128)(2,1)} %refs_0_.1) | copy-start | bytes 7526404
  50.1 15.4 %copy-start.4 = (f32[560]{0:T(1024)S(1)}, f32[560]{0:T(1024)}, u32[]{:S(2)}) copy-start(f32[560]{0:T(1024)} %param.9) | copy-start | bytes 6724
  50.1 28.7 %slice-start = ((s8[5160960]{0:T(1024)(128)(4,1)}), s8[4194304]{0:T(1024)(128)(4,1)S(1)}, s32[]{:S(2)}) async-start(s8[5160960]{0:T(1024)(128)(4,1)} %bitcast.9), calls=%async_computation | async-start | bytes 8388608
  55.9 13.8 %collective-permute-start.6 = (bf16[560,112]{1,0:T(8,128)(2,1)S(1)}, bf16[560,112]{1,0:T(8,128)(2,1)S(1)}, u32[]{:S(2)}, u32[]{:S(2)}) collective-permute-start(bf16[560,112]{1,0:T(8,128)(2,1)S(1)} %get-tuple-element.23), channel_id=1, source_target_pairs={{0,4},{4,8},{8,12},{1,5},{5,9},{9,13},{2,6},{6,10},{10,14},{3,7},{... | collective-permute-start | bytes 376328 | tf_op jit(solution)/shard_map/ppermute | solution.py:253
  59.7 10.1 %collective-permute-start.7 = (bf16[560,112]{1,0:T(8,128)(2,1)S(1)}, bf16[560,112]{1,0:T(8,128)(2,1)S(1)}, u32[]{:S(2)}, u32[]{:S(2)}) collective-permute-start(bf16[560,112]{1,0:T(8,128)(2,1)S(1)} %get-tuple-element.23), channel_id=1, source_target_pairs={{0,8},{4,12},{1,9},{5,13},{2,10},{6,14},{3,11},{7,15},{16,24},{20,... | collective-permute-start | bytes 376328 | tf_op jit(solution)/shard_map/ppermute | solution.py:253
  64.2 6.5 %collective-permute-start.8 = (bf16[560,112]{1,0:T(8,128)(2,1)S(1)}, bf16[560,112]{1,0:T(8,128)(2,1)S(1)}, u32[]{:S(2)}, u32[]{:S(2)}) collective-permute-start(bf16[560,112]{1,0:T(8,128)(2,1)S(1)} %get-tuple-element.23), channel_id=1, source_target_pairs={{0,12},{1,13},{2,14},{3,15},{16,28},{17,29},{18,30},{19,31}} | collective-permute-start | bytes 376328 | tf_op jit(solution)/shard_map/ppermute | solution.py:253
  65.6 5.1 %copy-start.2 = (s32[2]{0:T(128)S(1)}, s32[2]{0:T(128)}, u32[]{:S(2)}) copy-start(s32[2]{0:T(128)} %end_ref.1) | copy-start | bytes 28
  65.6 13.2 %slice-start.1 = ((s8[5160960]{0:T(1024)(128)(4,1)}), s8[966656]{0:T(1024)(128)(4,1)S(1)}, s32[]{:S(2)}) async-start(s8[5160960]{0:T(1024)(128)(4,1)} %bitcast.9), calls=%async_computation.1 | async-start | bytes 1933312
  72.1 1.6 %collective-permute-start.10 = (bf16[2,560,128]{2,1,0:T(8,128)(2,1)S(1)}, bf16[2,560,128]{2,1,0:T(8,128)(2,1)S(1)}, u32[]{:S(2)}, u32[]{:S(2)}) collective-permute-start(bf16[2,560,128]{2,1,0:T(8,128)(2,1)S(1)} %get-tuple-element.30), channel_id=1, source_target_pairs={{0,1},{1,0},{2,3},{3,2},{4,5},{5,4},{6,7},{7,6},{8,9},{9,8},{10,11... | collective-permute-start | bytes 860168 | tf_op jit(solution)/shard_map/ppermute | solution.py:250
  77.2 22.8 %collective-permute-start.12 = (bf16[2,1120,128]{2,1,0:T(8,128)(2,1)S(1)}, bf16[2,1120,128]{2,1,0:T(8,128)(2,1)S(1)}, u32[]{:S(2)}, u32[]{:S(2)}) collective-permute-start(bf16[2,1120,128]{2,1,0:T(8,128)(2,1)S(1)} %mix.6), channel_id=1, source_target_pairs={{0,2},{1,3},{2,0},{3,1},{4,6},{5,7},{6,4},{7,5},{8,10},{9,11},{10,... | collective-permute-start | bytes 1720328 | tf_op jit(solution)/shard_map/ppermute | solution.py:250
  78.8 3.4 %collective-permute-start.9 = (bf16[2,560,128]{2,1,0:T(8,128)(2,1)S(1)}, bf16[2,560,128]{2,1,0:T(8,128)(2,1)S(1)}, u32[]{:S(2)}, u32[]{:S(2)}) collective-permute-start(bf16[2,560,128]{2,1,0:T(8,128)(2,1)S(1)} %get-tuple-element.28), channel_id=1, source_target_pairs={{0,1},{1,0},{2,3},{3,2},{4,5},{5,4},{6,7},{7,6},{8,9},{9,8},{10,11... | collective-permute-start | bytes 860168 | tf_op jit(solution)/shard_map/ppermute | solution.py:250
  79.4 19.9 %collective-permute-start.13 = (bf16[2,560,128]{2,1,0:T(8,128)(2,1)S(1)}, bf16[2,560,128]{2,1,0:T(8,128)(2,1)S(1)}, u32[]{:S(2)}, u32[]{:S(2)}) collective-permute-start(bf16[2,560,128]{2,1,0:T(8,128)(2,1)S(1)} %mix.7), channel_id=1, source_target_pairs={{0,2},{1,3},{2,0},{3,1},{4,6},{5,7},{6,4},{7,5},{8,10},{9,11},{10,... | collective-permute-start | bytes 860168 | tf_op jit(solution)/shard_map/ppermute | solution.py:250
  80.6 24.0 %collective-permute-start.11 = (bf16[2,560,128]{2,1,0:T(8,128)(2,1)S(1)}, bf16[2,560,128]{2,1,0:T(8,128)(2,1)S(1)}, u32[]{:S(2)}, u32[]{:S(2)}) collective-permute-start(bf16[2,560,128]{2,1,0:T(8,128)(2,1)S(1)} %mix.5), channel_id=1, source_target_pairs={{0,2},{1,3},{2,0},{3,1},{4,6},{5,7},{6,4},{7,5},{8,10},{9,11},{10,... | collective-permute-start | bytes 860168 | tf_op jit(solution)/shard_map/ppermute | solution.py:250
where the time goes:
time: 107 us; the launch traced here: 106 us
  waiting for transfers between devices  44.4 us (41%)
  Pallas kernels  41.9 us (39%)
  starting transfers between devices  16.9 us (16%)
  local copies, waits for them, and re-layouts  1.82 us (2%)
    ppermute x11, waiting for transfers between devices, swap(): return lax.ppermute(v, 'row', [(i, i ^ k) for i in range(n_row)])  43.5 us
    pallas_call x3, Pallas kernels, project(): pl.pallas_call(kernel, in_specs=[VMEM] * len(given), out_specs=[VMEM] * l...  20.3 us
    ppermute x3, starting transfers between devices, shift(): return lax.ppermute(v, 'frm', [(i, i + s) for i in range(n_frm - s)])  9.53 us
    pallas_call x4, Pallas kernels, mix(): pl.pallas_call(kernel, in_specs=[VMEM] * (1 + n), out_specs=VMEM, out_sha...  8.85 us
    ppermute x11, starting transfers between devices, swap(): return lax.ppermute(v, 'row', [(i, i ^ k) for i in range(n_row)])  7.41 us
    pallas_call x1, Pallas kernels, turn(): pl.pallas_call(kernel, in_specs=[VMEM] * n, out_specs=VMEM, out_shape=jax...  4.78 us
    pallas_call x1, Pallas kernels, query(): pl.pallas_call(kernel, in_specs=[VMEM] * 2, out_specs=VMEM, out_shape=jax...  4.12 us
    pallas_call x3, Pallas kernels, finish(): pl.pallas_call(kernel, in_specs=[VMEM] * (1 + n) + ([] if buffer is None...  2.37 us
  transfers between devices with their start and end apart: 14, of which 6 were waited for; matrix products, arithmetic and copies ran while one was open for 2% of the time, Pallas kernels for 29%

commit v1 on v0

--- a/solution.py
+++ b/solution.py
@@ -167,87 +167,134 @@
     )(end, states, head_gain, *priors, *[a for a, _, _ in queries])
 
 
-def turn(pieces):
-    n = len(pieces)
-    group, width = pieces[0].shape
-
-    def kernel(*refs):
-        for k in range(n):
-            refs[n][:, k * group : (k + 1) * group] = refs[k][...].T
-
-    return pl.pallas_call(
-        kernel,
-        in_specs=[VMEM] * n,
+def turn(here, own, other, blocks, cuts):
+    group, width = own.shape
+    rows = width // blocks
+    sizes = [b - a for a, b in zip(cuts[:-1], cuts[1:])]
+
+    def kernel(here_ref, own_ref, other_ref, whole_ref, *pieces):
+        for first in range(2):
+
+            @pl.when(here_ref[0] == first)
+            def _():
+                for k, ref in enumerate((own_ref, other_ref)):
+                    at = (k ^ first) * group
+                    whole_ref[:, at : at + group] = ref[...].T
+
+        for a, piece in zip(cuts, pieces):
+            start = pl.multiple_of(here_ref[1] * rows + a, 16)
+            piece[...] = whole_ref[pl.ds(start, piece.shape[0]), :]
+
+    return pl.pallas_call(
+        kernel,
+        in_specs=[pl.BlockSpec(memory_space=pltpu.SMEM)] + [VMEM] * 2,
+        out_specs=[VMEM] * (1 + len(sizes)),
+        out_shape=[jax.ShapeDtypeStruct((width, 2 * group), BF16)]
+        + [jax.ShapeDtypeStruct((n, 2 * group), BF16) for n in sizes],
+        compiler_params=params(),
+        cost_estimate=cost(0, 16 * group * width),
+        name="turn",
+    )(here, own, other)
+
+
+def pack(both, here_ref, mine, other):
+    frames, group, lanes = mine.shape
+    for f in range(frames):
+        cols = slice(f * lanes, (f + 1) * lanes)
+        for ref, at in ((mine, here_ref[0]), (other, 1 - here_ref[0])):
+            both[pl.ds(pl.multiple_of(at * group, 16), group), cols] = ref[f]
+
+
+def mix(here, weights, mine, other):
+    frames, group, lanes = mine.shape
+    width = weights.shape[0]
+
+    def kernel(here_ref, w_ref, mine_ref, other_ref, out, both):
+        pack(both, here_ref, mine_ref, other_ref)
+        total = dot(w_ref[...], both[...])
+        for f in range(frames):
+            out[f] = total[:, f * lanes : (f + 1) * lanes]
+
+    return pl.pallas_call(
+        kernel,
+        in_specs=[pl.BlockSpec(memory_space=pltpu.SMEM)] + [VMEM] * 3,
         out_specs=VMEM,
-        out_shape=jax.ShapeDtypeStruct((width, n * group), BF16),
-        compiler_params=params(),
-        cost_estimate=cost(0, 4 * n * group * width),
-        name="turn",
-    )(*pieces)
-
-
-def mix(weights, heads_out, start, stop, dtype):
-    n = len(heads_out)
-    frames, group, lanes = heads_out[0].shape
-
-    def kernel(w_ref, *refs):
-        out, both = refs[n], refs[n + 1]
-        for k in range(n):
-            for f in range(frames):
-                both[k * group : (k + 1) * group, f * lanes : (f + 1) * lanes] = refs[k][f]
-        total = dot(w_ref[start:stop, :], both[...])
+        out_shape=jax.ShapeDtypeStruct((frames, width, lanes), F32),
+        scratch_shapes=[pltpu.VMEM((2 * group, frames * lanes), BF16)],
+        compiler_params=params(),
+        cost_estimate=cost(4 * width * group * frames * lanes, 4 * width * group),
+        name="mix",
+    )(here, weights, mine, other)
+
+
+def finish(here, order, own, chips):
+    frames, width, lanes = own.shape
+    blocks = len(order)
+    rows = width // blocks
+    counts = [[len(p) for p in pieces] for pieces, _, _ in chips]
+    group = chips[0][1].shape[1]
+    given = []
+    for pieces, mine, other in chips:
+        given += [mine, other] + [v for p in pieces for v in p]
+
+    def kernel(order_ref, here_ref, own_ref, *refs):
+        refs, out, both, w = refs[: len(given)], refs[-3], refs[-2], refs[-1]
+        step = pl.program_id(0)
+
+        @pl.when(step == 0)
+        def _():
+            at = 0
+            for k, count in enumerate(counts):
+                pack(both.at[k], here_ref, refs[at], refs[at + 1])
+                at += 2 + sum(count)
+
+        at = 0
+        for k, count in enumerate(counts):
+            at += 2
+            for r, n in enumerate(count):
+
+                @pl.when(step == r)
+                def _(k=k, first=at, n=n):
+                    row = 0
+                    for ref in refs[first : first + n]:
+                        w[k, row : row + ref.shape[0], :] = ref[...]
+                        row += ref.shape[0]
+
+                at += n
+        total = None
+        for k in range(len(counts)):
+            term = dot(w[k], both[k])
+            total = term if total is None else total + term
         for f in range(frames):
-            out[f] = total[:, f * lanes : (f + 1) * lanes].astype(dtype)
-
-    return pl.pallas_call(
-        kernel,
-        in_specs=[VMEM] * (1 + n),
-        out_specs=VMEM,
-        out_shape=jax.ShapeDtypeStruct((frames, stop - start, lanes), dtype),
-        scratch_shapes=[pltpu.VMEM((n * group, frames * lanes), BF16)],
-        compiler_params=params(),
-        cost_estimate=cost(2 * n * (stop - start) * group * frames * lanes, 2 * n * (stop - start) * group),
-        name="mix",
-    )(weights, *heads_out)
-
-
-def finish(buffer, own, arrived, start, whole_shape):
-    n = len(arrived)
-    frames, rows, lanes = arrived[0].shape
-
-    def kernel(*refs):
-        own_ref, got, out, staged, sem = refs[0], refs[1 : 1 + n], refs[-3], refs[-2], refs[-1]
-        copies = []
-        for f in range(frames):
-            total = own_ref[f, start : start + rows, :]
-            for g in got:
-                total = total + g[f].astype(F32)
-            staged[f] = total.astype(BF16)
-            copies.append(pltpu.make_async_copy(staged.at[f], out.at[f, pl.ds(start, rows), :], sem.at[f]))
-            copies[-1].start()
-        for c in copies:
-            c.wait()
-
-    given = [own, *arrived] + ([] if buffer is None else [buffer])
-    return pl.pallas_call(
-        kernel,
-        in_specs=[VMEM] * (1 + n) + ([] if buffer is None else [pl.BlockSpec(memory_space=pl.ANY)]),
-        out_specs=pl.BlockSpec(memory_space=pl.ANY),
-        out_shape=jax.ShapeDtypeStruct(whole_shape, BF16),
-        scratch_shapes=[pltpu.VMEM((frames, rows, lanes), BF16), pltpu.SemaphoreType.DMA((frames,))],
-        input_output_aliases={} if buffer is None else {1 + n: 0},
-        compiler_params=params(),
-        cost_estimate=cost(0, 8 * frames * rows * lanes),
+            out[f] = (own_ref[f] + total[:, f * lanes : (f + 1) * lanes]).astype(BF16)
+
+    block = pl.BlockSpec((frames, rows, lanes), lambda g, order_ref, here_ref: (0, order_ref[g], 0))
+    return pl.pallas_call(
+        kernel,
+        grid_spec=pltpu.PrefetchScalarGridSpec(
+            num_scalar_prefetch=2,
+            grid=(blocks,),
+            in_specs=[block] + [VMEM] * len(given),
+            out_specs=block,
+            scratch_shapes=[
+                pltpu.VMEM((len(chips), 2 * group, frames * lanes), BF16),
+                pltpu.VMEM((len(chips), rows, 2 * group), BF16),
+            ],
+        ),
+        out_shape=jax.ShapeDtypeStruct(own.shape, BF16),
+        compiler_params=params(),
+        cost_estimate=cost(4 * len(chips) * width * group * frames * lanes, 4 * len(chips) * width * group),
         name="finish",
-    )(*given)
-
-
-CUTS = (0.0, 0.25, 0.75, 1.0)
-
-
-def per_device(n_row, n_frm, hidden_in, norm_gain, qkv_weight, head_gain, output_matrix, block_end):
-    def swap(v, k):
-        return lax.ppermute(v, "row", [(i, i ^ k) for i in range(n_row)])
+    )(jnp.stack(order), here, own, *given)
+
+
+CUTS = (0.0, 0.34, 0.68, 1.0)
+
+
+def per_device(n_grp, n_row, n_frm, hidden_in, norm_gain, qkv_weight, head_gain, output_matrix, block_end):
+    def swap(v, k, axis="row"):
+        size = {"row": n_row, "grp": n_grp}[axis]
+        return lax.ppermute(v, axis, [(i, i ^ k) for i in range(size)])
 
     def shift(v, s):
         return lax.ppermute(v, "frm", [(i, i + s) for i in range(n_frm - s)])
@@ -268,8 +315,29 @@
 
     where = [[(0, f), (1, f)] for f in range(frames)]
     states, near_q = project([tokens, sibling], where, gain, weights, None, frames)
-    turned = turn([output_matrix, swap(output_matrix, 1)])
+    width = output_matrix.shape[1]
+    core = lax.axis_index("row") % 2
+    grp = lax.axis_index("grp")
+    blocks = 2 * n_grp
+    here = jnp.stack([core, 2 * grp + core])
+    cuts = [int(c * (width // blocks)) // 16 * 16 for c in CUTS]
+    near_rows = swap(output_matrix, 1)
+    turned, *pieces = turn(here, output_matrix, near_rows, blocks, cuts)
     states, turned = lax.optimization_barrier((states, turned))
+
+    order, chips = [], []
+    for g in range(n_grp):
+        for c in range(2):
+            order.append(2 * (grp ^ g) + (core ^ c))
+    for k in range(1, pairs):
+        held = {}
+        for j, piece in enumerate(pieces):
+            held[0, 0, j] = swap(piece, 2 * k)
+            for g in range(1, n_grp):
+                held[g, 0, j] = swap(held[0, 0, j], g, "grp")
+            for g in range(n_grp):
+                held[g, 1, j] = swap(held[g, 0, j], 1)
+        chips.append([[held[g, c, j] for j in range(len(pieces))] for g in range(n_grp) for c in range(2)])
     queries = []
     for f in range(frames):
         for k in range(1, pairs):
@@ -292,22 +360,12 @@
     queries.append((near_q, {f: f for f in range(frames)}, 0))
     heads_out = attend(block_end, states, priors, out_gain, queries, lanes)
 
-    got = {}
-    for k in list(range(1, pairs)) + [0]:
-        got[k] = swap(heads_out[2 * k + 1], 1)
-    width = output_matrix.shape[1]
-    cuts = [int(c * width) // 16 * 16 for c in CUTS]
-    spans = list(zip(cuts[:-1], cuts[1:]))
-    arrived = []
-    for i, (start, stop) in enumerate(spans):
-        arrived.append([])
-        for k in range(1, pairs):
-            part = mix(turned, (heads_out[2 * k], got[k]), start, stop, BF16)
-            arrived[i].append(swap(part, 2 * k))
-    own = mix(turned, (heads_out[0], got[0]), 0, width, F32)
-    out = None
-    for (start, stop), parts in zip(spans, arrived):
-        out = finish(out, own, parts, start, (frames, width, lanes))
+    across = []
+    for k in range(1, pairs):
+        across.append((swap(heads_out[2 * k], 2 * k), swap(heads_out[2 * k + 1], 2 * k + 1)))
+    own = mix(here, turned, heads_out[0], swap(heads_out[1], 1))
+    chips = [(held, *pair) for held, pair in zip(chips, across)]
+    out = finish(here, order, own, chips)
     return jnp.transpose(out, (2, 0, 1))
 
 
@@ -322,7 +380,7 @@
     )
 
     def body(*args):
-        return per_device(mesh.shape["row"], mesh.shape["frm"], *args)
+        return per_device(mesh.shape["grp"], mesh.shape["row"], mesh.shape["frm"], *args)
 
     return jax.shard_map(
         body, mesh=mesh, in_specs=placed, out_specs=P("row", ("grp", "frm"), None), check_vma=False

time: 107 us -> 125 us (1.17)
  starting transfers between devices: 16.9 us -> 25.2 us
  local copies, waits for them, and re-layouts: 1.82 us -> 9.5 us
  waiting for transfers between devices: 44.4 us -> 46.7 us
    unnamed x14 -> x36, local copies, waits for them, and re-layouts: 0.04 us -> 7.71 us
    ppermute x11 -> x21, starting transfers between devices: 7.41 us -> 15 us  [swap(): return lax.ppermute(v, axis, [(i, i ^ k) for i in range(size)])]
    ppermute x11 -> x21, waiting for transfers between devices: 43.5 us -> 46.7 us  [swap(): return lax.ppermute(v, axis, [(i, i ^ k) for i in range(size)])]
    pallas_call x8 -> x3, Pallas kernels: 16 us -> 17 us  [the longest x1 6.71 us: turn(): pl.pallas_call(kernel, in_specs=[pl.BlockSpec(memory_space=pltpu.SMEM)] +...]
  transfers between devices with their start and end apart: 14 -> 24, of which waited for: 6 -> 6; matrix products, arithmetic and copies ran while one was open for 2% -> 2% of each run, Pallas kernels for 29% -> 25%
where the time goes in v1:
time: 125 us
  waiting for transfers between devices  46.7 us (37%)
  Pallas kernels  42.8 us (34%)
  starting transfers between devices  25.2 us (20%)
  local copies, waits for them, and re-layouts  9.5 us (8%)
    ppermute x21, waiting for transfers between devices, swap(): return lax.ppermute(v, axis, [(i, i ^ k) for i in range(size)])  46.7 us
    pallas_call x3, Pallas kernels, project(): pl.pallas_call(kernel, in_specs=[VMEM] * len(given), out_specs=[VMEM] * l...  20.3 us
    ppermute x21, starting transfers between devices, swap(): return lax.ppermute(v, axis, [(i, i ^ k) for i in range(size)])  15 us
    ppermute x3, starting transfers between devices, shift(): return lax.ppermute(v, 'frm', [(i, i + s) for i in range(n_frm - s)])  10.2 us
    unnamed x36, local copies, waits for them, and re-layouts  7.71 us
    pallas_call x1, Pallas kernels, turn(): pl.pallas_call(kernel, in_specs=[pl.BlockSpec(memory_space=pltpu.SMEM)] +...  6.71 us
    pallas_call x1, Pallas kernels, finish(): pl.pallas_call(kernel, grid_spec=pltpu.PrefetchScalarGridSpec(num_scalar_...  5.91 us
    pallas_call x1, Pallas kernels, mix(): pl.pallas_call(kernel, in_specs=[pl.BlockSpec(memory_space=pltpu.SMEM)] +...  4.34 us
  transfers between devices with their start and end apart: 24, of which 6 were waited for; matrix products, arithmetic and copies ran while one was open for 2% of the time, Pallas kernels for 25%

profile of v1, /device:TPU:0, one launch (start us, length us, event | category | flops | bytes accessed | tf_op | source)
XLA Modules:
  0.0 124.7 jit_solution(15192708407980332001)
XLA Ops:
  0.0 0.5 collective-permute-start.1
  0.5 0.1 collective-permute-start
  0.6 1.3 %slice_bitcast_fusion = (bf16[2240,128]{1,0:T(8,128)(2,1)S(1)}, bf16[2240,128]{1,0:T(8,128)(2,1)S(1)}) fusion(bf16[2,2240,128]{2,1,0:T(8,128)(2,1)} %bitcast.15), kind=kLoop, calls=%fused_computation | loop fusion | bytes 2293760 | tf_op jit(solution)/shard_map/squeeze | solution.py:312
  1.9 0.0 copy-start.2
  1.9 3.0 %collective-permute-start.4 = (bf16[2240,128]{1,0:T(8,128)(2,1)S(1)}, bf16[2240,128]{1,0:T(8,128)(2,1)S(1)}, u32[]{:S(2)}, u32[]{:S(2)}) collective-permute-start(bf16[2240,128]{1,0:T(8,128)(2,1)S(1)} %get-tuple-element.39), channel_id=1, source_target_pairs={{0,2},{1,3},{2,0},{3,1},{4,6},{5,7},{6,4},{7,5},{8,10},{9,11},{10,... | collective-permute-start | bytes 1720328 | tf_op jit(solution)/shard_map/ppermute | solution.py:297
  4.9 0.1 collective-permute-start.2
  4.9 13.8 %collective-permute-done.4.refs_0_ = bf16[2240,128]{1,0:T(8,128)(2,1)S(1)} collective-permute-done((bf16[2240,128]{1,0:T(8,128)(2,1)S(1)}, bf16[2240,128]{1,0:T(8,128)(2,1)S(1)}, u32[]{:S(2)}, u32[]{:S(2)}) %collective-permute-start.4) | collective-permute-done | bytes 573472 | tf_op jit(solution)/shard_map/ppermute | solution.py:297
  18.7 0.0 collective-permute-start.5
  18.7 11.7 %collective-permute-done.2.refs_0_ = bf16[2240,128]{1,0:T(8,128)(2,1)S(1)} collective-permute-done((bf16[2240,128]{1,0:T(8,128)(2,1)S(1)}, bf16[2240,128]{1,0:T(8,128)(2,1)S(1)}, u32[]{:S(2)}, u32[]{:S(2)}) %collective-permute-start.2) | collective-permute-done | bytes 573472 | tf_op jit(solution)/shard_map/ppermute | solution.py:297
  30.4 0.0 collective-permute-start.3
  30.4 0.1 pad_add_fusion.1.here_ref
  30.4 0.3 reshape.12.refs_2_
  30.8 0.0 collective-permute-done.refs_1_
  30.8 0.0 copy-start.1
  30.8 8.8 %project.3 = (f32[2,560,112]{2,1,0:T(8,128)S(1)}, bf16[2,560,256]{2,1,0:T(8,128)(2,1)S(1)}) custom-call(bf16[2,2240,128]{2,1,0:T(8,128)(2,1)S(1)} %bitcast.16, bf16[2,2240,128]{2,1,0:T(8,128)(2,1)} %collective-permute-done.refs_1_, f32[2240,1]{1,0:T(8,128)S(1)} %reshape.12.refs_2_, bf16[1680,2240]{1,0:T(8,128)(2,1)} %bitcast.17), custom_call_target="tpu_custom_call" | custom-call | flops 3853516800 | bytes 2293760 | tf_op jit(solution)/shard_map/project/pallas_call | solution.py:95
  39.7 6.7 %turn.1 = (bf16[2240,1120]{1,0:T(8,128)(2,1)}, bf16[176,1120]{1,0:T(8,128)(2,1)S(1)}, bf16[192,1120]{1,0:T(8,128)(2,1)S(1)}, bf16[192,1120]{1,0:T(8,128)(2,1)S(1)}) custom-call(s32[2]{0:T(128)S(1)} %pad_add_fusion.1.here_ref, bf16[560,2240]{1,0:T(8,128)(2,1)S(1)} %copy-done.1, bf16[560,2240]{1,0:T(8,128)(2,1)} %collective-permute-done.1.other_ref), custom_call_target="tpu_custom_call" | custom-call | bytes 20070400 | tf_op jit(solution)/shard_map/turn/pallas_call | solution.py:188
  46.4 0.0 collective-permute-done.5.refs_1_
  46.4 6.1 %project.4 = (f32[2,560,112]{2,1,0:T(8,128)S(1)}, bf16[1,560,256]{2,1,0:T(8,128)(2,1)S(1)}) custom-call(bf16[2240,128]{1,0:T(8,128)(2,1)S(1)} %collective-permute-done.4.refs_0_, bf16[2240,128]{1,0:T(8,128)(2,1)S(1)} %collective-permute-done.5.refs_1_, f32[2240,1]{1,0:T(8,128)S(1)} %reshape.12.refs_2_, bf16[1680,2240]{1,0:T(8,128)(2,1)} %bitcast.18, ...), custom_call_target="tpu_custom_call" | custom-call | flops 1926758400 | bytes 1146880 | tf_op jit(solution)/shard_map/project/pallas_call | solution.py:95
  52.5 0.0 collective-permute-done.3.refs_1_
  52.5 0.0 copy-start.17
  52.5 5.5 %project.5 = (f32[2,560,112]{2,1,0:T(8,128)S(1)}, bf16[560,112]{1,0:T(8,128)(2,1)S(1)}, bf16[2240,256]{1,0:T(8,128)(2,1)S(1)}) custom-call(bf16[2240,128]{1,0:T(8,128)(2,1)S(1)} %collective-permute-done.2.refs_0_, bf16[2240,128]{1,0:T(8,128)(2,1)S(1)} %collective-permute-done.3.refs_1_, f32[2240,1]{1,0:T(8,128)S(1)} %reshape.12.refs_2_, ...), custom_call_target="tpu_custom_call" | custom-call | flops 1284505600 | bytes 1146880 | tf_op jit(solution)/shard_map/project/pallas_call | solution.py:95
  57.9 3.7 %collective-permute-start.6 = (bf16[560,112]{1,0:T(8,128)(2,1)S(1)}, bf16[560,112]{1,0:T(8,128)(2,1)S(1)}, u32[]{:S(2)}, u32[]{:S(2)}) collective-permute-start(bf16[560,112]{1,0:T(8,128)(2,1)S(1)} %get-tuple-element.28), channel_id=1, source_target_pairs={{0,4},{4,8},{8,12},{1,5},{5,9},{9,13},{2,6},{6,10},{10,14},{3,7},{... | collective-permute-start | bytes 376328 | tf_op jit(solution)/shard_map/ppermute | solution.py:300
  61.7 1.6 %collective-permute-start.13 = (bf16[192,1120]{1,0:T(8,128)(2,1)S(1)}, bf16[192,1120]{1,0:T(8,128)(2,1)S(1)}, u32[]{:S(2)}, u32[]{:S(2)}) collective-permute-start(bf16[192,1120]{1,0:T(8,128)(2,1)S(1)} %get-tuple-element.37), channel_id=1, source_target_pairs={{0,2},{1,3},{2,0},{3,1},{4,6},{5,7},{6,4},{7,5},{8,10},{9,11},{10,... | collective-permute-start | bytes 1290248 | tf_op jit(solution)/shard_map/ppermute | solution.py:297
  63.2 0.5 collective-permute-start.14
  63.8 1.5 %collective-permute-start.12 = (bf16[176,1120]{1,0:T(8,128)(2,1)S(1)}, bf16[176,1120]{1,0:T(8,128)(2,1)S(1)}, u32[]{:S(2)}, u32[]{:S(2)}) collective-permute-start(bf16[176,1120]{1,0:T(8,128)(2,1)S(1)} %get-tuple-element.36), channel_id=1, source_target_pairs={{0,2},{1,3},{2,0},{3,1},{4,6},{5,7},{6,4},{7,5},{8,10},{9,11},{10,... | collective-permute-start | bytes 1182728 | tf_op jit(solution)/shard_map/ppermute | solution.py:297
  65.3 4.5 %collective-permute-start.7 = (bf16[560,112]{1,0:T(8,128)(2,1)S(1)}, bf16[560,112]{1,0:T(8,128)(2,1)S(1)}, u32[]{:S(2)}, u32[]{:S(2)}) collective-permute-start(bf16[560,112]{1,0:T(8,128)(2,1)S(1)} %get-tuple-element.28), channel_id=1, source_target_pairs={{0,8},{4,12},{1,9},{5,13},{2,10},{6,14},{3,11},{7,15},{16,24},{20,... | collective-permute-start | bytes 376328 | tf_op jit(solution)/shard_map/ppermute | solution.py:300
  69.8 2.0 %collective-permute-start.8 = (bf16[560,112]{1,0:T(8,128)(2,1)S(1)}, bf16[560,112]{1,0:T(8,128)(2,1)S(1)}, u32[]{:S(2)}, u32[]{:S(2)}) collective-permute-start(bf16[560,112]{1,0:T(8,128)(2,1)S(1)} %get-tuple-element.28), channel_id=1, source_target_pairs={{0,12},{1,13},{2,14},{3,15},{16,28},{17,29},{18,30},{19,31}} | collective-permute-start | bytes 376328 | tf_op jit(solution)/shard_map/ppermute | solution.py:300
  71.8 0.1 reshape.13.gain_ref
  71.9 0.0 copy-start.15
  71.9 4.0 %query.1.rest_4_ = bf16[1,560,256]{2,1,0:T(8,128)(2,1)S(1)} custom-call(bf16[2240,256]{1,0:T(8,128)(2,1)S(1)} %get-tuple-element.30.x_ref, bf16[1680,2240]{1,0:T(8,128)(2,1)} %bitcast.20), custom_call_target="tpu_custom_call" | custom-call | flops 642252800 | bytes 1146880 | tf_op jit(solution)/shard_map/query/pallas_call | solution.py:114
  76.0 0.0 collective-permute-done.7.rest_1_
  76.0 0.0 collective-permute-done.8.rest_2_
  76.0 1.5 %attend.1 = (bf16[2,560,128]{2,1,0:T(8,128)(2,1)S(1)}, bf16[2,560,128]{2,1,0:T(8,128)(2,1)S(1)}, bf16[2,560,128]{2,1,0:T(8,128)(2,1)S(1)}, bf16[2,560,128]{2,1,0:T(8,128)(2,1)S(1)}) custom-call(s32[2]{0:T(128)S(1)} %copy-done.15, f32[2,560,112]{2,1,0:T(8,128)S(1)} %get-tuple-element.27.state_ref, f32[560,1]{1,0:T(8,128)S(1)} %reshape.13.gain_ref, ...), custom_call_target="tpu_custom_call" | custom-call | flops 128450560 | bytes 2293760 | tf_op jit(solution)/shard_map/attend/pallas_call | solution.py:158
  77.5 0.7 copy-done.11
  78.2 1.5 %collective-permute-start.10 = (bf16[2,560,128]{2,1,0:T(8,128)(2,1)S(1)}, bf16[2,560,128]{2,1,0:T(8,128)(2,1)S(1)}, u32[]{:S(2)}, u32[]{:S(2)}) collective-permute-start(bf16[2,560,128]{2,1,0:T(8,128)(2,1)S(1)} %get-tuple-element.34), channel_id=1, source_target_pairs={{0,2},{1,3},{2,0},{3,1},{4,6},{5,7},{6,4},{7,5},{8,10},{9,11},{10,... | collective-permute-start | bytes 860168 | tf_op jit(solution)/shard_map/ppermute | solution.py:297
  79.7 1.5 %collective-permute-start.19 = (bf16[192,1120]{1,0:T(8,128)(2,1)S(1)}, bf16[192,1120]{1,0:T(8,128)(2,1)S(1)}, u32[]{:S(2)}, u32[]{:S(2)}) collective-permute-start(bf16[192,1120]{1,0:T(8,128)(2,1)S(1)} %collective-permute-done.13.refs_3_), channel_id=1, source_target_pairs={{0,16},{16,0},{1,17},{17,1},{2,18},{18,2},{3,19},{19,3},{4,20},{20... | collective-permute-start | bytes 1290248 | tf_op jit(solution)/shard_map/ppermute | solution.py:297
  81.2 3.0 %collective-permute-done.14.refs_4_ = bf16[192,1120]{1,0:T(8,128)(2,1)S(1)} collective-permute-done((bf16[192,1120]{1,0:T(8,128)(2,1)S(1)}, bf16[192,1120]{1,0:T(8,128)(2,1)S(1)}, u32[]{:S(2)}, u32[]{:S(2)}) %collective-permute-start.14) | collective-permute-done | bytes 430112 | tf_op jit(solution)/shard_map/ppermute | solution.py:297
  84.3 1.5 %collective-permute-start.20 = (bf16[192,1120]{1,0:T(8,128)(2,1)S(1)}, bf16[192,1120]{1,0:T(8,128)(2,1)S(1)}, u32[]{:S(2)}, u32[]{:S(2)}) collective-permute-start(bf16[192,1120]{1,0:T(8,128)(2,1)S(1)} %collective-permute-done.14.refs_4_), channel_id=1, source_target_pairs={{0,16},{16,0},{1,17},{17,1},{2,18},{18,2},{3,19},{19,3},{4,20},{20... | collective-permute-start | bytes 1290248 | tf_op jit(solution)/shard_map/ppermute | solution.py:297
  85.8 7.2 %collective-permute-done.12.refs_2_ = bf16[176,1120]{1,0:T(8,128)(2,1)S(1)} collective-permute-done((bf16[176,1120]{1,0:T(8,128)(2,1)S(1)}, bf16[176,1120]{1,0:T(8,128)(2,1)S(1)}, u32[]{:S(2)}, u32[]{:S(2)}) %collective-permute-start.12) | collective-permute-done | bytes 394272 | tf_op jit(solution)/shard_map/ppermute | solution.py:297
  93.0 0.0 collective-permute-start.15
  93.0 0.0 collective-permute-done.9.other_ref
  93.0 0.7 copy-done.13
  93.7 1.5 %collective-permute-start.18 = (bf16[176,1120]{1,0:T(8,128)(2,1)S(1)}, bf16[176,1120]{1,0:T(8,128)(2,1)}, u32[]{:S(2)}, u32[]{:S(2)}) collective-permute-start(bf16[176,1120]{1,0:T(8,128)(2,1)S(1)} %collective-permute-done.12.refs_2_), channel_id=1, source_target_pairs={{0,16},{16,0},{1,17},{17,1},{2,18},{18,2},{3,19},{19,3},{4,20},{20... | collective-permute-start | bytes 1182728 | tf_op jit(solution)/shard_map/ppermute | solution.py:297
  95.2 0.7 copy-done.3
  96.0 2.4 %collective-permute-done.10.refs_0_ = bf16[2,560,128]{2,1,0:T(8,128)(2,1)S(1)} collective-permute-done((bf16[2,560,128]{2,1,0:T(8,128)(2,1)S(1)}, bf16[2,560,128]{2,1,0:T(8,128)(2,1)S(1)}, u32[]{:S(2)}, u32[]{:S(2)}) %collective-permute-start.10) | collective-permute-done | bytes 286752 | tf_op jit(solution)/shard_map/ppermute | solution.py:297
  98.4 0.7 copy-done.7
  99.1 0.5 collective-permute-start.11
  99.5 8.6 %collective-permute-done.11.refs_1_ = bf16[2,560,128]{2,1,0:T(8,128)(2,1)S(1)} collective-permute-done((bf16[2,560,128]{2,1,0:T(8,128)(2,1)S(1)}, bf16[2,560,128]{2,1,0:T(8,128)(2,1)S(1)}, u32[]{:S(2)}, u32[]{:S(2)}) %collective-permute-start.11) | collective-permute-done | bytes 286752 | tf_op jit(solution)/shard_map/ppermute | solution.py:297
  108.2 0.7 copy-done.9
  108.9 0.3 collective-permute-start.16
  109.2 0.7 copy-done.5
  109.9 0.2 collective-permute-start.17
  110.1 0.0 collective-permute-done.19.refs_9_
  110.1 0.3 collective-permute-start.22
  110.4 0.2 collective-permute-start.23
  110.7 0.0 collective-permute-done.18.refs_8_
  110.7 0.3 collective-permute-start.21
  110.9 0.1 pad_add_fusion.order_ref
  111.0 1.0 copy-done.12
  112.0 1.0 copy-done.14
  112.9 4.3 %mix.1.own_ref = f32[2,2240,128]{2,1,0:T(8,128)S(1)} custom-call(s32[2]{0:T(128)S(1)} %pad_add_fusion.1.here_ref, bf16[2240,1120]{1,0:T(8,128)(2,1)} %get-tuple-element.24.w_ref, bf16[2,560,128]{2,1,0:T(8,128)(2,1)S(1)} %copy-done.12, bf16[2,560,128]{2,1,0:T(8,128)(2,1)S(1)} %copy-done.14), custom_call_target="tpu_custom_call" | custom-call | flops 1284505600 | bytes 5017600 | tf_op jit(solution)/shard_map/mix/pallas_call | solution.py:218
  117.3 1.4 %copy-done = f32[2,2240,128]{2,1,0:T(8,128)} copy-done((f32[2,2240,128]{2,1,0:T(8,128)}, f32[2,2240,128]{2,1,0:T(8,128)S(1)}, u32[]{:S(2)}) %copy-start) | copy-done | bytes 2293784
  118.7 0.0 collective-permute-done.16.refs_6_
  118.8 5.9 %finish.1 = bf16[2,2240,128]{2,1,0:T(8,128)(2,1)} custom-call(s32[4]{0:T(128)S(1)} %pad_add_fusion.order_ref, s32[2]{0:T(128)S(1)} %pad_add_fusion.1.here_ref, f32[2,2240,128]{2,1,0:T(8,128)} %copy-done, bf16[2,560,128]{2,1,0:T(8,128)(2,1)S(1)} %copy-done.8, bf16[2,560,128]{2,1,0:T(8,128)(2,1)S(1)} %copy-done.10, bf16[176,1120]{1,0:T(8,128)(2,1)S(1)} %copy-done.4, ...), custom_call_target="tpu_custom_call" | custom-call | flops 1284505600 | bytes 5017600 | tf_op jit(solution)/shard_map/finish/pallas_call | solution.py:272
  (33 shorter events, 0.1 us)
Async XLA Ops:
  0.0 39.7 %collective-permute-start.1 = (bf16[560,2240]{1,0:T(8,128)(2,1)}, bf16[560,2240]{1,0:T(8,128)(2,1)}, u32[]{:S(2)}, u32[]{:S(2)}) collective-permute-start(bf16[560,2240]{1,0:T(8,128)(2,1)} %own_ref.1), channel_id=1, source_target_pairs={{0,1},{1,0},{2,3},{3,2},{4,5},{5,4},{6,7},{7,6},{8,9},{9,8},{10,11... | collective-permute-start | bytes 7526408 | tf_op jit(solution)/shard_map/ppermute | solution.py:297
  0.5 29.9 %copy-start.16 = (f32[2240]{0:T(1024)S(1)}, f32[2240]{0:T(1024)}, u32[]{:S(2)}) copy-start(f32[2240]{0:T(1024)} %param.7) | copy-start | bytes 26884
  0.5 30.3 %collective-permute-start = (bf16[2,2240,128]{2,1,0:T(8,128)(2,1)}, bf16[2,2240,128]{2,1,0:T(8,128)(2,1)}, u32[]{:S(2)}, u32[]{:S(2)}) collective-permute-start(bf16[2,2240,128]{2,1,0:T(8,128)(2,1)} %bitcast.14), channel_id=1, source_target_pairs={{0,1},{1,0},{2,3},{3,2},{4,5},{5,4},{6,7},{7,6},{8,9},{9,8},{10,11... | collective-permute-start | bytes 3440648 | tf_op jit(solution)/shard_map/ppermute | solution.py:297
  1.9 28.9 %copy-start.2 = (bf16[128,2,2240]{0,2,1:T(8,128)(2,1)S(1)}, bf16[128,2,2240]{0,2,1:T(8,128)(2,1)}, u32[]{:S(2)}) copy-start(bf16[128,2,2240]{0,2,1:T(8,128)(2,1)} %param.6) | copy-start | bytes 3440644
  1.9 16.8 %collective-permute-start.4 = (bf16[2240,128]{1,0:T(8,128)(2,1)S(1)}, bf16[2240,128]{1,0:T(8,128)(2,1)S(1)}, u32[]{:S(2)}, u32[]{:S(2)}) collective-permute-start(bf16[2240,128]{1,0:T(8,128)(2,1)S(1)} %get-tuple-element.39), channel_id=1, source_target_pairs={{0,2},{1,3},{2,0},{3,1},{4,6},{5,7},{6,4},{7,5},{8,10},{9,11},{10,... | collective-permute-start | bytes 1720328 | tf_op jit(solution)/shard_map/ppermute | solution.py:297
  4.9 25.5 %collective-permute-start.2 = (bf16[2240,128]{1,0:T(8,128)(2,1)S(1)}, bf16[2240,128]{1,0:T(8,128)(2,1)S(1)}, u32[]{:S(2)}, u32[]{:S(2)}) collective-permute-start(bf16[2240,128]{1,0:T(8,128)(2,1)S(1)} %get-tuple-element.40), channel_id=1, source_target_pairs={{0,2},{1,3},{2,0},{3,1},{4,6},{5,7},{6,4},{7,5},{8,10},{9,11},{10,... | collective-permute-start | bytes 1720328 | tf_op jit(solution)/shard_map/ppermute | solution.py:297
  18.7 27.7 %collective-permute-start.5 = (bf16[2240,128]{1,0:T(8,128)(2,1)S(1)}, bf16[2240,128]{1,0:T(8,128)(2,1)S(1)}, u32[]{:S(2)}, u32[]{:S(2)}) collective-permute-start(bf16[2240,128]{1,0:T(8,128)(2,1)S(1)} %collective-permute-done.4.refs_0_), channel_id=1, source_target_pairs={{0,1},{1,0},{2,3},{3,2},{4,5},{5,4},{6,7},{7,6},{8,9},{9,8},{10,11... | collective-permute-start | bytes 1720328 | tf_op jit(solution)/shard_map/ppermute | solution.py:297
  30.4 22.1 %collective-permute-start.3 = (bf16[2240,128]{1,0:T(8,128)(2,1)S(1)}, bf16[2240,128]{1,0:T(8,128)(2,1)S(1)}, u32[]{:S(2)}, u32[]{:S(2)}) collective-permute-start(bf16[2240,128]{1,0:T(8,128)(2,1)S(1)} %collective-permute-done.2.refs_0_), channel_id=1, source_target_pairs={{0,1},{1,0},{2,3},{3,2},{4,5},{5,4},{6,7},{7,6},{8,9},{9,8},{10,11... | collective-permute-start | bytes 1720328 | tf_op jit(solution)/shard_map/ppermute | solution.py:297
  30.8 8.9 %copy-start.1 = (bf16[560,2240]{1,0:T(8,128)(2,1)S(1)}, bf16[560,2240]{1,0:T(8,128)(2,1)}, u32[]{:S(2)}) copy-start(bf16[560,2240]{1,0:T(8,128)(2,1)} %own_ref.1) | copy-start | bytes 7526404
  52.5 19.3 %copy-start.17 = (f32[560]{0:T(1024)S(1)}, f32[560]{0:T(1024)}, u32[]{:S(2)}) copy-start(f32[560]{0:T(1024)} %param.9) | copy-start | bytes 6724
  57.9 11.8 %collective-permute-start.6 = (bf16[560,112]{1,0:T(8,128)(2,1)S(1)}, bf16[560,112]{1,0:T(8,128)(2,1)S(1)}, u32[]{:S(2)}, u32[]{:S(2)}) collective-permute-start(bf16[560,112]{1,0:T(8,128)(2,1)S(1)} %get-tuple-element.28), channel_id=1, source_target_pairs={{0,4},{4,8},{8,12},{1,5},{5,9},{9,13},{2,6},{6,10},{10,14},{3,7},{... | collective-permute-start | bytes 376328 | tf_op jit(solution)/shard_map/ppermute | solution.py:300
  61.7 18.0 %collective-permute-start.13 = (bf16[192,1120]{1,0:T(8,128)(2,1)S(1)}, bf16[192,1120]{1,0:T(8,128)(2,1)S(1)}, u32[]{:S(2)}, u32[]{:S(2)}) collective-permute-start(bf16[192,1120]{1,0:T(8,128)(2,1)S(1)} %get-tuple-element.37), channel_id=1, source_target_pairs={{0,2},{1,3},{2,0},{3,1},{4,6},{5,7},{6,4},{7,5},{8,10},{9,11},{10,... | collective-permute-start | bytes 1290248 | tf_op jit(solution)/shard_map/ppermute | solution.py:297
  63.2 21.0 %collective-permute-start.14 = (bf16[192,1120]{1,0:T(8,128)(2,1)S(1)}, bf16[192,1120]{1,0:T(8,128)(2,1)S(1)}, u32[]{:S(2)}, u32[]{:S(2)}) collective-permute-start(bf16[192,1120]{1,0:T(8,128)(2,1)S(1)} %get-tuple-element.38), channel_id=1, source_target_pairs={{0,2},{1,3},{2,0},{3,1},{4,6},{5,7},{6,4},{7,5},{8,10},{9,11},{10,... | collective-permute-start | bytes 1290248 | tf_op jit(solution)/shard_map/ppermute | solution.py:297
  63.8 29.2 %collective-permute-start.12 = (bf16[176,1120]{1,0:T(8,128)(2,1)S(1)}, bf16[176,1120]{1,0:T(8,128)(2,1)S(1)}, u32[]{:S(2)}, u32[]{:S(2)}) collective-permute-start(bf16[176,1120]{1,0:T(8,128)(2,1)S(1)} %get-tuple-element.36), channel_id=1, source_target_pairs={{0,2},{1,3},{2,0},{3,1},{4,6},{5,7},{6,4},{7,5},{8,10},{9,11},{10,... | collective-permute-start | bytes 1182728 | tf_op jit(solution)/shard_map/ppermute | solution.py:297
  65.3 10.7 %collective-permute-start.7 = (bf16[560,112]{1,0:T(8,128)(2,1)S(1)}, bf16[560,112]{1,0:T(8,128)(2,1)S(1)}, u32[]{:S(2)}, u32[]{:S(2)}) collective-permute-start(bf16[560,112]{1,0:T(8,128)(2,1)S(1)} %get-tuple-element.28), channel_id=1, source_target_pairs={{0,8},{4,12},{1,9},{5,13},{2,10},{6,14},{3,11},{7,15},{16,24},{20,... | collective-permute-start | bytes 376328 | tf_op jit(solution)/shard_map/ppermute | solution.py:300
  69.8 6.2 %collective-permute-start.8 = (bf16[560,112]{1,0:T(8,128)(2,1)S(1)}, bf16[560,112]{1,0:T(8,128)(2,1)S(1)}, u32[]{:S(2)}, u32[]{:S(2)}) collective-permute-start(bf16[560,112]{1,0:T(8,128)(2,1)S(1)} %get-tuple-element.28), channel_id=1, source_target_pairs={{0,12},{1,13},{2,14},{3,15},{16,28},{17,29},{18,30},{19,31}} | collective-permute-start | bytes 376328 | tf_op jit(solution)/shard_map/ppermute | solution.py:300
  71.9 4.1 %copy-start.15 = (s32[2]{0:T(128)S(1)}, s32[2]{0:T(128)}, u32[]{:S(2)}) copy-start(s32[2]{0:T(128)} %end_ref.1) | copy-start | bytes 28
  77.5 0.7 copy-start.11
  78.2 14.8 %collective-permute-start.9 = (bf16[2,560,128]{2,1,0:T(8,128)(2,1)S(1)}, bf16[2,560,128]{2,1,0:T(8,128)(2,1)S(1)}, u32[]{:S(2)}, u32[]{:S(2)}) collective-permute-start(bf16[2,560,128]{2,1,0:T(8,128)(2,1)S(1)} %get-tuple-element.33), channel_id=1, source_target_pairs={{0,1},{1,0},{2,3},{3,2},{4,5},{5,4},{6,7},{7,6},{8,9},{9,8},{10,11... | collective-permute-start | bytes 860168 | tf_op jit(solution)/shard_map/ppermute | solution.py:297
  78.2 20.1 %collective-permute-start.10 = (bf16[2,560,128]{2,1,0:T(8,128)(2,1)S(1)}, bf16[2,560,128]{2,1,0:T(8,128)(2,1)S(1)}, u32[]{:S(2)}, u32[]{:S(2)}) collective-permute-start(bf16[2,560,128]{2,1,0:T(8,128)(2,1)S(1)} %get-tuple-element.34), channel_id=1, source_target_pairs={{0,2},{1,3},{2,0},{3,1},{4,6},{5,7},{6,4},{7,5},{8,10},{9,11},{10,... | collective-permute-start | bytes 860168 | tf_op jit(solution)/shard_map/ppermute | solution.py:297
  79.7 30.4 %collective-permute-start.19 = (bf16[192,1120]{1,0:T(8,128)(2,1)S(1)}, bf16[192,1120]{1,0:T(8,128)(2,1)S(1)}, u32[]{:S(2)}, u32[]{:S(2)}) collective-permute-start(bf16[192,1120]{1,0:T(8,128)(2,1)S(1)} %collective-permute-done.13.refs_3_), channel_id=1, source_target_pairs={{0,16},{16,0},{1,17},{17,1},{2,18},{18,2},{3,19},{19,3},{4,20},{20... | collective-permute-start | bytes 1290248 | tf_op jit(solution)/shard_map/ppermute | solution.py:297
  84.3 26.1 %collective-permute-start.20 = (bf16[192,1120]{1,0:T(8,128)(2,1)S(1)}, bf16[192,1120]{1,0:T(8,128)(2,1)S(1)}, u32[]{:S(2)}, u32[]{:S(2)}) collective-permute-start(bf16[192,1120]{1,0:T(8,128)(2,1)S(1)} %collective-permute-done.14.refs_4_), channel_id=1, source_target_pairs={{0,16},{16,0},{1,17},{17,1},{2,18},{18,2},{3,19},{19,3},{4,20},{20... | collective-permute-start | bytes 1290248 | tf_op jit(solution)/shard_map/ppermute | solution.py:297
  93.0 16.2 %collective-permute-start.15 = (bf16[176,1120]{1,0:T(8,128)(2,1)S(1)}, bf16[176,1120]{1,0:T(8,128)(2,1)S(1)}, u32[]{:S(2)}, u32[]{:S(2)}) collective-permute-start(bf16[176,1120]{1,0:T(8,128)(2,1)S(1)} %collective-permute-done.12.refs_2_), channel_id=1, source_target_pairs={{0,1},{1,0},{2,3},{3,2},{4,5},{5,4},{6,7},{7,6},{8,9},{9,8},{10,11... | collective-permute-start | bytes 1182728 | tf_op jit(solution)/shard_map/ppermute | solution.py:297
  93.0 0.7 copy-start.13
  93.7 17.0 %collective-permute-start.18 = (bf16[176,1120]{1,0:T(8,128)(2,1)S(1)}, bf16[176,1120]{1,0:T(8,128)(2,1)}, u32[]{:S(2)}, u32[]{:S(2)}) collective-permute-start(bf16[176,1120]{1,0:T(8,128)(2,1)S(1)} %collective-permute-done.12.refs_2_), channel_id=1, source_target_pairs={{0,16},{16,0},{1,17},{17,1},{2,18},{18,2},{3,19},{19,3},{4,20},{20... | collective-permute-start | bytes 1182728 | tf_op jit(solution)/shard_map/ppermute | solution.py:297
  95.2 0.7 copy-start.3
  98.4 0.7 copy-start.7
  99.1 9.1 %collective-permute-start.11 = (bf16[2,560,128]{2,1,0:T(8,128)(2,1)S(1)}, bf16[2,560,128]{2,1,0:T(8,128)(2,1)S(1)}, u32[]{:S(2)}, u32[]{:S(2)}) collective-permute-start(bf16[2,560,128]{2,1,0:T(8,128)(2,1)S(1)} %get-tuple-element.35), channel_id=1, source_target_pairs={{0,3},{1,2},{2,1},{3,0},{4,7},{5,6},{6,5},{7,4},{8,11},{9,10},{10,... | collective-permute-start | bytes 860168 | tf_op jit(solution)/shard_map/ppermute | solution.py:297
  108.2 0.7 copy-start.9
  108.9 9.8 %collective-permute-start.16 = (bf16[192,1120]{1,0:T(8,128)(2,1)S(1)}, bf16[192,1120]{1,0:T(8,128)(2,1)S(1)}, u32[]{:S(2)}, u32[]{:S(2)}) collective-permute-start(bf16[192,1120]{1,0:T(8,128)(2,1)S(1)} %collective-permute-done.13.refs_3_), channel_id=1, source_target_pairs={{0,1},{1,0},{2,3},{3,2},{4,5},{5,4},{6,7},{7,6},{8,9},{9,8},{10,11... | collective-permute-start | bytes 1290248 | tf_op jit(solution)/shard_map/ppermute | solution.py:297
  109.1 0.7 copy-start.5
  109.9 8.8 %collective-permute-start.17 = (bf16[192,1120]{1,0:T(8,128)(2,1)S(1)}, bf16[192,1120]{1,0:T(8,128)(2,1)S(1)}, u32[]{:S(2)}, u32[]{:S(2)}) collective-permute-start(bf16[192,1120]{1,0:T(8,128)(2,1)S(1)} %collective-permute-done.14.refs_4_), channel_id=1, source_target_pairs={{0,1},{1,0},{2,3},{3,2},{4,5},{5,4},{6,7},{7,6},{8,9},{9,8},{10,11... | collective-permute-start | bytes 1290248 | tf_op jit(solution)/shard_map/ppermute | solution.py:297
  110.1 8.6 %collective-permute-start.22 = (bf16[192,1120]{1,0:T(8,128)(2,1)S(1)}, bf16[192,1120]{1,0:T(8,128)(2,1)S(1)}, u32[]{:S(2)}, u32[]{:S(2)}) collective-permute-start(bf16[192,1120]{1,0:T(8,128)(2,1)S(1)} %collective-permute-done.19.refs_9_), channel_id=1, source_target_pairs={{0,1},{1,0},{2,3},{3,2},{4,5},{5,4},{6,7},{7,6},{8,9},{9,8},{10,11... | collective-permute-start | bytes 1290248 | tf_op jit(solution)/shard_map/ppermute | solution.py:297
  110.4 8.3 %collective-permute-start.23 = (bf16[192,1120]{1,0:T(8,128)(2,1)S(1)}, bf16[192,1120]{1,0:T(8,128)(2,1)S(1)}, u32[]{:S(2)}, u32[]{:S(2)}) collective-permute-start(bf16[192,1120]{1,0:T(8,128)(2,1)S(1)} %collective-permute-done.20.refs_10_), channel_id=1, source_target_pairs={{0,1},{1,0},{2,3},{3,2},{4,5},{5,4},{6,7},{7,6},{8,9},{9,8},{10,11... | collective-permute-start | bytes 1290248 | tf_op jit(solution)/shard_map/ppermute | solution.py:297
  110.7 8.0 %collective-permute-start.21 = (bf16[176,1120]{1,0:T(8,128)(2,1)}, bf16[176,1120]{1,0:T(8,128)(2,1)}, u32[]{:S(2)}, u32[]{:S(2)}) collective-permute-start(bf16[176,1120]{1,0:T(8,128)(2,1)} %collective-permute-done.18.refs_8_), channel_id=1, source_target_pairs={{0,1},{1,0},{2,3},{3,2},{4,5},{5,4},{6,7},{7,6},{8,9},{9,8},{10,11... | collective-permute-start | bytes 1182728 | tf_op jit(solution)/shard_map/ppermute | solution.py:297
  111.0 1.0 copy-start.12
  112.0 1.0 copy-start.14
  112.9 5.8 %copy-start.4 = (bf16[176,1120]{1,0:T(8,128)(2,1)S(1)}, bf16[176,1120]{1,0:T(8,128)(2,1)}, u32[]{:S(2)}) copy-start(bf16[176,1120]{1,0:T(8,128)(2,1)} %copy-done.3) | copy-start | bytes 1182724
  112.9 5.8 %copy-start.6 = (bf16[176,1120]{1,0:T(8,128)(2,1)S(1)}, bf16[176,1120]{1,0:T(8,128)(2,1)}, u32[]{:S(2)}) copy-start(bf16[176,1120]{1,0:T(8,128)(2,1)} %copy-done.5) | copy-start | bytes 1182724
  112.9 5.8 %copy-start.8 = (bf16[2,560,128]{2,1,0:T(8,128)(2,1)S(1)}, bf16[2,560,128]{2,1,0:T(8,128)(2,1)}, u32[]{:S(2)}) copy-start(bf16[2,560,128]{2,1,0:T(8,128)(2,1)} %copy-done.7) | copy-start | bytes 860164
  112.9 5.8 %copy-start.10 = (bf16[2,560,128]{2,1,0:T(8,128)(2,1)S(1)}, bf16[2,560,128]{2,1,0:T(8,128)(2,1)}, u32[]{:S(2)}) copy-start(bf16[2,560,128]{2,1,0:T(8,128)(2,1)} %copy-done.9) | copy-start | bytes 860164
  117.3 1.4 %copy-start = (f32[2,2240,128]{2,1,0:T(8,128)}, f32[2,2240,128]{2,1,0:T(8,128)S(1)}, u32[]{:S(2)}) copy-start(f32[2,2240,128]{2,1,0:T(8,128)S(1)} %mix.1.own_ref) | copy-start | bytes 6881284

commit v2 on v0

--- a/solution.py
+++ b/solution.py
@@ -16,7 +16,7 @@
     return pl.CostEstimate(flops=int(flops), bytes_accessed=int(nbytes), transcendentals=0)
 
 
-def params(mib=48):
+def params(mib=24):
     return pltpu.CompilerParams(vmem_limit_bytes=mib << 20)
 
 
@@ -167,87 +167,119 @@
     )(end, states, head_gain, *priors, *[a for a, _, _ in queries])
 
 
-def turn(pieces):
-    n = len(pieces)
-    group, width = pieces[0].shape
-
-    def kernel(*refs):
-        for k in range(n):
-            refs[n][:, k * group : (k + 1) * group] = refs[k][...].T
-
-    return pl.pallas_call(
-        kernel,
-        in_specs=[VMEM] * n,
-        out_specs=VMEM,
-        out_shape=jax.ShapeDtypeStruct((width, n * group), BF16),
-        compiler_params=params(),
-        cost_estimate=cost(0, 4 * n * group * width),
-        name="turn",
-    )(*pieces)
-
-
-def mix(weights, heads_out, start, stop, dtype):
-    n = len(heads_out)
-    frames, group, lanes = heads_out[0].shape
-
-    def kernel(w_ref, *refs):
-        out, both = refs[n], refs[n + 1]
-        for k in range(n):
-            for f in range(frames):
-                both[k * group : (k + 1) * group, f * lanes : (f + 1) * lanes] = refs[k][f]
-        total = dot(w_ref[start:stop, :], both[...])
-        for f in range(frames):
-            out[f] = total[:, f * lanes : (f + 1) * lanes].astype(dtype)
-
-    return pl.pallas_call(
-        kernel,
-        in_specs=[VMEM] * (1 + n),
-        out_specs=VMEM,
-        out_shape=jax.ShapeDtypeStruct((frames, stop - start, lanes), dtype),
-        scratch_shapes=[pltpu.VMEM((n * group, frames * lanes), BF16)],
-        compiler_params=params(),
-        cost_estimate=cost(2 * n * (stop - start) * group * frames * lanes, 2 * n * (stop - start) * group),
-        name="mix",
-    )(weights, *heads_out)
-
-
-def finish(buffer, own, arrived, start, whole_shape):
-    n = len(arrived)
-    frames, rows, lanes = arrived[0].shape
-
-    def kernel(*refs):
-        own_ref, got, out, staged, sem = refs[0], refs[1 : 1 + n], refs[-3], refs[-2], refs[-1]
-        copies = []
-        for f in range(frames):
-            total = own_ref[f, start : start + rows, :]
-            for g in got:
-                total = total + g[f].astype(F32)
-            staged[f] = total.astype(BF16)
-            copies.append(pltpu.make_async_copy(staged.at[f], out.at[f, pl.ds(start, rows), :], sem.at[f]))
+def cut(source, start, sizes, aligned):
+    width = source.shape[-1]
+
+    def kernel(start_ref, src, *rest):
+        outs, sem = rest[: len(sizes)], rest[-1]
+        copies, at = [], 0
+        for k, (out, n) in enumerate(zip(outs, sizes)):
+            if source.ndim == 3:
+                view = src.at[start]
+            else:
+                view = src.at[pl.ds(pl.multiple_of(start_ref[0] + at, aligned), n), :]
+            copies.append(pltpu.make_async_copy(view, out, sem.at[k]))
             copies[-1].start()
+            at += n
         for c in copies:
             c.wait()
 
-    given = [own, *arrived] + ([] if buffer is None else [buffer])
-    return pl.pallas_call(
-        kernel,
-        in_specs=[VMEM] * (1 + n) + ([] if buffer is None else [pl.BlockSpec(memory_space=pl.ANY)]),
-        out_specs=pl.BlockSpec(memory_space=pl.ANY),
-        out_shape=jax.ShapeDtypeStruct(whole_shape, BF16),
-        scratch_shapes=[pltpu.VMEM((frames, rows, lanes), BF16), pltpu.SemaphoreType.DMA((frames,))],
-        input_output_aliases={} if buffer is None else {1 + n: 0},
-        compiler_params=params(),
-        cost_estimate=cost(0, 8 * frames * rows * lanes),
+    where = jnp.zeros((1,), jnp.int32) if source.ndim == 3 else start.reshape(1)
+    return pl.pallas_call(
+        kernel,
+        in_specs=[pl.BlockSpec(memory_space=pltpu.SMEM), pl.BlockSpec(memory_space=pl.ANY)],
+        out_specs=[VMEM] * len(sizes),
+        out_shape=[jax.ShapeDtypeStruct((n, width), source.dtype) for n in sizes],
+        scratch_shapes=[pltpu.SemaphoreType.DMA((len(sizes),))],
+        compiler_params=params(),
+        cost_estimate=cost(0, 4 * sum(sizes) * width),
+        name="cut",
+    )(where, source)
+
+
+def tokens_first(refs):
+    frames = refs[0].shape[0]
+    return [jnp.concatenate([r[f] for r in refs], axis=0).T for f in range(frames)]
+
+
+def mix(rows, heads_out):
+    frames, group, lanes = heads_out[0].shape
+    width = rows[0].shape[1]
+    n = len(rows)
+
+    def kernel(*refs):
+        out = refs[2 * n]
+        total = None
+        for w, x in zip(refs[:n], refs[n : 2 * n]):
+            left = jnp.concatenate(tokens_first([x]), axis=0)
+            term = dot(left, w[...])
+            total = term if total is None else total + term
+        out[...] = total
+
+    return pl.pallas_call(
+        kernel,
+        in_specs=[VMEM] * (2 * n),
+        out_specs=VMEM,
+        out_shape=jax.ShapeDtypeStruct((frames * lanes, width), F32),
+        compiler_params=params(),
+        cost_estimate=cost(4 * width * group * frames * lanes, 4 * width * group),
+        name="mix",
+    )(*rows, *heads_out)
+
+
+def finish(starts, own, chips, shape):
+    frames, width, lanes = shape
+    group = chips[0][0][0].shape[1]
+    given, plan = [], []
+    for heads_out, cores in chips:
+        plan.append((len(given), []))
+        given += heads_out
+        for core, lists in enumerate(cores):
+            for g, pieces in enumerate(lists):
+                at = 0
+                for p in pieces:
+                    plan[-1][1].append((len(given), core, g, at))
+                    given.append(p)
+                    at += p.shape[0]
+    n = len(given)
+    step = 640 if width > 640 else width
+    spans = [(a, min(a + step, width)) for a in range(0, width, step)]
+
+    def kernel(start_ref, own_ref, *refs):
+        out, w = refs[n], refs[n + 1]
+        lefts = []
+        for k, (first, pieces) in enumerate(plan):
+            for i, core, g, at in pieces:
+                row = pl.multiple_of(start_ref[g] + (core * group + at), 16)
+                w[k, pl.ds(row, refs[i].shape[0]), :] = refs[i][...]
+            lefts.append(jnp.concatenate(tokens_first(refs[first : first + 2]), axis=0))
+        for a, b in spans:
+            total = own_ref[:, a:b]
+            for k, left in enumerate(lefts):
+                total = total + dot(left, w[k, :, a:b])
+            total = total.astype(BF16)
+            for f in range(frames):
+                out[f, a:b, :] = total[f * lanes : (f + 1) * lanes].T
+
+    return pl.pallas_call(
+        kernel,
+        in_specs=[pl.BlockSpec(memory_space=pltpu.SMEM)] + [VMEM] * (1 + n),
+        out_specs=VMEM,
+        out_shape=jax.ShapeDtypeStruct(shape, BF16),
+        scratch_shapes=[pltpu.VMEM((len(chips), 2 * group, width), BF16)],
+        compiler_params=params(),
+        cost_estimate=cost(4 * len(chips) * width * group * frames * lanes, 4 * len(chips) * width * group),
         name="finish",
-    )(*given)
-
-
-CUTS = (0.0, 0.25, 0.75, 1.0)
-
-
-def per_device(n_row, n_frm, hidden_in, norm_gain, qkv_weight, head_gain, output_matrix, block_end):
-    def swap(v, k):
-        return lax.ppermute(v, "row", [(i, i ^ k) for i in range(n_row)])
+    )(starts, own, *given)
+
+
+PIECES = 3
+
+
+def per_device(n_grp, n_row, n_frm, hidden_in, norm_gain, qkv_weight, head_gain, output_matrix, block_end):
+    def swap(v, k, axis="row"):
+        size = {"row": n_row, "grp": n_grp}[axis]
+        return lax.ppermute(v, axis, [(i, i ^ k) for i in range(size)])
 
     def shift(v, s):
         return lax.ppermute(v, "frm", [(i, i + s) for i in range(n_frm - s)])
@@ -261,15 +293,33 @@
     pairs = n_row // 2
     crossed = {}
     for f in range(frames):
+        (frame,) = cut(tokens, f, [features], 1)
         for k in range(1, pairs):
-            crossed[k, f] = swap(tokens[f], 2 * k)
+            crossed[k, f] = swap(frame, 2 * k)
     sibling = swap(tokens, 1)
     passed = {key: swap(v, 1) for key, v in crossed.items()}
 
     where = [[(0, f), (1, f)] for f in range(frames)]
     states, near_q = project([tokens, sibling], where, gain, weights, None, frames)
-    turned = turn([output_matrix, swap(output_matrix, 1)])
-    states, turned = lax.optimization_barrier((states, turned))
+
+    group, width = output_matrix.shape
+    grp = lax.axis_index("grp")
+    share = -(-group // (16 * n_grp)) * 16
+    stride = (group - share) // max(n_grp - 1, 1)
+    sizes = [share // 16 * (j + 1) // PIECES * 16 - share // 16 * j // PIECES * 16 for j in range(PIECES)]
+    pieces = cut(output_matrix, grp * stride, sizes, 16)
+    near_rows = swap(output_matrix, 1)
+    starts = jnp.stack([(grp ^ g) * stride for g in range(n_grp)])
+    far_rows = []
+    for k in range(1, pairs):
+        held = {}
+        for j, piece in enumerate(pieces):
+            held[0, 0, j] = swap(piece, 2 * k)
+            for g in range(1, n_grp):
+                held[0, g, j] = swap(held[0, 0, j], g, "grp")
+            for g in range(n_grp):
+                held[1, g, j] = swap(held[0, g, j], 1)
+        far_rows.append([[[held[c, g, j] for j in range(PIECES)] for g in range(n_grp)] for c in range(2)])
     queries = []
     for f in range(frames):
         for k in range(1, pairs):
@@ -292,22 +342,11 @@
     queries.append((near_q, {f: f for f in range(frames)}, 0))
     heads_out = attend(block_end, states, priors, out_gain, queries, lanes)
 
-    got = {}
-    for k in list(range(1, pairs)) + [0]:
-        got[k] = swap(heads_out[2 * k + 1], 1)
-    width = output_matrix.shape[1]
-    cuts = [int(c * width) // 16 * 16 for c in CUTS]
-    spans = list(zip(cuts[:-1], cuts[1:]))
-    arrived = []
-    for i, (start, stop) in enumerate(spans):
-        arrived.append([])
-        for k in range(1, pairs):
-            part = mix(turned, (heads_out[2 * k], got[k]), start, stop, BF16)
-            arrived[i].append(swap(part, 2 * k))
-    own = mix(turned, (heads_out[0], got[0]), 0, width, F32)
-    out = None
-    for (start, stop), parts in zip(spans, arrived):
-        out = finish(out, own, parts, start, (frames, width, lanes))
+    across = []
+    for k in range(1, pairs):
+        across.append((swap(heads_out[2 * k], 2 * k), swap(heads_out[2 * k + 1], 2 * k + 1)))
+    own = mix([output_matrix, near_rows], [heads_out[0], swap(heads_out[1], 1)])
+    out = finish(starts, own, list(zip(across, far_rows)), (frames, width, lanes))
     return jnp.transpose(out, (2, 0, 1))
 
 
@@ -322,7 +361,7 @@
     )
 
     def body(*args):
-        return per_device(mesh.shape["row"], mesh.shape["frm"], *args)
+        return per_device(mesh.shape["grp"], mesh.shape["row"], mesh.shape["frm"], *args)
 
     return jax.shard_map(
         body, mesh=mesh, in_specs=placed, out_specs=P("row", ("grp", "frm"), None), check_vma=False

time: 107 us -> 121 us (1.13)
  Pallas kernels: 41.9 us -> 23.3 us
  waiting for transfers between devices: 44.4 us -> 56.5 us
  starting transfers between devices: 16.9 us -> 28.1 us
  local copies, waits for them, and re-layouts: 1.82 us -> 11.2 us
    ppermute x11 -> x21, waiting for transfers between devices: 43.5 us -> 54.6 us  [swap(): return lax.ppermute(v, axis, [(i, i ^ k) for i in range(size)])]
    unnamed x14 -> x40, local copies, waits for them, and re-layouts: 0.04 us -> 10.7 us
    pallas_call x3, Pallas kernels: 20.3 us -> 10.3 us  [project(): pl.pallas_call(kernel, in_specs=[VMEM] * len(given), out_specs=[VMEM] * l...]
    ppermute x11 -> x21, starting transfers between devices: 7.41 us -> 17 us  [swap(): return lax.ppermute(v, axis, [(i, i ^ k) for i in range(size)])]
    pallas_call x8 -> x5, Pallas kernels: 16 us -> 10.2 us  [the longest x1 5.32 us: finish(): pl.pallas_call(kernel, in_specs=[pl.BlockSpec(memory_space=pltpu.SMEM)] +...]
    pallas_call x1, Pallas kernels: 4.12 us -> 0.84 us  [query(): pl.pallas_call(kernel, in_specs=[VMEM] * 2, out_specs=VMEM, out_shape=jax...]
    ppermute x3, starting transfers between devices: 9.53 us -> 11.1 us  [shift(): return lax.ppermute(v, 'frm', [(i, i + s) for i in range(n_frm - s)])]
    squeeze x1 -> x0, local copies, waits for them, and re-layouts: 1.31 us -> none  [per_device(): crossed[k, f] = swap(tokens[f], 2 * k)]
  transfers between devices with their start and end apart: 14 -> 24, of which waited for: 6 -> 8; matrix products, arithmetic and copies ran while one was open for 2% -> 0% of each run, Pallas kernels for 29% -> 15%
where the time goes in v2:
time: 121 us; the launch traced here: 119 us
  waiting for transfers between devices  56.5 us (47%)
  starting transfers between devices  28.1 us (23%)
  Pallas kernels  23.3 us (19%)
  local copies, waits for them, and re-layouts  11.2 us (9%)
    ppermute x21, waiting for transfers between devices, swap(): return lax.ppermute(v, axis, [(i, i ^ k) for i in range(size)])  54.6 us
    ppermute x21, starting transfers between devices, swap(): return lax.ppermute(v, axis, [(i, i ^ k) for i in range(size)])  17 us
    ppermute x3, starting transfers between devices, shift(): return lax.ppermute(v, 'frm', [(i, i + s) for i in range(n_frm - s)])  11.1 us
    unnamed x40, local copies, waits for them, and re-layouts  10.7 us
    pallas_call x3, Pallas kernels, project(): pl.pallas_call(kernel, in_specs=[VMEM] * len(given), out_specs=[VMEM] * l...  10.3 us
    pallas_call x1, Pallas kernels, finish(): pl.pallas_call(kernel, in_specs=[pl.BlockSpec(memory_space=pltpu.SMEM)] +...  5.32 us
    pallas_call x1, Pallas kernels, mix(): pl.pallas_call(kernel, in_specs=[VMEM] * (2 * n), out_specs=VMEM, out_sha...  3.89 us
  transfers between devices with their start and end apart: 24, of which 8 were waited for; matrix products, arithmetic and copies ran while one was open for 0% of the time, Pallas kernels for 15%

profile of v2, /device:TPU:0, one launch (start us, length us, event | category | flops | bytes accessed | tf_op | source)
XLA Modules:
  0.0 119.4 jit_solution(16415765170073977746)
XLA Ops:
  0.0 0.5 collective-permute-start
  0.5 0.0 collective-permute-start.5
  0.5 1.7 %copy-done.2 = bf16[560,2240]{1,0:T(8,128)(2,1)S(1)} copy-done((bf16[560,2240]{1,0:T(8,128)(2,1)S(1)}, bf16[560,2240]{1,0:T(8,128)(2,1)}, u32[]{:S(2)}) %copy-start.2) | copy-done | bytes 2508824
  2.2 0.8 cut.5
  3.0 3.0 %collective-permute-start.12 = (bf16[96,2240]{1,0:T(8,128)(2,1)S(1)}, bf16[96,2240]{1,0:T(8,128)(2,1)S(1)}, u32[]{:S(2)}, u32[]{:S(2)}) collective-permute-start(bf16[96,2240]{1,0:T(8,128)(2,1)S(1)} %get-tuple-element.30), channel_id=1, source_target_pairs={{0,2},{1,3},{2,0},{3,1},{4,6},{5,7},{6,4},{7,5},{8,10},{9,11},{10,... | collective-permute-start | bytes 1290248 | tf_op jit(solution)/shard_map/ppermute | solution.py:282
  6.1 0.1 collective-permute-start.13
  6.2 0.1 cut.4
  6.3 0.0 copy-start.18
  6.3 2.0 %collective-permute-start.3 = (bf16[2240,128]{1,0:T(8,128)(2,1)S(1)}, bf16[2240,128]{1,0:T(8,128)(2,1)S(1)}, u32[]{:S(2)}, u32[]{:S(2)}) collective-permute-start(bf16[2240,128]{1,0:T(8,128)(2,1)S(1)} %cut.4), channel_id=1, source_target_pairs={{0,2},{1,3},{2,0},{3,1},{4,6},{5,7},{6,4},{7,5},{8,10},{9,11},{10,... | collective-permute-start | bytes 1720328 | tf_op jit(solution)/shard_map/ppermute | solution.py:282
  8.3 0.1 cut.3
  8.4 8.7 %collective-permute-done.12.refs_2_ = bf16[96,2240]{1,0:T(8,128)(2,1)S(1)} collective-permute-done((bf16[96,2240]{1,0:T(8,128)(2,1)S(1)}, bf16[96,2240]{1,0:T(8,128)(2,1)S(1)}, u32[]{:S(2)}, u32[]{:S(2)}) %collective-permute-start.12) | collective-permute-done | bytes 430112 | tf_op jit(solution)/shard_map/ppermute | solution.py:282
  17.1 2.0 %collective-permute-start.1 = (bf16[2240,128]{1,0:T(8,128)(2,1)S(1)}, bf16[2240,128]{1,0:T(8,128)(2,1)S(1)}, u32[]{:S(2)}, u32[]{:S(2)}) collective-permute-start(bf16[2240,128]{1,0:T(8,128)(2,1)S(1)} %cut.3), channel_id=1, source_target_pairs={{0,2},{1,3},{2,0},{3,1},{4,6},{5,7},{6,4},{7,5},{8,10},{9,11},{10,... | collective-permute-start | bytes 1720328 | tf_op jit(solution)/shard_map/ppermute | solution.py:282
  19.1 7.5 %collective-permute-done.13.refs_3_ = bf16[96,2240]{1,0:T(8,128)(2,1)S(1)} collective-permute-done((bf16[96,2240]{1,0:T(8,128)(2,1)S(1)}, bf16[96,2240]{1,0:T(8,128)(2,1)S(1)}, u32[]{:S(2)}, u32[]{:S(2)}) %collective-permute-start.13) | collective-permute-done | bytes 430112 | tf_op jit(solution)/shard_map/ppermute | solution.py:282
  26.6 2.0 %collective-permute-start.14 = (bf16[96,2240]{1,0:T(8,128)(2,1)S(1)}, bf16[96,2240]{1,0:T(8,128)(2,1)S(1)}, u32[]{:S(2)}, u32[]{:S(2)}) collective-permute-start(bf16[96,2240]{1,0:T(8,128)(2,1)S(1)} %get-tuple-element.32), channel_id=1, source_target_pairs={{0,2},{1,3},{2,0},{3,1},{4,6},{5,7},{6,4},{7,5},{8,10},{9,11},{10,... | collective-permute-start | bytes 1290248 | tf_op jit(solution)/shard_map/ppermute | solution.py:282
  28.6 10.3 %collective-permute-done.3.refs_0_ = bf16[2240,128]{1,0:T(8,128)(2,1)S(1)} collective-permute-done((bf16[2240,128]{1,0:T(8,128)(2,1)S(1)}, bf16[2240,128]{1,0:T(8,128)(2,1)S(1)}, u32[]{:S(2)}, u32[]{:S(2)}) %collective-permute-start.3) | collective-permute-done | bytes 573472 | tf_op jit(solution)/shard_map/ppermute | solution.py:282
  38.9 0.0 collective-permute-start.4
  38.9 12.3 %collective-permute-done.1.refs_0_ = bf16[2240,128]{1,0:T(8,128)(2,1)S(1)} collective-permute-done((bf16[2240,128]{1,0:T(8,128)(2,1)S(1)}, bf16[2240,128]{1,0:T(8,128)(2,1)S(1)}, u32[]{:S(2)}, u32[]{:S(2)}) %collective-permute-start.1) | collective-permute-done | bytes 573472 | tf_op jit(solution)/shard_map/ppermute | solution.py:282
  51.2 0.3 reshape.13.refs_2_
  51.5 8.4 %collective-permute-done.14.refs_4_ = bf16[96,2240]{1,0:T(8,128)(2,1)S(1)} collective-permute-done((bf16[96,2240]{1,0:T(8,128)(2,1)S(1)}, bf16[96,2240]{1,0:T(8,128)(2,1)S(1)}, u32[]{:S(2)}, u32[]{:S(2)}) %collective-permute-start.14) | collective-permute-done | bytes 430112 | tf_op jit(solution)/shard_map/ppermute | solution.py:282
  59.9 1.8 %collective-permute-start.15 = (bf16[96,2240]{1,0:T(8,128)(2,1)S(1)}, bf16[96,2240]{1,0:T(8,128)(2,1)}, u32[]{:S(2)}, u32[]{:S(2)}) collective-permute-start(bf16[96,2240]{1,0:T(8,128)(2,1)S(1)} %collective-permute-done.12.refs_2_), channel_id=1, source_target_pairs={{0,16},{16,0},{1,17},{17,1},{2,18},{18,2},{3,19},{19,3},{4,20},{20... | collective-permute-start | bytes 1290248 | tf_op jit(solution)/shard_map/ppermute | solution.py:282
  61.7 0.0 collective-permute-done.5.refs_1_
  61.7 0.3 collective-permute-start.16
  62.0 3.2 %copy-done = bf16[2240,3,560]{0,2,1:T(8,128)(2,1)S(1)} copy-done((bf16[2240,3,560]{0,2,1:T(8,128)(2,1)S(1)}, bf16[2240,3,560]{0,2,1:T(8,128)(2,1)}, u32[]{:S(2)}) %copy-start) | copy-done | bytes 7526424
  65.2 5.1 %project.3 = (f32[2,560,112]{2,1,0:T(8,128)S(1)}, bf16[2,560,256]{2,1,0:T(8,128)(2,1)S(1)}) custom-call(bf16[2,2240,128]{2,1,0:T(8,128)(2,1)S(1)} %bitcast.14, bf16[2,2240,128]{2,1,0:T(8,128)(2,1)S(1)} %collective-permute-done.5.refs_1_, f32[2240,1]{1,0:T(8,128)S(1)} %reshape.13.refs_2_, bf16[1680,2240]{1,0:T(8,128)(2,1)S(1)} %bitcast.7), custom_call_target="tpu_custom_call" | custom-call | flops 3853516800 | bytes 2293760 | tf_op jit(solution)/shard_map/project/pallas_call | solution.py:95
  70.3 0.0 collective-permute-done.4.refs_1_
  70.3 1.8 %collective-permute-start.17 = (bf16[96,2240]{1,0:T(8,128)(2,1)S(1)}, bf16[96,2240]{1,0:T(8,128)(2,1)}, u32[]{:S(2)}, u32[]{:S(2)}) collective-permute-start(bf16[96,2240]{1,0:T(8,128)(2,1)S(1)} %collective-permute-done.14.refs_4_), channel_id=1, source_target_pairs={{0,16},{16,0},{1,17},{17,1},{2,18},{18,2},{3,19},{19,3},{4,20},{20... | collective-permute-start | bytes 1290248 | tf_op jit(solution)/shard_map/ppermute | solution.py:282
  72.1 2.9 %project.4 = (f32[2,560,112]{2,1,0:T(8,128)S(1)}, bf16[1,560,256]{2,1,0:T(8,128)(2,1)S(1)}) custom-call(bf16[2240,128]{1,0:T(8,128)(2,1)S(1)} %collective-permute-done.3.refs_0_, bf16[2240,128]{1,0:T(8,128)(2,1)S(1)} %collective-permute-done.4.refs_1_, f32[2240,1]{1,0:T(8,128)S(1)} %reshape.13.refs_2_, bf16[1680,2240]{1,0:T(8,128)(2,1)S(1)} %bitcast.8, ...), custom_call_target="tpu_custom_call" | custom-call | flops 1926758400 | bytes 1146880 | tf_op jit(solution)/shard_map/project/pallas_call | solution.py:95
  75.1 0.0 copy-start.19
  75.1 2.3 %project.5 = (f32[2,560,112]{2,1,0:T(8,128)S(1)}, bf16[560,112]{1,0:T(8,128)(2,1)S(1)}, bf16[2240,256]{1,0:T(8,128)(2,1)S(1)}) custom-call(bf16[2240,128]{1,0:T(8,128)(2,1)S(1)} %collective-permute-done.1.refs_0_, bf16[2240,128]{1,0:T(8,128)(2,1)S(1)} %collective-permute-done.2.refs_1_, f32[2240,1]{1,0:T(8,128)S(1)} %reshape.13.refs_2_, ...), custom_call_target="tpu_custom_call" | custom-call | flops 1284505600 | bytes 1146880 | tf_op jit(solution)/shard_map/project/pallas_call | solution.py:95
  77.4 3.5 %collective-permute-start.6 = (bf16[560,112]{1,0:T(8,128)(2,1)S(1)}, bf16[560,112]{1,0:T(8,128)(2,1)S(1)}, u32[]{:S(2)}, u32[]{:S(2)}) collective-permute-start(bf16[560,112]{1,0:T(8,128)(2,1)S(1)} %get-tuple-element.22), channel_id=1, source_target_pairs={{0,4},{4,8},{8,12},{1,5},{5,9},{9,13},{2,6},{6,10},{10,14},{3,7},{... | collective-permute-start | bytes 376328 | tf_op jit(solution)/shard_map/ppermute | solution.py:285
  80.9 4.5 %collective-permute-start.7 = (bf16[560,112]{1,0:T(8,128)(2,1)S(1)}, bf16[560,112]{1,0:T(8,128)(2,1)S(1)}, u32[]{:S(2)}, u32[]{:S(2)}) collective-permute-start(bf16[560,112]{1,0:T(8,128)(2,1)S(1)} %get-tuple-element.22), channel_id=1, source_target_pairs={{0,8},{4,12},{1,9},{5,13},{2,10},{6,14},{3,11},{7,15},{16,24},{20,... | collective-permute-start | bytes 376328 | tf_op jit(solution)/shard_map/ppermute | solution.py:285
  85.4 0.0 collective-permute-done.16.refs_6_
  85.4 3.1 %collective-permute-start.8 = (bf16[560,112]{1,0:T(8,128)(2,1)S(1)}, bf16[560,112]{1,0:T(8,128)(2,1)S(1)}, u32[]{:S(2)}, u32[]{:S(2)}) collective-permute-start(bf16[560,112]{1,0:T(8,128)(2,1)S(1)} %get-tuple-element.22), channel_id=1, source_target_pairs={{0,12},{1,13},{2,14},{3,15},{16,28},{17,29},{18,30},{19,31}} | collective-permute-start | bytes 376328 | tf_op jit(solution)/shard_map/ppermute | solution.py:285
  88.5 0.0 collective-permute-done.6.rest_0_
  88.5 0.1 collective-permute-start.18
  88.6 0.0 collective-permute-done.7.rest_1_
  88.6 0.5 collective-permute-start.19
  89.1 1.9 %collective-permute-done.8.rest_2_ = bf16[560,112]{1,0:T(8,128)(2,1)S(1)} collective-permute-done((bf16[560,112]{1,0:T(8,128)(2,1)S(1)}, bf16[560,112]{1,0:T(8,128)(2,1)S(1)}, u32[]{:S(2)}, u32[]{:S(2)}) %collective-permute-start.8) | collective-permute-done | bytes 125472 | tf_op jit(solution)/shard_map/ppermute | solution.py:285
  91.0 0.0 collective-permute-start.20
  91.0 0.1 reshape.14.gain_ref
  91.1 0.0 copy-start.17
  91.1 0.0 copy-start.3
  91.1 0.8 query.1.rest_4_
  92.0 1.9 %attend.1 = (bf16[2,560,128]{2,1,0:T(8,128)(2,1)S(1)}, bf16[2,560,128]{2,1,0:T(8,128)(2,1)S(1)}, bf16[2,560,128]{2,1,0:T(8,128)(2,1)}, bf16[2,560,128]{2,1,0:T(8,128)(2,1)}) custom-call(s32[2]{0:T(128)S(1)} %copy-done.17, f32[2,560,112]{2,1,0:T(8,128)S(1)} %get-tuple-element.21.state_ref, f32[560,1]{1,0:T(8,128)S(1)} %reshape.14.gain_ref, ...), custom_call_target="tpu_custom_call" | custom-call | flops 128450560 | bytes 2293760 | tf_op jit(solution)/shard_map/attend/pallas_call | solution.py:158
  93.9 0.8 copy-done.13
  94.7 0.0 collective-permute-done.17.refs_7_
  94.7 0.5 collective-permute-start.9
  95.2 0.8 copy-done.7
  95.9 0.0 collective-permute-start.21
  96.0 0.8 copy-done.9
  96.8 0.5 collective-permute-start.22
  97.3 0.0 collective-permute-done.20.refs_10_
  97.3 0.8 copy-done.11
  98.0 0.0 collective-permute-start.23
  98.1 0.7 copy-done.15
  98.8 1.5 %collective-permute-start.10 = (bf16[2,560,128]{2,1,0:T(8,128)(2,1)}, bf16[2,560,128]{2,1,0:T(8,128)(2,1)}, u32[]{:S(2)}, u32[]{:S(2)}) collective-permute-start(bf16[2,560,128]{2,1,0:T(8,128)(2,1)} %get-tuple-element.28), channel_id=1, source_target_pairs={{0,2},{1,3},{2,0},{3,1},{4,6},{5,7},{6,4},{7,5},{8,10},{9,11},{10,... | collective-permute-start | bytes 860168 | tf_op jit(solution)/shard_map/ppermute | solution.py:282
  100.3 0.4 collective-permute-start.11
  100.7 0.1 pad_add_fusion.start_ref
  100.7 1.0 copy-done.14
  101.7 1.0 copy-done.16
  102.7 3.9 %mix.1.own_ref = f32[256,2240]{1,0:T(8,128)S(1)} custom-call(bf16[560,2240]{1,0:T(8,128)(2,1)S(1)} %copy-done.3, bf16[560,2240]{1,0:T(8,128)(2,1)} %collective-permute-done.refs_1_, bf16[2,560,128]{2,1,0:T(8,128)(2,1)S(1)} %copy-done.14, bf16[2,560,128]{2,1,0:T(8,128)(2,1)S(1)} %copy-done.16), custom_call_target="tpu_custom_call" | custom-call | flops 1284505600 | bytes 5017600 | tf_op jit(solution)/shard_map/mix/pallas_call | solution.py:219
  106.6 2.2 %collective-permute-done.10.refs_0_ = bf16[2,560,128]{2,1,0:T(8,128)(2,1)} collective-permute-done((bf16[2,560,128]{2,1,0:T(8,128)(2,1)}, bf16[2,560,128]{2,1,0:T(8,128)(2,1)}, u32[]{:S(2)}, u32[]{:S(2)}) %collective-permute-start.10) | collective-permute-done | bytes 286752 | tf_op jit(solution)/shard_map/ppermute | solution.py:282
  108.8 5.2 %collective-permute-done.11.refs_1_ = bf16[2,560,128]{2,1,0:T(8,128)(2,1)} collective-permute-done((bf16[2,560,128]{2,1,0:T(8,128)(2,1)}, bf16[2,560,128]{2,1,0:T(8,128)(2,1)}, u32[]{:S(2)}, u32[]{:S(2)}) %collective-permute-start.11) | collective-permute-done | bytes 286752 | tf_op jit(solution)/shard_map/ppermute | solution.py:282
  114.0 5.3 %finish.1 = bf16[2,2240,128]{2,1,0:T(8,128)(2,1)} custom-call(s32[2]{0:T(128)S(1)} %pad_add_fusion.start_ref, f32[256,2240]{1,0:T(8,128)S(1)} %mix.1.own_ref, bf16[2,560,128]{2,1,0:T(8,128)(2,1)} %collective-permute-done.10.refs_0_, bf16[2,560,128]{2,1,0:T(8,128)(2,1)} %collective-permute-done.11.refs_1_, ...), custom_call_target="tpu_custom_call" | custom-call | flops 1284505600 | bytes 5017600 | tf_op jit(solution)/shard_map/finish/pallas_call | solution.py:264
  (37 shorter events, 0.1 us)
Async XLA Ops:
  0.0 100.3 %collective-permute-start = (bf16[560,2240]{1,0:T(8,128)(2,1)}, bf16[560,2240]{1,0:T(8,128)(2,1)}, u32[]{:S(2)}, u32[]{:S(2)}) collective-permute-start(bf16[560,2240]{1,0:T(8,128)(2,1)} %src.1), channel_id=1, source_target_pairs={{0,1},{1,0},{2,3},{3,2},{4,5},{5,4},{6,7},{7,6},{8,9},{9,8},{10,11... | collective-permute-start | bytes 7526408 | tf_op jit(solution)/shard_map/ppermute | solution.py:282
  0.5 61.2 %collective-permute-start.5 = (bf16[2,2240,128]{2,1,0:T(8,128)(2,1)}, bf16[2,2240,128]{2,1,0:T(8,128)(2,1)S(1)}, u32[]{:S(2)}, u32[]{:S(2)}) collective-permute-start(bf16[2,2240,128]{2,1,0:T(8,128)(2,1)} %bitcast.11), channel_id=1, source_target_pairs={{0,1},{1,0},{2,3},{3,2},{4,5},{5,4},{6,7},{7,6},{8,9},{9,8},{10,11... | collective-permute-start | bytes 3440648 | tf_op jit(solution)/shard_map/ppermute | solution.py:282
  0.5 1.7 %copy-start.2 = (bf16[560,2240]{1,0:T(8,128)(2,1)S(1)}, bf16[560,2240]{1,0:T(8,128)(2,1)}, u32[]{:S(2)}) copy-start(bf16[560,2240]{1,0:T(8,128)(2,1)} %src.1) | copy-start | bytes 7526404
  2.2 3.9 %copy-start.4 = (bf16[128,2,2240]{0,2,1:T(8,128)(2,1)S(1)}, bf16[128,2,2240]{0,2,1:T(8,128)(2,1)}, u32[]{:S(2)}) copy-start(bf16[128,2,2240]{0,2,1:T(8,128)(2,1)} %param.6) | copy-start | bytes 3440644
  3.0 14.1 %collective-permute-start.12 = (bf16[96,2240]{1,0:T(8,128)(2,1)S(1)}, bf16[96,2240]{1,0:T(8,128)(2,1)S(1)}, u32[]{:S(2)}, u32[]{:S(2)}) collective-permute-start(bf16[96,2240]{1,0:T(8,128)(2,1)S(1)} %get-tuple-element.30), channel_id=1, source_target_pairs={{0,2},{1,3},{2,0},{3,1},{4,6},{5,7},{6,4},{7,5},{8,10},{9,11},{10,... | collective-permute-start | bytes 1290248 | tf_op jit(solution)/shard_map/ppermute | solution.py:282
  6.1 20.5 %collective-permute-start.13 = (bf16[96,2240]{1,0:T(8,128)(2,1)S(1)}, bf16[96,2240]{1,0:T(8,128)(2,1)S(1)}, u32[]{:S(2)}, u32[]{:S(2)}) collective-permute-start(bf16[96,2240]{1,0:T(8,128)(2,1)S(1)} %get-tuple-element.31), channel_id=1, source_target_pairs={{0,2},{1,3},{2,0},{3,1},{4,6},{5,7},{6,4},{7,5},{8,10},{9,11},{10,... | collective-permute-start | bytes 1290248 | tf_op jit(solution)/shard_map/ppermute | solution.py:282
  6.3 44.9 %copy-start.18 = (f32[2240]{0:T(1024)S(1)}, f32[2240]{0:T(1024)}, u32[]{:S(2)}) copy-start(f32[2240]{0:T(1024)} %param.7) | copy-start | bytes 26884
  6.3 32.6 %collective-permute-start.3 = (bf16[2240,128]{1,0:T(8,128)(2,1)S(1)}, bf16[2240,128]{1,0:T(8,128)(2,1)S(1)}, u32[]{:S(2)}, u32[]{:S(2)}) collective-permute-start(bf16[2240,128]{1,0:T(8,128)(2,1)S(1)} %cut.4), channel_id=1, source_target_pairs={{0,2},{1,3},{2,0},{3,1},{4,6},{5,7},{6,4},{7,5},{8,10},{9,11},{10,... | collective-permute-start | bytes 1720328 | tf_op jit(solution)/shard_map/ppermute | solution.py:282
  17.1 34.1 %collective-permute-start.1 = (bf16[2240,128]{1,0:T(8,128)(2,1)S(1)}, bf16[2240,128]{1,0:T(8,128)(2,1)S(1)}, u32[]{:S(2)}, u32[]{:S(2)}) collective-permute-start(bf16[2240,128]{1,0:T(8,128)(2,1)S(1)} %cut.3), channel_id=1, source_target_pairs={{0,2},{1,3},{2,0},{3,1},{4,6},{5,7},{6,4},{7,5},{8,10},{9,11},{10,... | collective-permute-start | bytes 1720328 | tf_op jit(solution)/shard_map/ppermute | solution.py:282
  26.6 33.4 %collective-permute-start.14 = (bf16[96,2240]{1,0:T(8,128)(2,1)S(1)}, bf16[96,2240]{1,0:T(8,128)(2,1)S(1)}, u32[]{:S(2)}, u32[]{:S(2)}) collective-permute-start(bf16[96,2240]{1,0:T(8,128)(2,1)S(1)} %get-tuple-element.32), channel_id=1, source_target_pairs={{0,2},{1,3},{2,0},{3,1},{4,6},{5,7},{6,4},{7,5},{8,10},{9,11},{10,... | collective-permute-start | bytes 1290248 | tf_op jit(solution)/shard_map/ppermute | solution.py:282
  38.9 31.4 %collective-permute-start.4 = (bf16[2240,128]{1,0:T(8,128)(2,1)S(1)}, bf16[2240,128]{1,0:T(8,128)(2,1)S(1)}, u32[]{:S(2)}, u32[]{:S(2)}) collective-permute-start(bf16[2240,128]{1,0:T(8,128)(2,1)S(1)} %collective-permute-done.3.refs_0_), channel_id=1, source_target_pairs={{0,1},{1,0},{2,3},{3,2},{4,5},{5,4},{6,7},{7,6},{8,9},{9,8},{10,11... | collective-permute-start | bytes 1720328 | tf_op jit(solution)/shard_map/ppermute | solution.py:282
  51.1 23.9 %collective-permute-start.2 = (bf16[2240,128]{1,0:T(8,128)(2,1)S(1)}, bf16[2240,128]{1,0:T(8,128)(2,1)S(1)}, u32[]{:S(2)}, u32[]{:S(2)}) collective-permute-start(bf16[2240,128]{1,0:T(8,128)(2,1)S(1)} %collective-permute-done.1.refs_0_), channel_id=1, source_target_pairs={{0,1},{1,0},{2,3},{3,2},{4,5},{5,4},{6,7},{7,6},{8,9},{9,8},{10,11... | collective-permute-start | bytes 1720328 | tf_op jit(solution)/shard_map/ppermute | solution.py:282
  59.9 31.0 %copy-start.5 = (bf16[96,2240]{1,0:T(8,128)(2,1)}, bf16[96,2240]{1,0:T(8,128)(2,1)S(1)}, u32[]{:S(2)}) copy-start(bf16[96,2240]{1,0:T(8,128)(2,1)S(1)} %collective-permute-done.14.refs_4_) | copy-start | bytes 1290244
  59.9 20.9 %collective-permute-start.15 = (bf16[96,2240]{1,0:T(8,128)(2,1)S(1)}, bf16[96,2240]{1,0:T(8,128)(2,1)}, u32[]{:S(2)}, u32[]{:S(2)}) collective-permute-start(bf16[96,2240]{1,0:T(8,128)(2,1)S(1)} %collective-permute-done.12.refs_2_), channel_id=1, source_target_pairs={{0,16},{16,0},{1,17},{17,1},{2,18},{18,2},{3,19},{19,3},{4,20},{20... | collective-permute-start | bytes 1290248 | tf_op jit(solution)/shard_map/ppermute | solution.py:282
  61.7 23.7 %collective-permute-start.16 = (bf16[96,2240]{1,0:T(8,128)(2,1)S(1)}, bf16[96,2240]{1,0:T(8,128)(2,1)}, u32[]{:S(2)}, u32[]{:S(2)}) collective-permute-start(bf16[96,2240]{1,0:T(8,128)(2,1)S(1)} %collective-permute-done.13.refs_3_), channel_id=1, source_target_pairs={{0,16},{16,0},{1,17},{17,1},{2,18},{18,2},{3,19},{19,3},{4,20},{20... | collective-permute-start | bytes 1290248 | tf_op jit(solution)/shard_map/ppermute | solution.py:282
  62.0 3.2 %copy-start = (bf16[2240,3,560]{0,2,1:T(8,128)(2,1)S(1)}, bf16[2240,3,560]{0,2,1:T(8,128)(2,1)}, u32[]{:S(2)}) copy-start(bf16[2240,3,560]{0,2,1:T(8,128)(2,1)} %param.8) | copy-start | bytes 22579204
  65.2 7.0 %copy-start.1 = (bf16[2240,3,560]{0,2,1:T(8,128)(2,1)S(1)}, bf16[2240,3,560]{0,2,1:T(8,128)(2,1)}, u32[]{:S(2)}) copy-start(bf16[2240,3,560]{0,2,1:T(8,128)(2,1)} %param.8) | copy-start | bytes 22579204
  70.3 24.4 %collective-permute-start.17 = (bf16[96,2240]{1,0:T(8,128)(2,1)S(1)}, bf16[96,2240]{1,0:T(8,128)(2,1)}, u32[]{:S(2)}, u32[]{:S(2)}) collective-permute-start(bf16[96,2240]{1,0:T(8,128)(2,1)S(1)} %collective-permute-done.14.refs_4_), channel_id=1, source_target_pairs={{0,16},{16,0},{1,17},{17,1},{2,18},{18,2},{3,19},{19,3},{4,20},{20... | collective-permute-start | bytes 1290248 | tf_op jit(solution)/shard_map/ppermute | solution.py:282
  75.1 15.9 %copy-start.19 = (f32[560]{0:T(1024)S(1)}, f32[560]{0:T(1024)}, u32[]{:S(2)}) copy-start(f32[560]{0:T(1024)} %param.9) | copy-start | bytes 6724
  77.4 11.1 %collective-permute-start.6 = (bf16[560,112]{1,0:T(8,128)(2,1)S(1)}, bf16[560,112]{1,0:T(8,128)(2,1)S(1)}, u32[]{:S(2)}, u32[]{:S(2)}) collective-permute-start(bf16[560,112]{1,0:T(8,128)(2,1)S(1)} %get-tuple-element.22), channel_id=1, source_target_pairs={{0,4},{4,8},{8,12},{1,5},{5,9},{9,13},{2,6},{6,10},{10,14},{3,7},{... | collective-permute-start | bytes 376328 | tf_op jit(solution)/shard_map/ppermute | solution.py:285
  80.9 7.7 %collective-permute-start.7 = (bf16[560,112]{1,0:T(8,128)(2,1)S(1)}, bf16[560,112]{1,0:T(8,128)(2,1)S(1)}, u32[]{:S(2)}, u32[]{:S(2)}) collective-permute-start(bf16[560,112]{1,0:T(8,128)(2,1)S(1)} %get-tuple-element.22), channel_id=1, source_target_pairs={{0,8},{4,12},{1,9},{5,13},{2,10},{6,14},{3,11},{7,15},{16,24},{20,... | collective-permute-start | bytes 376328 | tf_op jit(solution)/shard_map/ppermute | solution.py:285
  85.4 5.6 %collective-permute-start.8 = (bf16[560,112]{1,0:T(8,128)(2,1)S(1)}, bf16[560,112]{1,0:T(8,128)(2,1)S(1)}, u32[]{:S(2)}, u32[]{:S(2)}) collective-permute-start(bf16[560,112]{1,0:T(8,128)(2,1)S(1)} %get-tuple-element.22), channel_id=1, source_target_pairs={{0,12},{1,13},{2,14},{3,15},{16,28},{17,29},{18,30},{19,31}} | collective-permute-start | bytes 376328 | tf_op jit(solution)/shard_map/ppermute | solution.py:285
  88.5 6.7 %collective-permute-start.18 = (bf16[96,2240]{1,0:T(8,128)(2,1)S(1)}, bf16[96,2240]{1,0:T(8,128)(2,1)S(1)}, u32[]{:S(2)}, u32[]{:S(2)}) collective-permute-start(bf16[96,2240]{1,0:T(8,128)(2,1)S(1)} %collective-permute-done.12.refs_2_), channel_id=1, source_target_pairs={{0,1},{1,0},{2,3},{3,2},{4,5},{5,4},{6,7},{7,6},{8,9},{9,8},{10,11... | collective-permute-start | bytes 1290248 | tf_op jit(solution)/shard_map/ppermute | solution.py:282
  88.6 7.3 %collective-permute-start.19 = (bf16[96,2240]{1,0:T(8,128)(2,1)S(1)}, bf16[96,2240]{1,0:T(8,128)(2,1)S(1)}, u32[]{:S(2)}, u32[]{:S(2)}) collective-permute-start(bf16[96,2240]{1,0:T(8,128)(2,1)S(1)} %collective-permute-done.13.refs_3_), channel_id=1, source_target_pairs={{0,1},{1,0},{2,3},{3,2},{4,5},{5,4},{6,7},{7,6},{8,9},{9,8},{10,11... | collective-permute-start | bytes 1290248 | tf_op jit(solution)/shard_map/ppermute | solution.py:282
  91.0 6.3 %collective-permute-start.20 = (bf16[96,2240]{1,0:T(8,128)(2,1)S(1)}, bf16[96,2240]{1,0:T(8,128)(2,1)S(1)}, u32[]{:S(2)}, u32[]{:S(2)}) collective-permute-start(bf16[96,2240]{1,0:T(8,128)(2,1)S(1)} %collective-permute-done.14.refs_4_), channel_id=1, source_target_pairs={{0,1},{1,0},{2,3},{3,2},{4,5},{5,4},{6,7},{7,6},{8,9},{9,8},{10,11... | collective-permute-start | bytes 1290248 | tf_op jit(solution)/shard_map/ppermute | solution.py:282
  91.1 0.9 copy-start.17
  91.1 9.6 %copy-start.3 = (bf16[560,2240]{1,0:T(8,128)(2,1)S(1)}, bf16[560,2240]{1,0:T(8,128)(2,1)}, u32[]{:S(2)}) copy-start(bf16[560,2240]{1,0:T(8,128)(2,1)} %src.1) | copy-start | bytes 7526404
  93.9 0.8 copy-start.13
  94.7 3.4 %collective-permute-start.9 = (bf16[2,560,128]{2,1,0:T(8,128)(2,1)S(1)}, bf16[2,560,128]{2,1,0:T(8,128)(2,1)S(1)}, u32[]{:S(2)}, u32[]{:S(2)}) collective-permute-start(bf16[2,560,128]{2,1,0:T(8,128)(2,1)S(1)} %get-tuple-element.27), channel_id=1, source_target_pairs={{0,1},{1,0},{2,3},{3,2},{4,5},{5,4},{6,7},{7,6},{8,9},{9,8},{10,11... | collective-permute-start | bytes 860168 | tf_op jit(solution)/shard_map/ppermute | solution.py:282
  95.2 0.8 copy-start.7
  95.9 10.6 %collective-permute-start.21 = (bf16[96,2240]{1,0:T(8,128)(2,1)}, bf16[96,2240]{1,0:T(8,128)(2,1)}, u32[]{:S(2)}, u32[]{:S(2)}) collective-permute-start(bf16[96,2240]{1,0:T(8,128)(2,1)} %collective-permute-done.15.refs_5_), channel_id=1, source_target_pairs={{0,1},{1,0},{2,3},{3,2},{4,5},{5,4},{6,7},{7,6},{8,9},{9,8},{10,11... | collective-permute-start | bytes 1290248 | tf_op jit(solution)/shard_map/ppermute | solution.py:282
  96.0 0.8 copy-start.9
  96.8 9.8 %collective-permute-start.22 = (bf16[96,2240]{1,0:T(8,128)(2,1)}, bf16[96,2240]{1,0:T(8,128)(2,1)}, u32[]{:S(2)}, u32[]{:S(2)}) collective-permute-start(bf16[96,2240]{1,0:T(8,128)(2,1)} %collective-permute-done.16.refs_6_), channel_id=1, source_target_pairs={{0,1},{1,0},{2,3},{3,2},{4,5},{5,4},{6,7},{7,6},{8,9},{9,8},{10,11... | collective-permute-start | bytes 1290248 | tf_op jit(solution)/shard_map/ppermute | solution.py:282
  97.3 0.8 copy-start.11
  98.0 8.5 %collective-permute-start.23 = (bf16[96,2240]{1,0:T(8,128)(2,1)}, bf16[96,2240]{1,0:T(8,128)(2,1)}, u32[]{:S(2)}, u32[]{:S(2)}) collective-permute-start(bf16[96,2240]{1,0:T(8,128)(2,1)} %collective-permute-done.17.refs_7_), channel_id=1, source_target_pairs={{0,1},{1,0},{2,3},{3,2},{4,5},{5,4},{6,7},{7,6},{8,9},{9,8},{10,11... | collective-permute-start | bytes 1290248 | tf_op jit(solution)/shard_map/ppermute | solution.py:282
  98.0 0.7 copy-start.15
  98.8 10.0 %collective-permute-start.10 = (bf16[2,560,128]{2,1,0:T(8,128)(2,1)}, bf16[2,560,128]{2,1,0:T(8,128)(2,1)}, u32[]{:S(2)}, u32[]{:S(2)}) collective-permute-start(bf16[2,560,128]{2,1,0:T(8,128)(2,1)} %get-tuple-element.28), channel_id=1, source_target_pairs={{0,2},{1,3},{2,0},{3,1},{4,6},{5,7},{6,4},{7,5},{8,10},{9,11},{10,... | collective-permute-start | bytes 860168 | tf_op jit(solution)/shard_map/ppermute | solution.py:282
  100.3 13.7 %collective-permute-start.11 = (bf16[2,560,128]{2,1,0:T(8,128)(2,1)}, bf16[2,560,128]{2,1,0:T(8,128)(2,1)}, u32[]{:S(2)}, u32[]{:S(2)}) collective-permute-start(bf16[2,560,128]{2,1,0:T(8,128)(2,1)} %get-tuple-element.29), channel_id=1, source_target_pairs={{0,3},{1,2},{2,1},{3,0},{4,7},{5,6},{6,5},{7,4},{8,11},{9,10},{10,... | collective-permute-start | bytes 860168 | tf_op jit(solution)/shard_map/ppermute | solution.py:282
  100.7 1.0 copy-start.14
  101.7 1.0 copy-start.16
  102.6 11.4 %copy-start.6 = (bf16[96,2240]{1,0:T(8,128)(2,1)S(1)}, bf16[96,2240]{1,0:T(8,128)(2,1)}, u32[]{:S(2)}) copy-start(bf16[96,2240]{1,0:T(8,128)(2,1)} %copy-done.5) | copy-start | bytes 1290244
  102.7 11.4 %copy-start.8 = (bf16[96,2240]{1,0:T(8,128)(2,1)S(1)}, bf16[96,2240]{1,0:T(8,128)(2,1)}, u32[]{:S(2)}) copy-start(bf16[96,2240]{1,0:T(8,128)(2,1)} %copy-done.7) | copy-start | bytes 1290244
  102.7 11.4 %copy-start.10 = (bf16[96,2240]{1,0:T(8,128)(2,1)S(1)}, bf16[96,2240]{1,0:T(8,128)(2,1)}, u32[]{:S(2)}) copy-start(bf16[96,2240]{1,0:T(8,128)(2,1)} %copy-done.9) | copy-start | bytes 1290244
  102.7 11.4 %copy-start.12 = (bf16[96,2240]{1,0:T(8,128)(2,1)S(1)}, bf16[96,2240]{1,0:T(8,128)(2,1)}, u32[]{:S(2)}) copy-start(bf16[96,2240]{1,0:T(8,128)(2,1)} %copy-done.11) | copy-start | bytes 1290244

commit v3 on v2

--- a/solution.py
+++ b/solution.py
@@ -104,18 +104,21 @@
     )(*given)
 
 
-def query(normed, weights):
+def query(normed, weights, frames):
     features, total = normed.shape
     group = weights.shape[0] // 3
+    width = total // frames
 
     def kernel(x_ref, w_ref, q_ref):
-        q_ref[0] = jnp.maximum(dot(w_ref[:group, :], x_ref[...]), 0.0).astype(BF16)
+        q = jnp.maximum(dot(w_ref[:group, :], x_ref[...]), 0.0).astype(BF16)
+        for f in range(frames):
+            q_ref[f] = q[:, f * width : (f + 1) * width]
 
     return pl.pallas_call(
         kernel,
         in_specs=[VMEM] * 2,
         out_specs=VMEM,
-        out_shape=jax.ShapeDtypeStruct((1, group, total), BF16),
+        out_shape=jax.ShapeDtypeStruct((frames, group, width), BF16),
         compiler_params=params(),
         cost_estimate=cost(2 * group * features * total, 2 * features * total),
         name="query",
@@ -174,17 +177,13 @@
         outs, sem = rest[: len(sizes)], rest[-1]
         copies, at = [], 0
         for k, (out, n) in enumerate(zip(outs, sizes)):
-            if source.ndim == 3:
-                view = src.at[start]
-            else:
-                view = src.at[pl.ds(pl.multiple_of(start_ref[0] + at, aligned), n), :]
+            view = src.at[pl.ds(pl.multiple_of(start_ref[0] + at, aligned), n), :]
             copies.append(pltpu.make_async_copy(view, out, sem.at[k]))
             copies[-1].start()
             at += n
         for c in copies:
             c.wait()
 
-    where = jnp.zeros((1,), jnp.int32) if source.ndim == 3 else start.reshape(1)
     return pl.pallas_call(
         kernel,
         in_specs=[pl.BlockSpec(memory_space=pltpu.SMEM), pl.BlockSpec(memory_space=pl.ANY)],
@@ -194,12 +193,11 @@
         compiler_params=params(),
         cost_estimate=cost(0, 4 * sum(sizes) * width),
         name="cut",
-    )(where, source)
-
-
-def tokens_first(refs):
-    frames = refs[0].shape[0]
-    return [jnp.concatenate([r[f] for r in refs], axis=0).T for f in range(frames)]
+    )(start.reshape(1), source)
+
+
+def tokens_first(ref):
+    return jnp.concatenate([ref[f].T for f in range(ref.shape[0])], axis=0)
 
 
 def mix(rows, heads_out):
@@ -211,8 +209,7 @@
         out = refs[2 * n]
         total = None
         for w, x in zip(refs[:n], refs[n : 2 * n]):
-            left = jnp.concatenate(tokens_first([x]), axis=0)
-            term = dot(left, w[...])
+            term = dot(tokens_first(x), w[...])
             total = term if total is None else total + term
         out[...] = total
 
@@ -227,50 +224,46 @@
     )(*rows, *heads_out)
 
 
-def finish(starts, own, chips, shape):
-    frames, width, lanes = shape
-    group = chips[0][0][0].shape[1]
+def add_heads(starts, total, heads_out, lists, last):
+    frames, group, lanes = heads_out.shape
+    width = total.shape[1]
     given, plan = [], []
-    for heads_out, cores in chips:
-        plan.append((len(given), []))
-        given += heads_out
-        for core, lists in enumerate(cores):
-            for g, pieces in enumerate(lists):
-                at = 0
-                for p in pieces:
-                    plan[-1][1].append((len(given), core, g, at))
-                    given.append(p)
-                    at += p.shape[0]
+    for g, pieces in enumerate(lists):
+        at = 0
+        for p in pieces:
+            plan.append((g, at))
+            given.append(p)
+            at += p.shape[0]
     n = len(given)
     step = 640 if width > 640 else width
     spans = [(a, min(a + step, width)) for a in range(0, width, step)]
 
-    def kernel(start_ref, own_ref, *refs):
+    def kernel(start_ref, total_ref, heads_ref, *refs):
         out, w = refs[n], refs[n + 1]
-        lefts = []
-        for k, (first, pieces) in enumerate(plan):
-            for i, core, g, at in pieces:
-                row = pl.multiple_of(start_ref[g] + (core * group + at), 16)
-                w[k, pl.ds(row, refs[i].shape[0]), :] = refs[i][...]
-            lefts.append(jnp.concatenate(tokens_first(refs[first : first + 2]), axis=0))
+        for ref, (g, at) in zip(refs[:n], plan):
+            row = pl.multiple_of(start_ref[g] + at, 16)
+            w[pl.ds(row, ref.shape[0]), :] = ref[...]
+        left = tokens_first(heads_ref)
         for a, b in spans:
-            total = own_ref[:, a:b]
-            for k, left in enumerate(lefts):
-                total = total + dot(left, w[k, :, a:b])
-            total = total.astype(BF16)
+            now = total_ref[:, a:b] + dot(left, w[:, a:b])
+            if not last:
+                out[:, a:b] = now
+                continue
+            now = now.astype(BF16)
             for f in range(frames):
-                out[f, a:b, :] = total[f * lanes : (f + 1) * lanes].T
-
-    return pl.pallas_call(
-        kernel,
-        in_specs=[pl.BlockSpec(memory_space=pltpu.SMEM)] + [VMEM] * (1 + n),
+                out[f, a:b, :] = now[f * lanes : (f + 1) * lanes].T
+
+    shape = (frames, width, lanes) if last else total.shape
+    return pl.pallas_call(
+        kernel,
+        in_specs=[pl.BlockSpec(memory_space=pltpu.SMEM)] + [VMEM] * (2 + n),
         out_specs=VMEM,
-        out_shape=jax.ShapeDtypeStruct(shape, BF16),
-        scratch_shapes=[pltpu.VMEM((len(chips), 2 * group, width), BF16)],
-        compiler_params=params(),
-        cost_estimate=cost(4 * len(chips) * width * group * frames * lanes, 4 * len(chips) * width * group),
-        name="finish",
-    )(starts, own, *given)
+        out_shape=jax.ShapeDtypeStruct(shape, BF16 if last else F32),
+        scratch_shapes=[pltpu.VMEM((group, width), BF16)],
+        compiler_params=params(),
+        cost_estimate=cost(2 * width * group * frames * lanes, 2 * width * group),
+        name="add_heads",
+    )(starts, total, heads_out, *given)
 
 
 PIECES = 3
@@ -291,18 +284,14 @@
     out_gain = head_gain.reshape(-1, 1)
 
     pairs = n_row // 2
-    crossed = {}
-    for f in range(frames):
-        (frame,) = cut(tokens, f, [features], 1)
-        for k in range(1, pairs):
-            crossed[k, f] = swap(frame, 2 * k)
+    crossed = {k: swap(tokens, 2 * k) for k in range(1, pairs)}
     sibling = swap(tokens, 1)
-    passed = {key: swap(v, 1) for key, v in crossed.items()}
+    passed = {k: swap(v, 1) for k, v in crossed.items()}
 
     where = [[(0, f), (1, f)] for f in range(frames)]
     states, near_q = project([tokens, sibling], where, gain, weights, None, frames)
 
-    group, width = output_matrix.shape
+    group, _ = output_matrix.shape
     grp = lax.axis_index("grp")
     share = -(-group // (16 * n_grp)) * 16
     stride = (group - share) // max(n_grp - 1, 1)
@@ -320,17 +309,16 @@
             for g in range(n_grp):
                 held[1, g, j] = swap(held[0, g, j], 1)
         far_rows.append([[[held[c, g, j] for j in range(PIECES)] for g in range(n_grp)] for c in range(2)])
-    queries = []
-    for f in range(frames):
-        for k in range(1, pairs):
-            last = f == frames - 1 and k == pairs - 1
-            blocks = [crossed[k, f], passed[k, f]]
-            out = project(blocks, [[(0, None), (1, None)]], gain, weights, states, frames, f, last)
+    queries = [(near_q, {f: f for f in range(frames)}, 0)]
+    for k in range(1, pairs):
+        for c, block in enumerate((crossed[k], passed[k])):
+            last = c == 1 and k == pairs - 1
+            out = project([block], [[(0, f)] for f in range(frames)], gain, weights, states, frames, 0, last)
             states = out[0]
             if last:
                 own_sum, normed = out[1:]
             else:
-                queries.append((out[1], {f: 0}, 2 * k))
+                queries.append((out[1], {f: f for f in range(frames)}, 2 * k + c))
     if n_frm <= 4:
         priors = [shift(own_sum, s) for s in range(1, n_frm)]
     else:
@@ -338,16 +326,20 @@
         while s < n_frm:
             total, s = total + shift(total, s), 2 * s
         priors = [total]
-    queries.append((query(normed, weights), {frames - 1: 0}, n_row - 2))
-    queries.append((near_q, {f: f for f in range(frames)}, 0))
+    late = query(normed, weights, frames)
+    queries.append((late, {f: f for f in range(frames)}, n_row - 1))
     heads_out = attend(block_end, states, priors, out_gain, queries, lanes)
 
     across = []
     for k in range(1, pairs):
         across.append((swap(heads_out[2 * k], 2 * k), swap(heads_out[2 * k + 1], 2 * k + 1)))
     own = mix([output_matrix, near_rows], [heads_out[0], swap(heads_out[1], 1)])
-    out = finish(starts, own, list(zip(across, far_rows)), (frames, width, lanes))
-    return jnp.transpose(out, (2, 0, 1))
+    total, left = own, 2 * (pairs - 1)
+    for heads, rows in zip(across, far_rows):
+        for c in range(2):
+            left -= 1
+            total = add_heads(starts, total, heads[c], rows[c], left == 0)
+    return jnp.transpose(total, (2, 0, 1))
 
 
 def solution(mesh):

time: 121 us -> 115 us (0.950)
  waiting for transfers between devices: 56.5 us -> 51.7 us
  Pallas kernels: 23.3 us -> 25.5 us
  local copies, waits for them, and re-layouts: 11.2 us -> 9.53 us
    ppermute x21 -> x19, waiting for transfers between devices: 54.6 us -> 49.4 us  [swap(): return lax.ppermute(v, axis, [(i, i ^ k) for i in range(size)])]
    ppermute x21 -> x19, starting transfers between devices: 17 us -> 14.3 us  [swap(): return lax.ppermute(v, axis, [(i, i ^ k) for i in range(size)])]
    ppermute x3, starting transfers between devices: 11.1 us -> 12.8 us  [shift(): return lax.ppermute(v, 'frm', [(i, i + s) for i in range(n_frm - s)])]
    unnamed x40 -> x34, local copies, waits for them, and re-layouts: 10.7 us -> 9.06 us
    pallas_call x1 -> x2, Pallas kernels: 5.32 us -> 6.88 us  [add_heads(): pl.pallas_call(kernel, in_specs=[pl.BlockSpec(memory_space=pltpu.SMEM)] +...]
  transfers between devices with their start and end apart: 24 -> 22, of which waited for: 8 -> 6; matrix products, arithmetic and copies ran while one was open for 0% -> 0% of each run, Pallas kernels for 15% -> 19%
where the time goes in v3:
time: 115 us; the launch traced here: 114 us
  waiting for transfers between devices  51.7 us (45%)
  starting transfers between devices  27.2 us (24%)
  Pallas kernels  25.5 us (22%)
  local copies, waits for them, and re-layouts  9.53 us (8%)
    ppermute x19, waiting for transfers between devices, swap(): return lax.ppermute(v, axis, [(i, i ^ k) for i in range(size)])  49.4 us
    ppermute x19, starting transfers between devices, swap(): return lax.ppermute(v, axis, [(i, i ^ k) for i in range(size)])  14.3 us
    ppermute x3, starting transfers between devices, shift(): return lax.ppermute(v, 'frm', [(i, i + s) for i in range(n_frm - s)])  12.8 us
    pallas_call x3, Pallas kernels, project(): pl.pallas_call(kernel, in_specs=[VMEM] * len(given), out_specs=[VMEM] * l...  11.2 us
    unnamed x34, local copies, waits for them, and re-layouts  9.06 us
    pallas_call x2, Pallas kernels, add_heads(): pl.pallas_call(kernel, in_specs=[pl.BlockSpec(memory_space=pltpu.SMEM)] +...  6.88 us
    pallas_call x1, Pallas kernels, mix(): pl.pallas_call(kernel, in_specs=[VMEM] * (2 * n), out_specs=VMEM, out_sha...  3.84 us
    ppermute x3, waiting for transfers between devices, shift(): return lax.ppermute(v, 'frm', [(i, i + s) for i in range(n_frm - s)])  2.34 us
  transfers between devices with their start and end apart: 22, of which 6 were waited for; matrix products, arithmetic and copies ran while one was open for 0% of the time, Pallas kernels for 19%

profile of v3, /device:TPU:0, one launch (start us, length us, event | category | flops | bytes accessed | tf_op | source)
XLA Modules:
  0.0 114.3 jit_solution(11302829418779473640)
XLA Ops:
  0.0 3.0 %collective-permute-start.1 = (bf16[2,2240,128]{2,1,0:T(8,128)(2,1)}, bf16[2,2240,128]{2,1,0:T(8,128)(2,1)S(1)}, u32[]{:S(2)}, u32[]{:S(2)}) collective-permute-start(bf16[2,2240,128]{2,1,0:T(8,128)(2,1)} %bitcast.11), channel_id=1, source_target_pairs={{0,2},{1,3},{2,0},{3,1},{4,6},{5,7},{6,4},{7,5},{8,10},{9,11},{10,... | collective-permute-start | bytes 3440648 | tf_op jit(solution)/shard_map/ppermute | solution.py:275
  3.0 0.0 collective-permute-start
  3.0 0.5 collective-permute-start.3
  3.5 25.0 %collective-permute-done.1.refs_0_ = bf16[2,2240,128]{2,1,0:T(8,128)(2,1)S(1)} collective-permute-done((bf16[2,2240,128]{2,1,0:T(8,128)(2,1)}, bf16[2,2240,128]{2,1,0:T(8,128)(2,1)S(1)}, u32[]{:S(2)}, u32[]{:S(2)}) %collective-permute-start.1) | collective-permute-done | bytes 1146912 | tf_op jit(solution)/shard_map/ppermute | solution.py:275
  28.4 0.0 collective-permute-start.2
  28.4 1.7 %copy-done.2 = bf16[560,2240]{1,0:T(8,128)(2,1)S(1)} copy-done((bf16[560,2240]{1,0:T(8,128)(2,1)S(1)}, bf16[560,2240]{1,0:T(8,128)(2,1)}, u32[]{:S(2)}) %copy-start.2) | copy-done | bytes 2508824
  30.2 0.8 cut.1
  31.0 0.0 copy-start.13
  31.0 1.8 %collective-permute-start.9 = (bf16[96,2240]{1,0:T(8,128)(2,1)S(1)}, bf16[96,2240]{1,0:T(8,128)(2,1)S(1)}, u32[]{:S(2)}, u32[]{:S(2)}) collective-permute-start(bf16[96,2240]{1,0:T(8,128)(2,1)S(1)} %get-tuple-element.29), channel_id=1, source_target_pairs={{0,2},{1,3},{2,0},{3,1},{4,6},{5,7},{6,4},{7,5},{8,10},{9,11},{10,... | collective-permute-start | bytes 1290248 | tf_op jit(solution)/shard_map/ppermute | solution.py:275
  32.8 0.3 collective-permute-start.10
  33.1 0.3 reshape.13.refs_2_.refs_1_
  33.4 10.7 %collective-permute-done.9.refs_0_ = bf16[96,2240]{1,0:T(8,128)(2,1)S(1)} collective-permute-done((bf16[96,2240]{1,0:T(8,128)(2,1)S(1)}, bf16[96,2240]{1,0:T(8,128)(2,1)S(1)}, u32[]{:S(2)}, u32[]{:S(2)}) %collective-permute-start.9) | collective-permute-done | bytes 430112 | tf_op jit(solution)/shard_map/ppermute | solution.py:275
  44.1 1.7 %collective-permute-start.11 = (bf16[96,2240]{1,0:T(8,128)(2,1)S(1)}, bf16[96,2240]{1,0:T(8,128)(2,1)}, u32[]{:S(2)}, u32[]{:S(2)}) collective-permute-start(bf16[96,2240]{1,0:T(8,128)(2,1)S(1)} %get-tuple-element.31), channel_id=1, source_target_pairs={{0,2},{1,3},{2,0},{3,1},{4,6},{5,7},{6,4},{7,5},{8,10},{9,11},{10,... | collective-permute-start | bytes 1290248 | tf_op jit(solution)/shard_map/ppermute | solution.py:275
  45.8 7.7 %collective-permute-done.10.refs_1_ = bf16[96,2240]{1,0:T(8,128)(2,1)S(1)} collective-permute-done((bf16[96,2240]{1,0:T(8,128)(2,1)S(1)}, bf16[96,2240]{1,0:T(8,128)(2,1)S(1)}, u32[]{:S(2)}, u32[]{:S(2)}) %collective-permute-start.10) | collective-permute-done | bytes 430112 | tf_op jit(solution)/shard_map/ppermute | solution.py:275
  53.6 1.8 %collective-permute-start.12 = (bf16[96,2240]{1,0:T(8,128)(2,1)S(1)}, bf16[96,2240]{1,0:T(8,128)(2,1)}, u32[]{:S(2)}, u32[]{:S(2)}) collective-permute-start(bf16[96,2240]{1,0:T(8,128)(2,1)S(1)} %collective-permute-done.9.refs_0_), channel_id=1, source_target_pairs={{0,16},{16,0},{1,17},{17,1},{2,18},{18,2},{3,19},{19,3},{4,20},{20... | collective-permute-start | bytes 1290248 | tf_op jit(solution)/shard_map/ppermute | solution.py:275
  55.3 0.0 collective-permute-done.3.refs_1_
  55.3 0.3 collective-permute-start.13
  55.6 3.2 %copy-done = bf16[2240,3,560]{0,2,1:T(8,128)(2,1)S(1)} copy-done((bf16[2240,3,560]{0,2,1:T(8,128)(2,1)S(1)}, bf16[2240,3,560]{0,2,1:T(8,128)(2,1)}, u32[]{:S(2)}) %copy-start) | copy-done | bytes 7526424
  58.8 5.2 %project.3 = (f32[2,560,112]{2,1,0:T(8,128)S(1)}, bf16[2,560,256]{2,1,0:T(8,128)(2,1)S(1)}) custom-call(bf16[2,2240,128]{2,1,0:T(8,128)(2,1)S(1)} %bitcast.13, bf16[2,2240,128]{2,1,0:T(8,128)(2,1)S(1)} %collective-permute-done.3.refs_1_, f32[2240,1]{1,0:T(8,128)S(1)} %reshape.13.refs_2_.refs_1_, bf16[1680,2240]{1,0:T(8,128)(2,1)S(1)} %bitcast.7), custom_call_target="tpu_custom_call" | custom-call | flops 3853516800 | bytes 2293760 | tf_op jit(solution)/shard_map/project/pallas_call | solution.py:95
  64.0 3.4 %project.4 = (f32[2,560,112]{2,1,0:T(8,128)S(1)}, bf16[2,560,128]{2,1,0:T(8,128)(2,1)S(1)}) custom-call(bf16[2,2240,128]{2,1,0:T(8,128)(2,1)S(1)} %collective-permute-done.1.refs_0_, f32[2240,1]{1,0:T(8,128)S(1)} %reshape.13.refs_2_.refs_1_, bf16[1680,2240]{1,0:T(8,128)(2,1)S(1)} %bitcast.8, f32[2,560,112]{2,1,0:T(8,128)S(1)} %get-tuple-element.19.refs_3_), custom_call_target="tpu_custom_call" | custom-call | flops 1926758400 | bytes 1146880 | tf_op jit(solution)/shard_map/project/pallas_call | solution.py:95
  67.4 0.0 collective-permute-done.2.refs_0_
  67.4 0.0 copy-start.16
  67.4 2.6 %project.5 = (f32[2,560,112]{2,1,0:T(8,128)S(1)}, bf16[560,112]{1,0:T(8,128)(2,1)S(1)}, bf16[2240,256]{1,0:T(8,128)(2,1)S(1)}) custom-call(bf16[2,2240,128]{2,1,0:T(8,128)(2,1)S(1)} %collective-permute-done.2.refs_0_, f32[2240,1]{1,0:T(8,128)S(1)} %reshape.13.refs_2_.refs_1_, bf16[1680,2240]{1,0:T(8,128)(2,1)S(1)} %bitcast.9, ...), custom_call_target="tpu_custom_call" | custom-call | flops 1284505600 | bytes 1146880 | tf_op jit(solution)/shard_map/project/pallas_call | solution.py:95
  70.0 3.7 %collective-permute-start.4 = (bf16[560,112]{1,0:T(8,128)(2,1)S(1)}, bf16[560,112]{1,0:T(8,128)(2,1)S(1)}, u32[]{:S(2)}, u32[]{:S(2)}) collective-permute-start(bf16[560,112]{1,0:T(8,128)(2,1)S(1)} %get-tuple-element.22), channel_id=1, source_target_pairs={{0,4},{4,8},{8,12},{1,5},{5,9},{9,13},{2,6},{6,10},{10,14},{3,7},{... | collective-permute-start | bytes 376328 | tf_op jit(solution)/shard_map/ppermute | solution.py:278
  73.8 0.0 collective-permute-done.11.refs_2_
  73.8 1.6 %collective-permute-start.14 = (bf16[96,2240]{1,0:T(8,128)(2,1)}, bf16[96,2240]{1,0:T(8,128)(2,1)}, u32[]{:S(2)}, u32[]{:S(2)}) collective-permute-start(bf16[96,2240]{1,0:T(8,128)(2,1)} %collective-permute-done.11.refs_2_), channel_id=1, source_target_pairs={{0,16},{16,0},{1,17},{17,1},{2,18},{18,2},{3,19},{19,3},{4,20},{20... | collective-permute-start | bytes 1290248 | tf_op jit(solution)/shard_map/ppermute | solution.py:275
  75.4 0.0 collective-permute-done.12.refs_3_
  75.4 4.5 %collective-permute-start.5 = (bf16[560,112]{1,0:T(8,128)(2,1)S(1)}, bf16[560,112]{1,0:T(8,128)(2,1)S(1)}, u32[]{:S(2)}, u32[]{:S(2)}) collective-permute-start(bf16[560,112]{1,0:T(8,128)(2,1)S(1)} %get-tuple-element.22), channel_id=1, source_target_pairs={{0,8},{4,12},{1,9},{5,13},{2,10},{6,14},{3,11},{7,15},{16,24},{20,... | collective-permute-start | bytes 376328 | tf_op jit(solution)/shard_map/ppermute | solution.py:278
  79.9 0.0 collective-permute-done.4.rest_0_
  79.9 4.6 %collective-permute-start.6 = (bf16[560,112]{1,0:T(8,128)(2,1)S(1)}, bf16[560,112]{1,0:T(8,128)(2,1)S(1)}, u32[]{:S(2)}, u32[]{:S(2)}) collective-permute-start(bf16[560,112]{1,0:T(8,128)(2,1)S(1)} %get-tuple-element.22), channel_id=1, source_target_pairs={{0,12},{1,13},{2,14},{3,15},{16,28},{17,29},{18,30},{19,31}} | collective-permute-start | bytes 376328 | tf_op jit(solution)/shard_map/ppermute | solution.py:278
  84.5 0.0 collective-permute-done.5.rest_1_
  84.5 0.1 collective-permute-start.16
  84.6 2.3 %collective-permute-done.6.rest_2_ = bf16[560,112]{1,0:T(8,128)(2,1)S(1)} collective-permute-done((bf16[560,112]{1,0:T(8,128)(2,1)S(1)}, bf16[560,112]{1,0:T(8,128)(2,1)S(1)}, u32[]{:S(2)}, u32[]{:S(2)}) %collective-permute-start.6) | collective-permute-done | bytes 125472 | tf_op jit(solution)/shard_map/ppermute | solution.py:278
  86.9 0.0 collective-permute-start.17
  86.9 0.1 reshape.14.gain_ref
  87.1 0.0 copy-start.12
  87.1 0.0 copy-start.3
  87.1 0.8 query.1.rest_5_
  88.0 2.0 %attend.1 = (bf16[2,560,128]{2,1,0:T(8,128)(2,1)S(1)}, bf16[2,560,128]{2,1,0:T(8,128)(2,1)S(1)}, bf16[2,560,128]{2,1,0:T(8,128)(2,1)}, bf16[2,560,128]{2,1,0:T(8,128)(2,1)S(1)}) custom-call(s32[2]{0:T(128)S(1)} %copy-done.12, f32[2,560,112]{2,1,0:T(8,128)S(1)} %get-tuple-element.21.state_ref, f32[560,1]{1,0:T(8,128)S(1)} %reshape.14.gain_ref, ...), custom_call_target="tpu_custom_call" | custom-call | flops 128450560 | bytes 2293760 | tf_op jit(solution)/shard_map/attend/pallas_call | solution.py:161
  90.0 0.7 copy-done.8
  90.7 0.7 copy-done.14
  91.4 0.0 collective-permute-done.13.refs_4_
  91.4 0.5 collective-permute-start.7
  91.9 1.5 %collective-permute-start.8 = (bf16[2,560,128]{2,1,0:T(8,128)(2,1)}, bf16[2,560,128]{2,1,0:T(8,128)(2,1)}, u32[]{:S(2)}, u32[]{:S(2)}) collective-permute-start(bf16[2,560,128]{2,1,0:T(8,128)(2,1)} %get-tuple-element.28), channel_id=1, source_target_pairs={{0,2},{1,3},{2,0},{3,1},{4,6},{5,7},{6,4},{7,5},{8,10},{9,11},{10,... | collective-permute-start | bytes 860168 | tf_op jit(solution)/shard_map/ppermute | solution.py:275
  93.4 0.0 collective-permute-done.16.refs_0_
  93.4 0.0 collective-permute-start.18
  93.4 0.5 collective-permute-start.19
  93.9 0.0 collective-permute-done.refs_1_
  93.9 0.1 collective-permute-start.20
  94.0 0.0 collective-permute-done.7.refs_3_
  94.0 0.7 copy-done.10
  94.8 0.4 collective-permute-start.21
  95.2 5.9 %collective-permute-done.8.heads_ref = bf16[2,560,128]{2,1,0:T(8,128)(2,1)} collective-permute-done((bf16[2,560,128]{2,1,0:T(8,128)(2,1)}, bf16[2,560,128]{2,1,0:T(8,128)(2,1)}, u32[]{:S(2)}, u32[]{:S(2)}) %collective-permute-start.8) | collective-permute-done | bytes 286752 | tf_op jit(solution)/shard_map/ppermute | solution.py:275
  101.1 0.3 collective-permute-start.15
  101.4 0.1 pad_add_fusion.start_ref
  101.4 1.0 copy-done.9
  102.4 1.0 copy-done.11
  103.4 3.8 %mix.1.total_ref = f32[256,2240]{1,0:T(8,128)S(1)} custom-call(bf16[560,2240]{1,0:T(8,128)(2,1)S(1)} %copy-done.3, bf16[560,2240]{1,0:T(8,128)(2,1)} %collective-permute-done.refs_1_, bf16[2,560,128]{2,1,0:T(8,128)(2,1)S(1)} %copy-done.9, bf16[2,560,128]{2,1,0:T(8,128)(2,1)S(1)} %copy-done.11), custom_call_target="tpu_custom_call" | custom-call | flops 1284505600 | bytes 5017600 | tf_op jit(solution)/shard_map/mix/pallas_call | solution.py:216
  107.2 3.0 %add_heads.2.total_ref = f32[256,2240]{1,0:T(8,128)S(1)} custom-call(s32[2]{0:T(128)S(1)} %pad_add_fusion.start_ref, f32[256,2240]{1,0:T(8,128)S(1)} %mix.1.total_ref, bf16[2,560,128]{2,1,0:T(8,128)(2,1)} %collective-permute-done.8.heads_ref, bf16[96,2240]{1,0:T(8,128)(2,1)S(1)} %copy-done.5, bf16[96,2240]{1,0:T(8,128)(2,1)S(1)} %copy-done.7, ...), custom_call_target="tpu_custom_call" | custom-call | flops 642252800 | bytes 2508800 | tf_op jit(solution)/shard_map/add_heads/pallas_call | solution.py:257
  110.2 0.0 collective-permute-done.18.refs_2_
  110.2 0.0 collective-permute-done.20.refs_4_
  110.2 0.0 collective-permute-done.21.refs_5_
  110.2 0.1 collective-permute-done.15.heads_ref
  110.4 3.9 %add_heads.3 = bf16[2,2240,128]{2,1,0:T(8,128)(2,1)} custom-call(s32[2]{0:T(128)S(1)} %pad_add_fusion.start_ref, f32[256,2240]{1,0:T(8,128)S(1)} %add_heads.2.total_ref, bf16[2,560,128]{2,1,0:T(8,128)(2,1)S(1)} %collective-permute-done.15.heads_ref, bf16[96,2240]{1,0:T(8,128)(2,1)S(1)} %collective-permute-done.16.refs_0_, ...), custom_call_target="tpu_custom_call" | custom-call | flops 642252800 | bytes 2508800 | tf_op jit(solution)/shard_map/add_heads/pallas_call | solution.py:257
  (26 shorter events, 0.0 us)
Async XLA Ops:
  0.0 28.4 %collective-permute-start.1 = (bf16[2,2240,128]{2,1,0:T(8,128)(2,1)}, bf16[2,2240,128]{2,1,0:T(8,128)(2,1)S(1)}, u32[]{:S(2)}, u32[]{:S(2)}) collective-permute-start(bf16[2,2240,128]{2,1,0:T(8,128)(2,1)} %bitcast.11), channel_id=1, source_target_pairs={{0,2},{1,3},{2,0},{3,1},{4,6},{5,7},{6,4},{7,5},{8,10},{9,11},{10,... | collective-permute-start | bytes 3440648 | tf_op jit(solution)/shard_map/ppermute | solution.py:275
  3.0 91.0 %collective-permute-start = (bf16[560,2240]{1,0:T(8,128)(2,1)}, bf16[560,2240]{1,0:T(8,128)(2,1)}, u32[]{:S(2)}, u32[]{:S(2)}) collective-permute-start(bf16[560,2240]{1,0:T(8,128)(2,1)} %src.1), channel_id=1, source_target_pairs={{0,1},{1,0},{2,3},{3,2},{4,5},{5,4},{6,7},{7,6},{8,9},{9,8},{10,11... | collective-permute-start | bytes 7526408 | tf_op jit(solution)/shard_map/ppermute | solution.py:275
  3.0 52.4 %collective-permute-start.3 = (bf16[2,2240,128]{2,1,0:T(8,128)(2,1)}, bf16[2,2240,128]{2,1,0:T(8,128)(2,1)S(1)}, u32[]{:S(2)}, u32[]{:S(2)}) collective-permute-start(bf16[2,2240,128]{2,1,0:T(8,128)(2,1)} %bitcast.12), channel_id=1, source_target_pairs={{0,1},{1,0},{2,3},{3,2},{4,5},{5,4},{6,7},{7,6},{8,9},{9,8},{10,11... | collective-permute-start | bytes 3440648 | tf_op jit(solution)/shard_map/ppermute | solution.py:275
  28.4 39.0 %collective-permute-start.2 = (bf16[2,2240,128]{2,1,0:T(8,128)(2,1)S(1)}, bf16[2,2240,128]{2,1,0:T(8,128)(2,1)S(1)}, u32[]{:S(2)}, u32[]{:S(2)}) collective-permute-start(bf16[2,2240,128]{2,1,0:T(8,128)(2,1)S(1)} %collective-permute-done.1.refs_0_), channel_id=1, source_target_pairs={{0,1},{1,0},{2,3},{3,2},{4,5},{5,4},{6,7},{7,6},{8,9},{9,8},{10,11... | collective-permute-start | bytes 3440648 | tf_op jit(solution)/shard_map/ppermute | solution.py:275
  28.4 1.7 %copy-start.2 = (bf16[560,2240]{1,0:T(8,128)(2,1)S(1)}, bf16[560,2240]{1,0:T(8,128)(2,1)}, u32[]{:S(2)}) copy-start(bf16[560,2240]{1,0:T(8,128)(2,1)} %src.1) | copy-start | bytes 7526404
  30.2 2.9 %copy-start.15 = (f32[2240]{0:T(1024)S(1)}, f32[2240]{0:T(1024)}, u32[]{:S(2)}) copy-start(f32[2240]{0:T(1024)} %param.7) | copy-start | bytes 26884
  31.0 24.6 %copy-start.13 = (bf16[128,2,2240]{0,2,1:T(8,128)(2,1)S(1)}, bf16[128,2,2240]{0,2,1:T(8,128)(2,1)}, u32[]{:S(2)}) copy-start(bf16[128,2,2240]{0,2,1:T(8,128)(2,1)} %param.6) | copy-start | bytes 3440644
  31.0 13.1 %collective-permute-start.9 = (bf16[96,2240]{1,0:T(8,128)(2,1)S(1)}, bf16[96,2240]{1,0:T(8,128)(2,1)S(1)}, u32[]{:S(2)}, u32[]{:S(2)}) collective-permute-start(bf16[96,2240]{1,0:T(8,128)(2,1)S(1)} %get-tuple-element.29), channel_id=1, source_target_pairs={{0,2},{1,3},{2,0},{3,1},{4,6},{5,7},{6,4},{7,5},{8,10},{9,11},{10,... | collective-permute-start | bytes 1290248 | tf_op jit(solution)/shard_map/ppermute | solution.py:275
  32.8 20.8 %collective-permute-start.10 = (bf16[96,2240]{1,0:T(8,128)(2,1)S(1)}, bf16[96,2240]{1,0:T(8,128)(2,1)S(1)}, u32[]{:S(2)}, u32[]{:S(2)}) collective-permute-start(bf16[96,2240]{1,0:T(8,128)(2,1)S(1)} %get-tuple-element.30), channel_id=1, source_target_pairs={{0,2},{1,3},{2,0},{3,1},{4,6},{5,7},{6,4},{7,5},{8,10},{9,11},{10,... | collective-permute-start | bytes 1290248 | tf_op jit(solution)/shard_map/ppermute | solution.py:275
  44.1 40.4 %copy-start.4 = (bf16[96,2240]{1,0:T(8,128)(2,1)}, bf16[96,2240]{1,0:T(8,128)(2,1)S(1)}, u32[]{:S(2)}) copy-start(bf16[96,2240]{1,0:T(8,128)(2,1)S(1)} %collective-permute-done.9.refs_0_) | copy-start | bytes 1290244
  44.1 29.7 %collective-permute-start.11 = (bf16[96,2240]{1,0:T(8,128)(2,1)S(1)}, bf16[96,2240]{1,0:T(8,128)(2,1)}, u32[]{:S(2)}, u32[]{:S(2)}) collective-permute-start(bf16[96,2240]{1,0:T(8,128)(2,1)S(1)} %get-tuple-element.31), channel_id=1, source_target_pairs={{0,2},{1,3},{2,0},{3,1},{4,6},{5,7},{6,4},{7,5},{8,10},{9,11},{10,... | collective-permute-start | bytes 1290248 | tf_op jit(solution)/shard_map/ppermute | solution.py:275
  53.6 33.4 %copy-start.6 = (bf16[96,2240]{1,0:T(8,128)(2,1)}, bf16[96,2240]{1,0:T(8,128)(2,1)S(1)}, u32[]{:S(2)}) copy-start(bf16[96,2240]{1,0:T(8,128)(2,1)S(1)} %collective-permute-done.10.refs_1_) | copy-start | bytes 1290244
  53.6 21.8 %collective-permute-start.12 = (bf16[96,2240]{1,0:T(8,128)(2,1)S(1)}, bf16[96,2240]{1,0:T(8,128)(2,1)}, u32[]{:S(2)}, u32[]{:S(2)}) collective-permute-start(bf16[96,2240]{1,0:T(8,128)(2,1)S(1)} %collective-permute-done.9.refs_0_), channel_id=1, source_target_pairs={{0,16},{16,0},{1,17},{17,1},{2,18},{18,2},{3,19},{19,3},{4,20},{20... | collective-permute-start | bytes 1290248 | tf_op jit(solution)/shard_map/ppermute | solution.py:275
  55.3 36.1 %collective-permute-start.13 = (bf16[96,2240]{1,0:T(8,128)(2,1)S(1)}, bf16[96,2240]{1,0:T(8,128)(2,1)}, u32[]{:S(2)}, u32[]{:S(2)}) collective-permute-start(bf16[96,2240]{1,0:T(8,128)(2,1)S(1)} %collective-permute-done.10.refs_1_), channel_id=1, source_target_pairs={{0,16},{16,0},{1,17},{17,1},{2,18},{18,2},{3,19},{19,3},{4,20},{20... | collective-permute-start | bytes 1290248 | tf_op jit(solution)/shard_map/ppermute | solution.py:275
  55.6 3.2 %copy-start = (bf16[2240,3,560]{0,2,1:T(8,128)(2,1)S(1)}, bf16[2240,3,560]{0,2,1:T(8,128)(2,1)}, u32[]{:S(2)}) copy-start(bf16[2240,3,560]{0,2,1:T(8,128)(2,1)} %param.8) | copy-start | bytes 22579204
  58.8 5.2 %copy-start.1 = (bf16[2240,3,560]{0,2,1:T(8,128)(2,1)S(1)}, bf16[2240,3,560]{0,2,1:T(8,128)(2,1)}, u32[]{:S(2)}) copy-start(bf16[2240,3,560]{0,2,1:T(8,128)(2,1)} %param.8) | copy-start | bytes 22579204
  67.4 19.5 %copy-start.16 = (f32[560]{0:T(1024)S(1)}, f32[560]{0:T(1024)}, u32[]{:S(2)}) copy-start(f32[560]{0:T(1024)} %param.9) | copy-start | bytes 6724
  70.0 9.8 %collective-permute-start.4 = (bf16[560,112]{1,0:T(8,128)(2,1)S(1)}, bf16[560,112]{1,0:T(8,128)(2,1)S(1)}, u32[]{:S(2)}, u32[]{:S(2)}) collective-permute-start(bf16[560,112]{1,0:T(8,128)(2,1)S(1)} %get-tuple-element.22), channel_id=1, source_target_pairs={{0,4},{4,8},{8,12},{1,5},{5,9},{9,13},{2,6},{6,10},{10,14},{3,7},{... | collective-permute-start | bytes 376328 | tf_op jit(solution)/shard_map/ppermute | solution.py:278
  73.8 18.1 %collective-permute-start.14 = (bf16[96,2240]{1,0:T(8,128)(2,1)}, bf16[96,2240]{1,0:T(8,128)(2,1)}, u32[]{:S(2)}, u32[]{:S(2)}) collective-permute-start(bf16[96,2240]{1,0:T(8,128)(2,1)} %collective-permute-done.11.refs_2_), channel_id=1, source_target_pairs={{0,16},{16,0},{1,17},{17,1},{2,18},{18,2},{3,19},{19,3},{4,20},{20... | collective-permute-start | bytes 1290248 | tf_op jit(solution)/shard_map/ppermute | solution.py:275
  75.4 9.1 %collective-permute-start.5 = (bf16[560,112]{1,0:T(8,128)(2,1)S(1)}, bf16[560,112]{1,0:T(8,128)(2,1)S(1)}, u32[]{:S(2)}, u32[]{:S(2)}) collective-permute-start(bf16[560,112]{1,0:T(8,128)(2,1)S(1)} %get-tuple-element.22), channel_id=1, source_target_pairs={{0,8},{4,12},{1,9},{5,13},{2,10},{6,14},{3,11},{7,15},{16,24},{20,... | collective-permute-start | bytes 376328 | tf_op jit(solution)/shard_map/ppermute | solution.py:278
  79.9 7.0 %collective-permute-start.6 = (bf16[560,112]{1,0:T(8,128)(2,1)S(1)}, bf16[560,112]{1,0:T(8,128)(2,1)S(1)}, u32[]{:S(2)}, u32[]{:S(2)}) collective-permute-start(bf16[560,112]{1,0:T(8,128)(2,1)S(1)} %get-tuple-element.22), channel_id=1, source_target_pairs={{0,12},{1,13},{2,14},{3,15},{16,28},{17,29},{18,30},{19,31}} | collective-permute-start | bytes 376328 | tf_op jit(solution)/shard_map/ppermute | solution.py:278
  84.5 8.9 %collective-permute-start.16 = (bf16[96,2240]{1,0:T(8,128)(2,1)S(1)}, bf16[96,2240]{1,0:T(8,128)(2,1)S(1)}, u32[]{:S(2)}, u32[]{:S(2)}) collective-permute-start(bf16[96,2240]{1,0:T(8,128)(2,1)S(1)} %collective-permute-done.9.refs_0_), channel_id=1, source_target_pairs={{0,1},{1,0},{2,3},{3,2},{4,5},{5,4},{6,7},{7,6},{8,9},{9,8},{10,11... | collective-permute-start | bytes 1290248 | tf_op jit(solution)/shard_map/ppermute | solution.py:275
  86.9 6.5 %collective-permute-start.17 = (bf16[96,2240]{1,0:T(8,128)(2,1)S(1)}, bf16[96,2240]{1,0:T(8,128)(2,1)S(1)}, u32[]{:S(2)}, u32[]{:S(2)}) collective-permute-start(bf16[96,2240]{1,0:T(8,128)(2,1)S(1)} %collective-permute-done.10.refs_1_), channel_id=1, source_target_pairs={{0,1},{1,0},{2,3},{3,2},{4,5},{5,4},{6,7},{7,6},{8,9},{9,8},{10,11... | collective-permute-start | bytes 1290248 | tf_op jit(solution)/shard_map/ppermute | solution.py:275
  87.1 0.9 copy-start.12
  87.1 14.3 %copy-start.3 = (bf16[560,2240]{1,0:T(8,128)(2,1)S(1)}, bf16[560,2240]{1,0:T(8,128)(2,1)}, u32[]{:S(2)}) copy-start(bf16[560,2240]{1,0:T(8,128)(2,1)} %src.1) | copy-start | bytes 7526404
  90.0 0.7 copy-start.8
  90.7 0.7 copy-start.14
  91.4 2.6 %collective-permute-start.7 = (bf16[2,560,128]{2,1,0:T(8,128)(2,1)S(1)}, bf16[2,560,128]{2,1,0:T(8,128)(2,1)S(1)}, u32[]{:S(2)}, u32[]{:S(2)}) collective-permute-start(bf16[2,560,128]{2,1,0:T(8,128)(2,1)S(1)} %get-tuple-element.27), channel_id=1, source_target_pairs={{0,1},{1,0},{2,3},{3,2},{4,5},{5,4},{6,7},{7,6},{8,9},{9,8},{10,11... | collective-permute-start | bytes 860168 | tf_op jit(solution)/shard_map/ppermute | solution.py:275
  91.9 9.1 %collective-permute-start.8 = (bf16[2,560,128]{2,1,0:T(8,128)(2,1)}, bf16[2,560,128]{2,1,0:T(8,128)(2,1)}, u32[]{:S(2)}, u32[]{:S(2)}) collective-permute-start(bf16[2,560,128]{2,1,0:T(8,128)(2,1)} %get-tuple-element.28), channel_id=1, source_target_pairs={{0,2},{1,3},{2,0},{3,1},{4,6},{5,7},{6,4},{7,5},{8,10},{9,11},{10,... | collective-permute-start | bytes 860168 | tf_op jit(solution)/shard_map/ppermute | solution.py:275
  93.4 16.8 %collective-permute-start.18 = (bf16[96,2240]{1,0:T(8,128)(2,1)}, bf16[96,2240]{1,0:T(8,128)(2,1)}, u32[]{:S(2)}, u32[]{:S(2)}) collective-permute-start(bf16[96,2240]{1,0:T(8,128)(2,1)} %collective-permute-done.11.refs_2_), channel_id=1, source_target_pairs={{0,1},{1,0},{2,3},{3,2},{4,5},{5,4},{6,7},{7,6},{8,9},{9,8},{10,11... | collective-permute-start | bytes 1290248 | tf_op jit(solution)/shard_map/ppermute | solution.py:275
  93.4 16.8 %collective-permute-start.19 = (bf16[96,2240]{1,0:T(8,128)(2,1)}, bf16[96,2240]{1,0:T(8,128)(2,1)}, u32[]{:S(2)}, u32[]{:S(2)}) collective-permute-start(bf16[96,2240]{1,0:T(8,128)(2,1)} %collective-permute-done.12.refs_3_), channel_id=1, source_target_pairs={{0,1},{1,0},{2,3},{3,2},{4,5},{5,4},{6,7},{7,6},{8,9},{9,8},{10,11... | collective-permute-start | bytes 1290248 | tf_op jit(solution)/shard_map/ppermute | solution.py:275
  93.9 16.3 %collective-permute-start.20 = (bf16[96,2240]{1,0:T(8,128)(2,1)}, bf16[96,2240]{1,0:T(8,128)(2,1)}, u32[]{:S(2)}, u32[]{:S(2)}) collective-permute-start(bf16[96,2240]{1,0:T(8,128)(2,1)} %collective-permute-done.13.refs_4_), channel_id=1, source_target_pairs={{0,1},{1,0},{2,3},{3,2},{4,5},{5,4},{6,7},{7,6},{8,9},{9,8},{10,11... | collective-permute-start | bytes 1290248 | tf_op jit(solution)/shard_map/ppermute | solution.py:275
  94.0 0.7 copy-start.10
  94.8 15.5 %collective-permute-start.21 = (bf16[96,2240]{1,0:T(8,128)(2,1)}, bf16[96,2240]{1,0:T(8,128)(2,1)}, u32[]{:S(2)}, u32[]{:S(2)}) collective-permute-start(bf16[96,2240]{1,0:T(8,128)(2,1)} %collective-permute-done.14.refs_5_), channel_id=1, source_target_pairs={{0,1},{1,0},{2,3},{3,2},{4,5},{5,4},{6,7},{7,6},{8,9},{9,8},{10,11... | collective-permute-start | bytes 1290248 | tf_op jit(solution)/shard_map/ppermute | solution.py:275
  101.1 9.3 %collective-permute-start.15 = (bf16[2,560,128]{2,1,0:T(8,128)(2,1)}, bf16[2,560,128]{2,1,0:T(8,128)(2,1)S(1)}, u32[]{:S(2)}, u32[]{:S(2)}) collective-permute-start(bf16[2,560,128]{2,1,0:T(8,128)(2,1)} %copy-done.14), channel_id=1, source_target_pairs={{0,3},{1,2},{2,1},{3,0},{4,7},{5,6},{6,5},{7,4},{8,11},{9,10},{10,... | collective-permute-start | bytes 860168 | tf_op jit(solution)/shard_map/ppermute | solution.py:275
  101.4 1.0 copy-start.9
  102.4 1.0 copy-start.11
  103.4 3.9 %copy-start.5 = (bf16[96,2240]{1,0:T(8,128)(2,1)S(1)}, bf16[96,2240]{1,0:T(8,128)(2,1)}, u32[]{:S(2)}) copy-start(bf16[96,2240]{1,0:T(8,128)(2,1)} %copy-done.4) | copy-start | bytes 1290244
  103.4 3.9 %copy-start.7 = (bf16[96,2240]{1,0:T(8,128)(2,1)S(1)}, bf16[96,2240]{1,0:T(8,128)(2,1)}, u32[]{:S(2)}) copy-start(bf16[96,2240]{1,0:T(8,128)(2,1)} %copy-done.6) | copy-start | bytes 1290244

commit v4 on v3

--- a/solution.py
+++ b/solution.py
@@ -170,17 +170,16 @@
     )(end, states, head_gain, *priors, *[a for a, _, _ in queries])
 
 
-def cut(source, start, sizes, aligned):
+def cut(source, starts, sizes):
     width = source.shape[-1]
 
     def kernel(start_ref, src, *rest):
         outs, sem = rest[: len(sizes)], rest[-1]
-        copies, at = [], 0
+        copies = []
         for k, (out, n) in enumerate(zip(outs, sizes)):
-            view = src.at[pl.ds(pl.multiple_of(start_ref[0] + at, aligned), n), :]
+            view = src.at[pl.ds(pl.multiple_of(start_ref[k], 16), n), :]
             copies.append(pltpu.make_async_copy(view, out, sem.at[k]))
             copies[-1].start()
-            at += n
         for c in copies:
             c.wait()
 
@@ -190,10 +189,43 @@
         out_specs=[VMEM] * len(sizes),
         out_shape=[jax.ShapeDtypeStruct((n, width), source.dtype) for n in sizes],
         scratch_shapes=[pltpu.SemaphoreType.DMA((len(sizes),))],
-        compiler_params=params(),
+        compiler_params=params(8),
         cost_estimate=cost(0, 4 * sum(sizes) * width),
         name="cut",
-    )(start.reshape(1), source)
+    )(starts, source)
+
+
+def copy_pieces(start_ref, refs, plan, matrix, sem):
+    copies = []
+    for i, (ref, (k, at)) in enumerate(zip(refs, plan)):
+        row = pl.multiple_of(start_ref[k] + at, 16)
+        copies.append(pltpu.make_async_copy(ref, matrix.at[pl.ds(row, ref.shape[0]), :], sem.at[i]))
+        copies[-1].start()
+    return copies
+
+
+def place(starts, matrix, pieces, shape):
+    n = len(pieces)
+    plan = [(k, at) for _, k, at in pieces]
+
+    def kernel(start_ref, *refs):
+        for c in copy_pieces(start_ref, refs[:n], plan, refs[-2], refs[-1]):
+            c.wait()
+
+    given = [p for p, _, _ in pieces] + ([] if matrix is None else [matrix])
+    return pl.pallas_call(
+        kernel,
+        in_specs=[pl.BlockSpec(memory_space=pltpu.SMEM)]
+        + [pl.BlockSpec(memory_space=pl.ANY)] * n
+        + ([] if matrix is None else [VMEM]),
+        out_specs=VMEM,
+        out_shape=pltpu.VMEM(shape, BF16),
+        scratch_shapes=[pltpu.SemaphoreType.DMA((n,))],
+        input_output_aliases={} if matrix is None else {1 + n: 0},
+        compiler_params=params(8),
+        cost_estimate=cost(0, sum(4 * p.size for p, _, _ in pieces)),
+        name="place",
+    )(starts, *given)
 
 
 def tokens_first(ref):
@@ -224,26 +256,22 @@
     )(*rows, *heads_out)
 
 
-def add_heads(starts, total, heads_out, lists, last):
-    frames, group, lanes = heads_out.shape
+def add_heads(starts, total, heads_out, matrix, pieces, last):
+    frames, group, lanes = heads_out[0].shape
     width = total.shape[1]
-    given, plan = [], []
-    for g, pieces in enumerate(lists):
-        at = 0
-        for p in pieces:
-            plan.append((g, at))
-            given.append(p)
-            at += p.shape[0]
-    n = len(given)
+    n = len(pieces)
+    plan = [(k, at) for _, k, at in pieces]
     step = 640 if width > 640 else width
     spans = [(a, min(a + step, width)) for a in range(0, width, step)]
 
-    def kernel(start_ref, total_ref, heads_ref, *refs):
-        out, w = refs[n], refs[n + 1]
-        for ref, (g, at) in zip(refs[:n], plan):
-            row = pl.multiple_of(start_ref[g] + at, 16)
-            w[pl.ds(row, ref.shape[0]), :] = ref[...]
-        left = tokens_first(heads_ref)
+    def kernel(start_ref, total_ref, x_ref, y_ref, *refs):
+        out, w, sem = refs[n + 1], refs[n + 2], refs[n + 3]
+        copies = copy_pieces(start_ref, refs[:n], plan, w, sem)
+        left = jnp.concatenate(
+            [jnp.concatenate([x_ref[f], y_ref[f]], axis=0).T for f in range(frames)], axis=0
+        )
+        for c in copies:
+            c.wait()
         for a, b in spans:
             now = total_ref[:, a:b] + dot(left, w[:, a:b])
             if not last:
@@ -256,22 +284,23 @@
     shape = (frames, width, lanes) if last else total.shape
     return pl.pallas_call(
         kernel,
-        in_specs=[pl.BlockSpec(memory_space=pltpu.SMEM)] + [VMEM] * (2 + n),
-        out_specs=VMEM,
-        out_shape=jax.ShapeDtypeStruct(shape, BF16 if last else F32),
-        scratch_shapes=[pltpu.VMEM((group, width), BF16)],
+        in_specs=[pl.BlockSpec(memory_space=pltpu.SMEM)]
+        + [VMEM] * 3
+        + [pl.BlockSpec(memory_space=pl.ANY)] * n
+        + [VMEM],
+        out_specs=[VMEM] * 2,
+        out_shape=[jax.ShapeDtypeStruct(shape, BF16 if last else F32), pltpu.VMEM(matrix.shape, BF16)],
+        scratch_shapes=[pltpu.SemaphoreType.DMA((n,))],
+        input_output_aliases={4 + n: 1},
         compiler_params=params(),
-        cost_estimate=cost(2 * width * group * frames * lanes, 2 * width * group),
+        cost_estimate=cost(4 * width * group * frames * lanes, 4 * width * group),
         name="add_heads",
-    )(starts, total, heads_out, *given)
-
-
-PIECES = 3
+    )(starts, total, *heads_out, *[p for p, _, _ in pieces], matrix)[0]
 
 
 def per_device(n_grp, n_row, n_frm, hidden_in, norm_gain, qkv_weight, head_gain, output_matrix, block_end):
     def swap(v, k, axis="row"):
-        size = {"row": n_row, "grp": n_grp}[axis]
+        size = {"row": n_row, "grp": n_grp, "frm": n_frm}[axis]
         return lax.ppermute(v, axis, [(i, i ^ k) for i in range(size)])
 
     def shift(v, s):
@@ -291,24 +320,44 @@
     where = [[(0, f), (1, f)] for f in range(frames)]
     states, near_q = project([tokens, sibling], where, gain, weights, None, frames)
 
-    group, _ = output_matrix.shape
+
+    group, width = output_matrix.shape
     grp = lax.axis_index("grp")
+    side = lax.axis_index("frm") % 2
     share = -(-group // (16 * n_grp)) * 16
     stride = (group - share) // max(n_grp - 1, 1)
-    sizes = [share // 16 * (j + 1) // PIECES * 16 - share // 16 * j // PIECES * 16 for j in range(PIECES)]
-    pieces = cut(output_matrix, grp * stride, sizes, 16)
+    half = share // 96 * 16
+    outer = (share - 2 * half) // 32 * 16
+    rest = share - 2 * half - outer
+    base = grp * stride
+    pieces = cut(
+        output_matrix, jnp.stack([base, base + outer + side * half, base + outer + 2 * half]), [outer, half, rest]
+    )
     near_rows = swap(output_matrix, 1)
-    starts = jnp.stack([(grp ^ g) * stride for g in range(n_grp)])
+    starts, index = [], {}
+    for c in range(2):
+        for g in range(n_grp):
+            first = c * group + (grp ^ g) * stride
+            for z, offset in enumerate((0, side * half, (1 - side) * half)):
+                index[c, g, z] = len(starts)
+                starts.append(first + offset)
+    starts = jnp.stack(starts)
     far_rows = []
     for k in range(1, pairs):
-        held = {}
+        early, middle, late = [], [], []
         for j, piece in enumerate(pieces):
-            held[0, 0, j] = swap(piece, 2 * k)
+            held = [(0, 0, swap(piece, 2 * k))]
             for g in range(1, n_grp):
-                held[0, g, j] = swap(held[0, 0, j], g, "grp")
-            for g in range(n_grp):
-                held[1, g, j] = swap(held[0, g, j], 1)
-        far_rows.append([[[held[c, g, j] for j in range(PIECES)] for g in range(n_grp)] for c in range(2)])
+                held.append((g, 0, swap(held[0][2], g, "grp")))
+            if j == 1:
+                held += [(g, 1, swap(v, 1, "frm")) for g, _, v in held]
+            for g, z, v in held:
+                at = (0, outer, outer + 2 * half)[j]
+                zone = 0 if j != 1 else 1 + z
+                where_to = early if j == 0 else late if g and (j == 2 or z) else middle
+                where_to.append((v, index[0, g, zone], at))
+                where_to.append((swap(v, 1), index[1, g, zone], at))
+        far_rows.append((early, middle, late))
     queries = [(near_q, {f: f for f in range(frames)}, 0)]
     for k in range(1, pairs):
         for c, block in enumerate((crossed[k], passed[k])):
@@ -334,11 +383,12 @@
     for k in range(1, pairs):
         across.append((swap(heads_out[2 * k], 2 * k), swap(heads_out[2 * k + 1], 2 * k + 1)))
     own = mix([output_matrix, near_rows], [heads_out[0], swap(heads_out[1], 1)])
-    total, left = own, 2 * (pairs - 1)
-    for heads, rows in zip(across, far_rows):
-        for c in range(2):
-            left -= 1
-            total = add_heads(starts, total, heads[c], rows[c], left == 0)
+    total = own
+    for k, (heads, (early, middle, late)) in enumerate(zip(across, far_rows)):
+        shape = (2 * group, width)
+        matrix = place(starts, None, early, shape)
+        matrix = place(starts, matrix, middle, shape)
+        total = add_heads(starts, total, heads, matrix, late, k == pairs - 2)
     return jnp.transpose(total, (2, 0, 1))
 
 

time: 115 us -> 129 us (1.12)
  starting transfers between devices: 27.2 us -> 34.3 us
  Pallas kernels: 25.5 us -> 31 us
  local copies, waits for them, and re-layouts: 9.53 us -> 12.4 us
  waiting for transfers between devices: 51.7 us -> 49.4 us
    ppermute x19 -> x23, waiting for transfers between devices: 49.4 us -> 44.1 us  [swap(): return lax.ppermute(v, axis, [(i, i ^ k) for i in range(size)])]
    pallas_call x0 -> x2, Pallas kernels: none -> 4.47 us  [place(): pl.pallas_call(kernel, in_specs=[pl.BlockSpec(memory_space=pltpu.SMEM)] +...]
    ppermute x19 -> x23, starting transfers between devices: 14.3 us -> 18.3 us  [swap(): return lax.ppermute(v, axis, [(i, i ^ k) for i in range(size)])]
    ppermute x3, starting transfers between devices: 12.8 us -> 16 us  [shift(): return lax.ppermute(v, 'frm', [(i, i + s) for i in range(n_frm - s)])]
    ppermute x3, waiting for transfers between devices: 2.34 us -> 5.37 us  [shift(): return lax.ppermute(v, 'frm', [(i, i + s) for i in range(n_frm - s)])]
    unnamed x34 -> x64, local copies, waits for them, and re-layouts: 9.06 us -> 11.8 us
    pallas_call x3, Pallas kernels: 11.2 us -> 13.6 us  [project(): pl.pallas_call(kernel, in_specs=[VMEM] * len(given), out_specs=[VMEM] * l...]
    pallas_call x2 -> x1, Pallas kernels: 6.88 us -> 5.56 us  [add_heads(): pl.pallas_call(kernel, in_specs=[pl.BlockSpec(memory_space=pltpu.SMEM)] +...]
  transfers between devices with their start and end apart: 22 -> 26, of which waited for: 6 -> 8; matrix products, arithmetic and copies ran while one was open for 0% -> 0% of each run, Pallas kernels for 19% -> 20%
where the time goes in v4:
time: 129 us; the launch traced here: 128 us
  waiting for transfers between devices  49.4 us (38%)
  starting transfers between devices  34.3 us (27%)
  Pallas kernels  31 us (24%)
  local copies, waits for them, and re-layouts  12.4 us (10%)
    ppermute x23, waiting for transfers between devices, swap(): return lax.ppermute(v, axis, [(i, i ^ k) for i in range(size)])  44.1 us
    ppermute x23, starting transfers between devices, swap(): return lax.ppermute(v, axis, [(i, i ^ k) for i in range(size)])  18.3 us
    ppermute x3, starting transfers between devices, shift(): return lax.ppermute(v, 'frm', [(i, i + s) for i in range(n_frm - s)])  16 us
    pallas_call x3, Pallas kernels, project(): pl.pallas_call(kernel, in_specs=[VMEM] * len(given), out_specs=[VMEM] * l...  13.6 us
    unnamed x64, local copies, waits for them, and re-layouts  11.8 us
    pallas_call x1, Pallas kernels, add_heads(): pl.pallas_call(kernel, in_specs=[pl.BlockSpec(memory_space=pltpu.SMEM)] +...  5.56 us
    ppermute x3, waiting for transfers between devices, shift(): return lax.ppermute(v, 'frm', [(i, i + s) for i in range(n_frm - s)])  5.37 us
    pallas_call x2, Pallas kernels, place(): pl.pallas_call(kernel, in_specs=[pl.BlockSpec(memory_space=pltpu.SMEM)] +...  4.47 us
  transfers between devices with their start and end apart: 26, of which 8 were waited for; matrix products, arithmetic and copies ran while one was open for 0% of the time, Pallas kernels for 20%

profile of v4, /device:TPU:0, one launch (start us, length us, event | category | flops | bytes accessed | tf_op | source)
XLA Modules:
  0.0 127.8 jit_solution(14999426611189038826)
XLA Ops:
  0.0 3.0 %collective-permute-start.1 = (bf16[2,2240,128]{2,1,0:T(8,128)(2,1)}, bf16[2,2240,128]{2,1,0:T(8,128)(2,1)}, u32[]{:S(2)}, u32[]{:S(2)}) collective-permute-start(bf16[2,2240,128]{2,1,0:T(8,128)(2,1)} %bitcast.23), channel_id=1, source_target_pairs={{0,2},{1,3},{2,0},{3,1},{4,6},{5,7},{6,4},{7,5},{8,10},{9,11},{10,... | collective-permute-start | bytes 3440648 | tf_op jit(solution)/shard_map/ppermute | solution.py:304
  3.0 0.0 collective-permute-start
  3.0 0.5 collective-permute-start.3
  3.5 0.1 pad_add_fusion.start_ref
  3.6 1.7 %copy-done.2 = bf16[560,2240]{1,0:T(8,128)(2,1)S(1)} copy-done((bf16[560,2240]{1,0:T(8,128)(2,1)S(1)}, bf16[560,2240]{1,0:T(8,128)(2,1)}, u32[]{:S(2)}) %copy-start.2) | copy-done | bytes 2508824
  5.3 1.4 %cut.1 = (bf16[96,2240]{1,0:T(8,128)(2,1)S(1)}, bf16[48,2240]{1,0:T(8,128)(2,1)S(1)}, bf16[96,2240]{1,0:T(8,128)(2,1)S(1)}) custom-call(s32[3]{0:T(128)S(1)} %pad_add_fusion.start_ref, bf16[560,2240]{1,0:T(8,128)(2,1)S(1)} %copy-done.2), custom_call_target="tpu_custom_call" | custom-call | bytes 2150400 | tf_op jit(solution)/shard_map/cut/pallas_call | solution.py:186
  6.7 0.1 collective-permute-start.22
  6.8 2.0 %collective-permute-start.10 = (bf16[48,2240]{1,0:T(8,128)(2,1)S(1)}, bf16[48,2240]{1,0:T(8,128)(2,1)S(1)}, u32[]{:S(2)}, u32[]{:S(2)}) collective-permute-start(bf16[48,2240]{1,0:T(8,128)(2,1)S(1)} %get-tuple-element.31), channel_id=1, source_target_pairs={{0,2},{1,3},{2,0},{3,1},{4,6},{5,7},{6,4},{7,5},{8,10},{9,11},{10,... | collective-permute-start | bytes 645128 | tf_op jit(solution)/shard_map/ppermute | solution.py:304
  8.8 20.6 %collective-permute-done.1.refs_0_ = bf16[2,2240,128]{2,1,0:T(8,128)(2,1)} collective-permute-done((bf16[2,2240,128]{2,1,0:T(8,128)(2,1)}, bf16[2,2240,128]{2,1,0:T(8,128)(2,1)}, u32[]{:S(2)}, u32[]{:S(2)}) %collective-permute-start.1) | collective-permute-done | bytes 1146912 | tf_op jit(solution)/shard_map/ppermute | solution.py:304
  29.4 0.0 collective-permute-start.2
  29.4 13.3 %collective-permute-done.10.refs_0_ = bf16[48,2240]{1,0:T(8,128)(2,1)S(1)} collective-permute-done((bf16[48,2240]{1,0:T(8,128)(2,1)S(1)}, bf16[48,2240]{1,0:T(8,128)(2,1)S(1)}, u32[]{:S(2)}, u32[]{:S(2)}) %collective-permute-start.10) | collective-permute-done | bytes 215072 | tf_op jit(solution)/shard_map/ppermute | solution.py:304
  42.7 1.8 %collective-permute-start.11 = (bf16[48,2240]{1,0:T(8,128)(2,1)S(1)}, bf16[48,2240]{1,0:T(8,128)(2,1)S(1)}, u32[]{:S(2)}, u32[]{:S(2)}) collective-permute-start(bf16[48,2240]{1,0:T(8,128)(2,1)S(1)} %collective-permute-done.10.refs_0_), channel_id=1, source_target_pairs={{0,16},{16,0},{1,17},{17,1},{2,18},{18,2},{3,19},{19,3},{4,20},{20... | collective-permute-start | bytes 645128 | tf_op jit(solution)/shard_map/ppermute | solution.py:304
  44.4 0.0 collective-permute-done.22.refs_0_
  44.4 1.6 %collective-permute-start.19 = (bf16[48,2240]{1,0:T(8,128)(2,1)S(1)}, bf16[48,2240]{1,0:T(8,128)(2,1)S(1)}, u32[]{:S(2)}, u32[]{:S(2)}) collective-permute-start(bf16[48,2240]{1,0:T(8,128)(2,1)S(1)} %collective-permute-done.10.refs_0_), channel_id=1, source_target_pairs={{0,4},{4,0},{8,12},{12,8},{1,5},{5,1},{9,13},{13,9},{2,6},{6,2},{1... | collective-permute-start | bytes 645128 | tf_op jit(solution)/shard_map/ppermute | solution.py:304
  46.0 3.2 %collective-permute-done.11.refs_2_ = bf16[48,2240]{1,0:T(8,128)(2,1)S(1)} collective-permute-done((bf16[48,2240]{1,0:T(8,128)(2,1)S(1)}, bf16[48,2240]{1,0:T(8,128)(2,1)S(1)}, u32[]{:S(2)}, u32[]{:S(2)}) %collective-permute-start.11) | collective-permute-done | bytes 215072 | tf_op jit(solution)/shard_map/ppermute | solution.py:304
  49.3 1.5 %collective-permute-start.14 = (bf16[96,2240]{1,0:T(8,128)(2,1)S(1)}, bf16[96,2240]{1,0:T(8,128)(2,1)S(1)}, u32[]{:S(2)}, u32[]{:S(2)}) collective-permute-start(bf16[96,2240]{1,0:T(8,128)(2,1)S(1)} %get-tuple-element.32), channel_id=1, source_target_pairs={{0,2},{1,3},{2,0},{3,1},{4,6},{5,7},{6,4},{7,5},{8,10},{9,11},{10,... | collective-permute-start | bytes 1290248 | tf_op jit(solution)/shard_map/ppermute | solution.py:304
  50.7 0.3 reshape.12.refs_2_.refs_1_
  51.1 1.1 collective-permute-done.17.refs_1_
  52.2 0.7 copy-done.22
  52.9 1.5 %collective-permute-start.24 = (bf16[96,2240]{1,0:T(8,128)(2,1)S(1)}, bf16[96,2240]{1,0:T(8,128)(2,1)S(1)}, u32[]{:S(2)}, u32[]{:S(2)}) collective-permute-start(bf16[96,2240]{1,0:T(8,128)(2,1)S(1)} %collective-permute-done.22.refs_0_), channel_id=1, source_target_pairs={{0,16},{16,0},{1,17},{17,1},{2,18},{18,2},{3,19},{19,3},{4,20},{20... | collective-permute-start | bytes 1290248 | tf_op jit(solution)/shard_map/ppermute | solution.py:304
  54.4 5.3 %collective-permute-done.14.refs_6_ = bf16[96,2240]{1,0:T(8,128)(2,1)S(1)} collective-permute-done((bf16[96,2240]{1,0:T(8,128)(2,1)S(1)}, bf16[96,2240]{1,0:T(8,128)(2,1)S(1)}, u32[]{:S(2)}, u32[]{:S(2)}) %collective-permute-start.14) | collective-permute-done | bytes 430112 | tf_op jit(solution)/shard_map/ppermute | solution.py:304
  59.7 1.3 collective-permute-start.15
  61.0 3.2 %copy-done = bf16[2240,3,560]{0,2,1:T(8,128)(2,1)S(1)} copy-done((bf16[2240,3,560]{0,2,1:T(8,128)(2,1)S(1)}, bf16[2240,3,560]{0,2,1:T(8,128)(2,1)}, u32[]{:S(2)}) %copy-start) | copy-done | bytes 7526424
  64.2 6.5 %project.3 = (f32[2,560,112]{2,1,0:T(8,128)S(1)}, bf16[2,560,256]{2,1,0:T(8,128)(2,1)S(1)}) custom-call(bf16[2,2240,128]{2,1,0:T(8,128)(2,1)S(1)} %bitcast.25, bf16[2,2240,128]{2,1,0:T(8,128)(2,1)} %collective-permute-done.3.refs_1_, f32[2240,1]{1,0:T(8,128)S(1)} %reshape.12.refs_2_.refs_1_, bf16[1680,2240]{1,0:T(8,128)(2,1)S(1)} %bitcast.19), custom_call_target="tpu_custom_call" | custom-call | flops 3853516800 | bytes 2293760 | tf_op jit(solution)/shard_map/project/pallas_call | solution.py:95
  70.8 1.6 %collective-permute-start.12 = (bf16[48,2240]{1,0:T(8,128)(2,1)S(1)}, bf16[48,2240]{1,0:T(8,128)(2,1)}, u32[]{:S(2)}, u32[]{:S(2)}) collective-permute-start(bf16[48,2240]{1,0:T(8,128)(2,1)S(1)} %collective-permute-done.11.refs_2_), channel_id=1, source_target_pairs={{0,4},{4,0},{8,12},{12,8},{1,5},{5,1},{9,13},{13,9},{2,6},{6,2},{1... | collective-permute-start | bytes 645128 | tf_op jit(solution)/shard_map/ppermute | solution.py:304
  72.4 0.0 collective-permute-start.20
  72.4 4.5 %project.4 = (f32[2,560,112]{2,1,0:T(8,128)S(1)}, bf16[2,560,128]{2,1,0:T(8,128)(2,1)S(1)}) custom-call(bf16[2,2240,128]{2,1,0:T(8,128)(2,1)} %collective-permute-done.1.refs_0_, f32[2240,1]{1,0:T(8,128)S(1)} %reshape.12.refs_2_.refs_1_, bf16[1680,2240]{1,0:T(8,128)(2,1)S(1)} %bitcast.20, f32[2,560,112]{2,1,0:T(8,128)S(1)} %get-tuple-element.20.refs_3_), custom_call_target="tpu_custom_call" | custom-call | flops 1926758400 | bytes 1146880 | tf_op jit(solution)/shard_map/project/pallas_call | solution.py:95
  77.0 0.0 copy-start.31
  77.0 2.6 %project.5 = (f32[2,560,112]{2,1,0:T(8,128)S(1)}, bf16[560,112]{1,0:T(8,128)(2,1)S(1)}, bf16[2240,256]{1,0:T(8,128)(2,1)S(1)}) custom-call(bf16[2,2240,128]{2,1,0:T(8,128)(2,1)S(1)} %collective-permute-done.2.refs_0_, f32[2240,1]{1,0:T(8,128)S(1)} %reshape.12.refs_2_.refs_1_, bf16[1680,2240]{1,0:T(8,128)(2,1)S(1)} %bitcast.21, ...), custom_call_target="tpu_custom_call" | custom-call | flops 1284505600 | bytes 1146880 | tf_op jit(solution)/shard_map/project/pallas_call | solution.py:95
  79.6 0.0 collective-permute-done.20.refs_5_
  79.6 2.4 %collective-permute-start.4 = (bf16[560,112]{1,0:T(8,128)(2,1)S(1)}, bf16[560,112]{1,0:T(8,128)(2,1)S(1)}, u32[]{:S(2)}, u32[]{:S(2)}) collective-permute-start(bf16[560,112]{1,0:T(8,128)(2,1)S(1)} %get-tuple-element.23), channel_id=1, source_target_pairs={{0,4},{4,8},{8,12},{1,5},{5,9},{9,13},{2,6},{6,10},{10,14},{3,7},{... | collective-permute-start | bytes 376328 | tf_op jit(solution)/shard_map/ppermute | solution.py:307
  82.0 0.0 collective-permute-done.12.refs_0_
  82.0 0.3 collective-permute-start.23
  82.3 4.5 %collective-permute-start.5 = (bf16[560,112]{1,0:T(8,128)(2,1)S(1)}, bf16[560,112]{1,0:T(8,128)(2,1)S(1)}, u32[]{:S(2)}, u32[]{:S(2)}) collective-permute-start(bf16[560,112]{1,0:T(8,128)(2,1)S(1)} %get-tuple-element.23), channel_id=1, source_target_pairs={{0,8},{4,12},{1,9},{5,13},{2,10},{6,14},{3,11},{7,15},{16,24},{20,... | collective-permute-start | bytes 376328 | tf_op jit(solution)/shard_map/ppermute | solution.py:307
  86.8 0.0 collective-permute-done.15.refs_2_
  86.8 0.1 collective-permute-start.21
  86.9 0.5 collective-permute-start.25
  87.4 2.9 %collective-permute-done.5.rest_1_ = bf16[560,112]{1,0:T(8,128)(2,1)S(1)} collective-permute-done((bf16[560,112]{1,0:T(8,128)(2,1)S(1)}, bf16[560,112]{1,0:T(8,128)(2,1)S(1)}, u32[]{:S(2)}, u32[]{:S(2)}) %collective-permute-start.5) | collective-permute-done | bytes 125472 | tf_op jit(solution)/shard_map/ppermute | solution.py:307
  90.3 9.1 %collective-permute-start.6 = (bf16[560,112]{1,0:T(8,128)(2,1)S(1)}, bf16[560,112]{1,0:T(8,128)(2,1)S(1)}, u32[]{:S(2)}, u32[]{:S(2)}) collective-permute-start(bf16[560,112]{1,0:T(8,128)(2,1)S(1)} %get-tuple-element.23), channel_id=1, source_target_pairs={{0,12},{1,13},{2,14},{3,15},{16,28},{17,29},{18,30},{19,31}} | collective-permute-start | bytes 376328 | tf_op jit(solution)/shard_map/ppermute | solution.py:307
  99.4 0.1 reshape.13.gain_ref
  99.5 2.5 %collective-permute-done.6.rest_2_ = bf16[560,112]{1,0:T(8,128)(2,1)S(1)} collective-permute-done((bf16[560,112]{1,0:T(8,128)(2,1)S(1)}, bf16[560,112]{1,0:T(8,128)(2,1)S(1)}, u32[]{:S(2)}, u32[]{:S(2)}) %collective-permute-start.6) | collective-permute-done | bytes 125472 | tf_op jit(solution)/shard_map/ppermute | solution.py:307
  102.0 0.0 collective-permute-start.16
  102.0 0.8 query.1.rest_5_
  102.9 2.2 %attend.1 = (bf16[2,560,128]{2,1,0:T(8,128)(2,1)S(1)}, bf16[2,560,128]{2,1,0:T(8,128)(2,1)}, bf16[2,560,128]{2,1,0:T(8,128)(2,1)}, bf16[2,560,128]{2,1,0:T(8,128)(2,1)}) custom-call(s32[2]{0:T(128)S(1)} %copy-done.28, f32[2,560,112]{2,1,0:T(8,128)S(1)} %get-tuple-element.22.state_ref, f32[560,1]{1,0:T(8,128)S(1)} %reshape.13.gain_ref, ...), custom_call_target="tpu_custom_call" | custom-call | flops 128450560 | bytes 2293760 | tf_op jit(solution)/shard_map/attend/pallas_call | solution.py:161
  105.1 0.7 copy-done.14
  105.8 0.0 collective-permute-done.23.refs_1_
  105.8 0.8 copy-done.8
  106.5 0.5 collective-permute-start.7
  107.1 0.8 copy-done.10
  107.9 1.5 %collective-permute-start.8 = (bf16[2,560,128]{2,1,0:T(8,128)(2,1)}, bf16[2,560,128]{2,1,0:T(8,128)(2,1)}, u32[]{:S(2)}, u32[]{:S(2)}) collective-permute-start(bf16[2,560,128]{2,1,0:T(8,128)(2,1)} %get-tuple-element.29), channel_id=1, source_target_pairs={{0,2},{1,3},{2,0},{3,1},{4,6},{5,7},{6,4},{7,5},{8,10},{9,11},{10,... | collective-permute-start | bytes 860168 | tf_op jit(solution)/shard_map/ppermute | solution.py:304
  109.3 0.0 collective-permute-done.25.refs_3_
  109.3 0.8 copy-done.12
  110.1 0.0 collective-permute-start.9
  110.1 0.7 collective-permute-start.13
  110.8 0.1 stack.61.start_ref
  110.9 1.0 copy-done.7
  111.9 1.0 copy-done.9
  112.9 1.0 copy-done.13
  114.0 1.6 %place.2.refs_8_ = bf16[1120,2240]{1,0:T(8,128)(2,1)S(1)} custom-call(s32[12]{0:T(128)S(1)} %stack.61.start_ref, bf16[96,2240]{1,0:T(8,128)(2,1)S(1)} %collective-permute-done.22.refs_0_, bf16[96,2240]{1,0:T(8,128)(2,1)S(1)} %copy-done.9, bf16[96,2240]{1,0:T(8,128)(2,1)S(1)} %copy-done.7, bf16[96,2240]{1,0:T(8,128)(2,1)S(1)} %copy-done.13), custom_call_target="tpu_custom_call" | custom-call | bytes 3440640 | tf_op jit(solution)/shard_map/place/pallas_call | solution.py:216
  115.7 0.0 copy-start.3
  115.7 2.9 %place.3.refs_4_ = bf16[1120,2240]{1,0:T(8,128)(2,1)S(1)} custom-call(s32[12]{0:T(128)S(1)} %stack.61.start_ref, bf16[48,2240]{1,0:T(8,128)(2,1)S(1)} %copy-done.17, bf16[48,2240]{1,0:T(8,128)(2,1)S(1)} %copy-done.23, bf16[48,2240]{1,0:T(8,128)(2,1)S(1)} %copy-done.19, bf16[48,2240]{1,0:T(8,128)(2,1)S(1)} %copy-done.25, ...), custom_call_target="tpu_custom_call", output_to_operand_aliasing={{}: (9, {})} | custom-call | bytes 4300800 | tf_op jit(solution)/shard_map/place/pallas_call | solution.py:216
  118.6 3.0 %mix.1.total_ref = f32[256,2240]{1,0:T(8,128)S(1)} custom-call(bf16[560,2240]{1,0:T(8,128)(2,1)S(1)} %copy-done.3, bf16[560,2240]{1,0:T(8,128)(2,1)S(1)} %collective-permute-done.refs_1_, bf16[2,560,128]{2,1,0:T(8,128)(2,1)S(1)} %copy-done.15, bf16[2,560,128]{2,1,0:T(8,128)(2,1)} %collective-permute-done.7.refs_3_), custom_call_target="tpu_custom_call" | custom-call | flops 1284505600 | bytes 5017600 | tf_op jit(solution)/shard_map/mix/pallas_call | solution.py:248
  121.6 0.5 collective-permute-done.9.y_ref
  122.1 5.6 %add_heads.1 = (bf16[2,2240,128]{2,1,0:T(8,128)(2,1)}, bf16[1120,2240]{1,0:T(8,128)(2,1)S(1)}) custom-call(s32[12]{0:T(128)S(1)} %stack.61.start_ref, f32[256,2240]{1,0:T(8,128)S(1)} %mix.1.total_ref, bf16[2,560,128]{2,1,0:T(8,128)(2,1)} %collective-permute-done.8.x_ref, ...), custom_call_target="tpu_custom_call", output_to_operand_aliasing={{1}: (8, {})} | custom-call | flops 1284505600 | bytes 5017600 | tf_op jit(solution)/shard_map/add_heads/pallas_call | solution.py:285
  (66 shorter events, 0.1 us)
Async XLA Ops:
  0.0 50.7 %copy-start.30 = (f32[2240]{0:T(1024)S(1)}, f32[2240]{0:T(1024)}, u32[]{:S(2)}) copy-start(f32[2240]{0:T(1024)} %param.7) | copy-start | bytes 26884
  0.0 29.4 %collective-permute-start.1 = (bf16[2,2240,128]{2,1,0:T(8,128)(2,1)}, bf16[2,2240,128]{2,1,0:T(8,128)(2,1)}, u32[]{:S(2)}, u32[]{:S(2)}) collective-permute-start(bf16[2,2240,128]{2,1,0:T(8,128)(2,1)} %bitcast.23), channel_id=1, source_target_pairs={{0,2},{1,3},{2,0},{3,1},{4,6},{5,7},{6,4},{7,5},{8,10},{9,11},{10,... | collective-permute-start | bytes 3440648 | tf_op jit(solution)/shard_map/ppermute | solution.py:304
  3.0 107.2 %collective-permute-start = (bf16[560,2240]{1,0:T(8,128)(2,1)}, bf16[560,2240]{1,0:T(8,128)(2,1)S(1)}, u32[]{:S(2)}, u32[]{:S(2)}) collective-permute-start(bf16[560,2240]{1,0:T(8,128)(2,1)} %src.1), channel_id=1, source_target_pairs={{0,1},{1,0},{2,3},{3,2},{4,5},{5,4},{6,7},{7,6},{8,9},{9,8},{10,11... | collective-permute-start | bytes 7526408 | tf_op jit(solution)/shard_map/ppermute | solution.py:304
  3.0 56.8 %collective-permute-start.3 = (bf16[2,2240,128]{2,1,0:T(8,128)(2,1)}, bf16[2,2240,128]{2,1,0:T(8,128)(2,1)}, u32[]{:S(2)}, u32[]{:S(2)}) collective-permute-start(bf16[2,2240,128]{2,1,0:T(8,128)(2,1)} %bitcast.24), channel_id=1, source_target_pairs={{0,1},{1,0},{2,3},{3,2},{4,5},{5,4},{6,7},{7,6},{8,9},{9,8},{10,11... | collective-permute-start | bytes 3440648 | tf_op jit(solution)/shard_map/ppermute | solution.py:304
  3.6 1.7 %copy-start.2 = (bf16[560,2240]{1,0:T(8,128)(2,1)S(1)}, bf16[560,2240]{1,0:T(8,128)(2,1)}, u32[]{:S(2)}) copy-start(bf16[560,2240]{1,0:T(8,128)(2,1)} %src.1) | copy-start | bytes 7526404
  5.3 55.7 %copy-start.29 = (bf16[128,2,2240]{0,2,1:T(8,128)(2,1)S(1)}, bf16[128,2,2240]{0,2,1:T(8,128)(2,1)}, u32[]{:S(2)}) copy-start(bf16[128,2,2240]{0,2,1:T(8,128)(2,1)} %param.6) | copy-start | bytes 3440644
  6.7 37.8 %collective-permute-start.22 = (bf16[96,2240]{1,0:T(8,128)(2,1)S(1)}, bf16[96,2240]{1,0:T(8,128)(2,1)S(1)}, u32[]{:S(2)}, u32[]{:S(2)}) collective-permute-start(bf16[96,2240]{1,0:T(8,128)(2,1)S(1)} %get-tuple-element.33), channel_id=1, source_target_pairs={{0,2},{1,3},{2,0},{3,1},{4,6},{5,7},{6,4},{7,5},{8,10},{9,11},{10,... | collective-permute-start | bytes 1290248 | tf_op jit(solution)/shard_map/ppermute | solution.py:304
  6.8 35.9 %collective-permute-start.10 = (bf16[48,2240]{1,0:T(8,128)(2,1)S(1)}, bf16[48,2240]{1,0:T(8,128)(2,1)S(1)}, u32[]{:S(2)}, u32[]{:S(2)}) collective-permute-start(bf16[48,2240]{1,0:T(8,128)(2,1)S(1)} %get-tuple-element.31), channel_id=1, source_target_pairs={{0,2},{1,3},{2,0},{3,1},{4,6},{5,7},{6,4},{7,5},{8,10},{9,11},{10,... | collective-permute-start | bytes 645128 | tf_op jit(solution)/shard_map/ppermute | solution.py:304
  29.4 43.0 %collective-permute-start.2 = (bf16[2,2240,128]{2,1,0:T(8,128)(2,1)}, bf16[2,2240,128]{2,1,0:T(8,128)(2,1)S(1)}, u32[]{:S(2)}, u32[]{:S(2)}) collective-permute-start(bf16[2,2240,128]{2,1,0:T(8,128)(2,1)} %collective-permute-done.1.refs_0_), channel_id=1, source_target_pairs={{0,1},{1,0},{2,3},{3,2},{4,5},{5,4},{6,7},{7,6},{8,9},{9,8},{10,11... | collective-permute-start | bytes 3440648 | tf_op jit(solution)/shard_map/ppermute | solution.py:304
  42.7 18.4 %copy-start.16 = (bf16[48,2240]{1,0:T(8,128)(2,1)}, bf16[48,2240]{1,0:T(8,128)(2,1)S(1)}, u32[]{:S(2)}) copy-start(bf16[48,2240]{1,0:T(8,128)(2,1)S(1)} %collective-permute-done.10.refs_0_) | copy-start | bytes 645124
  42.7 6.6 %collective-permute-start.11 = (bf16[48,2240]{1,0:T(8,128)(2,1)S(1)}, bf16[48,2240]{1,0:T(8,128)(2,1)S(1)}, u32[]{:S(2)}, u32[]{:S(2)}) collective-permute-start(bf16[48,2240]{1,0:T(8,128)(2,1)S(1)} %collective-permute-done.10.refs_0_), channel_id=1, source_target_pairs={{0,16},{16,0},{1,17},{17,1},{2,18},{18,2},{3,19},{19,3},{4,20},{20... | collective-permute-start | bytes 645128 | tf_op jit(solution)/shard_map/ppermute | solution.py:304
  44.4 6.3 %collective-permute-start.19 = (bf16[48,2240]{1,0:T(8,128)(2,1)S(1)}, bf16[48,2240]{1,0:T(8,128)(2,1)S(1)}, u32[]{:S(2)}, u32[]{:S(2)}) collective-permute-start(bf16[48,2240]{1,0:T(8,128)(2,1)S(1)} %collective-permute-done.10.refs_0_), channel_id=1, source_target_pairs={{0,4},{4,0},{8,12},{12,8},{1,5},{5,1},{9,13},{13,9},{2,6},{6,2},{1... | collective-permute-start | bytes 645128 | tf_op jit(solution)/shard_map/ppermute | solution.py:304
  49.3 21.5 %copy-start.18 = (bf16[48,2240]{1,0:T(8,128)(2,1)}, bf16[48,2240]{1,0:T(8,128)(2,1)S(1)}, u32[]{:S(2)}) copy-start(bf16[48,2240]{1,0:T(8,128)(2,1)S(1)} %collective-permute-done.11.refs_2_) | copy-start | bytes 645124
  49.3 10.5 %collective-permute-start.14 = (bf16[96,2240]{1,0:T(8,128)(2,1)S(1)}, bf16[96,2240]{1,0:T(8,128)(2,1)S(1)}, u32[]{:S(2)}, u32[]{:S(2)}) collective-permute-start(bf16[96,2240]{1,0:T(8,128)(2,1)S(1)} %get-tuple-element.32), channel_id=1, source_target_pairs={{0,2},{1,3},{2,0},{3,1},{4,6},{5,7},{6,4},{7,5},{8,10},{9,11},{10,... | collective-permute-start | bytes 1290248 | tf_op jit(solution)/shard_map/ppermute | solution.py:304
  50.7 21.7 %copy-start.20 = (bf16[48,2240]{1,0:T(8,128)(2,1)}, bf16[48,2240]{1,0:T(8,128)(2,1)S(1)}, u32[]{:S(2)}) copy-start(bf16[48,2240]{1,0:T(8,128)(2,1)S(1)} %collective-permute-done.19.refs_4_) | copy-start | bytes 645124
  50.7 1.5 %collective-permute-start.17 = (bf16[48,2240]{1,0:T(8,128)(2,1)S(1)}, bf16[48,2240]{1,0:T(8,128)(2,1)S(1)}, u32[]{:S(2)}, u32[]{:S(2)}) collective-permute-start(bf16[48,2240]{1,0:T(8,128)(2,1)S(1)} %collective-permute-done.10.refs_0_), channel_id=1, source_target_pairs={{0,1},{1,0},{2,3},{3,2},{4,5},{5,4},{6,7},{7,6},{8,9},{9,8},{10,11... | collective-permute-start | bytes 645128 | tf_op jit(solution)/shard_map/ppermute | solution.py:304
  52.2 0.7 copy-start.22
  52.9 29.4 %collective-permute-start.24 = (bf16[96,2240]{1,0:T(8,128)(2,1)S(1)}, bf16[96,2240]{1,0:T(8,128)(2,1)S(1)}, u32[]{:S(2)}, u32[]{:S(2)}) collective-permute-start(bf16[96,2240]{1,0:T(8,128)(2,1)S(1)} %collective-permute-done.22.refs_0_), channel_id=1, source_target_pairs={{0,16},{16,0},{1,17},{17,1},{2,18},{18,2},{3,19},{19,3},{4,20},{20... | collective-permute-start | bytes 1290248 | tf_op jit(solution)/shard_map/ppermute | solution.py:304
  59.7 27.0 %copy-start.4 = (bf16[96,2240]{1,0:T(8,128)(2,1)}, bf16[96,2240]{1,0:T(8,128)(2,1)S(1)}, u32[]{:S(2)}) copy-start(bf16[96,2240]{1,0:T(8,128)(2,1)S(1)} %collective-permute-done.14.refs_6_) | copy-start | bytes 1290244
  59.7 11.0 %collective-permute-start.18 = (bf16[48,2240]{1,0:T(8,128)(2,1)S(1)}, bf16[48,2240]{1,0:T(8,128)(2,1)S(1)}, u32[]{:S(2)}, u32[]{:S(2)}) collective-permute-start(bf16[48,2240]{1,0:T(8,128)(2,1)S(1)} %collective-permute-done.11.refs_2_), channel_id=1, source_target_pairs={{0,1},{1,0},{2,3},{3,2},{4,5},{5,4},{6,7},{7,6},{8,9},{9,8},{10,11... | collective-permute-start | bytes 645128 | tf_op jit(solution)/shard_map/ppermute | solution.py:304
  59.7 27.0 %collective-permute-start.15 = (bf16[96,2240]{1,0:T(8,128)(2,1)S(1)}, bf16[96,2240]{1,0:T(8,128)(2,1)S(1)}, u32[]{:S(2)}, u32[]{:S(2)}) collective-permute-start(bf16[96,2240]{1,0:T(8,128)(2,1)S(1)} %collective-permute-done.14.refs_6_), channel_id=1, source_target_pairs={{0,16},{16,0},{1,17},{17,1},{2,18},{18,2},{3,19},{19,3},{4,20},{20... | collective-permute-start | bytes 1290248 | tf_op jit(solution)/shard_map/ppermute | solution.py:304
  61.0 3.2 %copy-start = (bf16[2240,3,560]{0,2,1:T(8,128)(2,1)S(1)}, bf16[2240,3,560]{0,2,1:T(8,128)(2,1)}, u32[]{:S(2)}) copy-start(bf16[2240,3,560]{0,2,1:T(8,128)(2,1)} %param.8) | copy-start | bytes 22579204
  64.2 8.2 %copy-start.1 = (bf16[2240,3,560]{0,2,1:T(8,128)(2,1)S(1)}, bf16[2240,3,560]{0,2,1:T(8,128)(2,1)}, u32[]{:S(2)}) copy-start(bf16[2240,3,560]{0,2,1:T(8,128)(2,1)} %param.8) | copy-start | bytes 22579204
  70.8 6.2 %copy-start.24 = (bf16[48,2240]{1,0:T(8,128)(2,1)}, bf16[48,2240]{1,0:T(8,128)(2,1)S(1)}, u32[]{:S(2)}) copy-start(bf16[48,2240]{1,0:T(8,128)(2,1)S(1)} %collective-permute-done.18.refs_3_) | copy-start | bytes 645124
  70.8 11.2 %collective-permute-start.12 = (bf16[48,2240]{1,0:T(8,128)(2,1)S(1)}, bf16[48,2240]{1,0:T(8,128)(2,1)}, u32[]{:S(2)}, u32[]{:S(2)}) collective-permute-start(bf16[48,2240]{1,0:T(8,128)(2,1)S(1)} %collective-permute-done.11.refs_2_), channel_id=1, source_target_pairs={{0,4},{4,0},{8,12},{12,8},{1,5},{5,1},{9,13},{13,9},{2,6},{6,2},{1... | collective-permute-start | bytes 645128 | tf_op jit(solution)/shard_map/ppermute | solution.py:304
  72.4 7.2 %collective-permute-start.20 = (bf16[48,2240]{1,0:T(8,128)(2,1)S(1)}, bf16[48,2240]{1,0:T(8,128)(2,1)S(1)}, u32[]{:S(2)}, u32[]{:S(2)}) collective-permute-start(bf16[48,2240]{1,0:T(8,128)(2,1)S(1)} %collective-permute-done.19.refs_4_), channel_id=1, source_target_pairs={{0,1},{1,0},{2,3},{3,2},{4,5},{5,4},{6,7},{7,6},{8,9},{9,8},{10,11... | collective-permute-start | bytes 645128 | tf_op jit(solution)/shard_map/ppermute | solution.py:304
  77.0 22.4 %copy-start.31 = (f32[560]{0:T(1024)S(1)}, f32[560]{0:T(1024)}, u32[]{:S(2)}) copy-start(f32[560]{0:T(1024)} %param.9) | copy-start | bytes 6724
  79.6 23.3 %copy-start.26 = (bf16[48,2240]{1,0:T(8,128)(2,1)}, bf16[48,2240]{1,0:T(8,128)(2,1)S(1)}, u32[]{:S(2)}) copy-start(bf16[48,2240]{1,0:T(8,128)(2,1)S(1)} %collective-permute-done.20.refs_5_) | copy-start | bytes 645124
  79.6 7.3 %collective-permute-start.4 = (bf16[560,112]{1,0:T(8,128)(2,1)S(1)}, bf16[560,112]{1,0:T(8,128)(2,1)S(1)}, u32[]{:S(2)}, u32[]{:S(2)}) collective-permute-start(bf16[560,112]{1,0:T(8,128)(2,1)S(1)} %get-tuple-element.23), channel_id=1, source_target_pairs={{0,4},{4,8},{8,12},{1,5},{5,9},{9,13},{2,6},{6,10},{10,14},{3,7},{... | collective-permute-start | bytes 376328 | tf_op jit(solution)/shard_map/ppermute | solution.py:307
  82.0 23.8 %collective-permute-start.23 = (bf16[96,2240]{1,0:T(8,128)(2,1)S(1)}, bf16[96,2240]{1,0:T(8,128)(2,1)S(1)}, u32[]{:S(2)}, u32[]{:S(2)}) collective-permute-start(bf16[96,2240]{1,0:T(8,128)(2,1)S(1)} %collective-permute-done.22.refs_0_), channel_id=1, source_target_pairs={{0,1},{1,0},{2,3},{3,2},{4,5},{5,4},{6,7},{7,6},{8,9},{9,8},{10,11... | collective-permute-start | bytes 1290248 | tf_op jit(solution)/shard_map/ppermute | solution.py:304
  82.3 20.6 %copy-start.6 = (bf16[96,2240]{1,0:T(8,128)(2,1)}, bf16[96,2240]{1,0:T(8,128)(2,1)S(1)}, u32[]{:S(2)}) copy-start(bf16[96,2240]{1,0:T(8,128)(2,1)S(1)} %collective-permute-done.24.refs_2_) | copy-start | bytes 1290244
  82.3 8.0 %collective-permute-start.5 = (bf16[560,112]{1,0:T(8,128)(2,1)S(1)}, bf16[560,112]{1,0:T(8,128)(2,1)S(1)}, u32[]{:S(2)}, u32[]{:S(2)}) collective-permute-start(bf16[560,112]{1,0:T(8,128)(2,1)S(1)} %get-tuple-element.23), channel_id=1, source_target_pairs={{0,8},{4,12},{1,9},{5,13},{2,10},{6,14},{3,11},{7,15},{16,24},{20,... | collective-permute-start | bytes 376328 | tf_op jit(solution)/shard_map/ppermute | solution.py:307
  86.8 20.3 %collective-permute-start.21 = (bf16[96,2240]{1,0:T(8,128)(2,1)S(1)}, bf16[96,2240]{1,0:T(8,128)(2,1)S(1)}, u32[]{:S(2)}, u32[]{:S(2)}) collective-permute-start(bf16[96,2240]{1,0:T(8,128)(2,1)S(1)} %collective-permute-done.14.refs_6_), channel_id=1, source_target_pairs={{0,1},{1,0},{2,3},{3,2},{4,5},{5,4},{6,7},{7,6},{8,9},{9,8},{10,11... | collective-permute-start | bytes 1290248 | tf_op jit(solution)/shard_map/ppermute | solution.py:304
  86.9 22.5 %collective-permute-start.25 = (bf16[96,2240]{1,0:T(8,128)(2,1)S(1)}, bf16[96,2240]{1,0:T(8,128)(2,1)S(1)}, u32[]{:S(2)}, u32[]{:S(2)}) collective-permute-start(bf16[96,2240]{1,0:T(8,128)(2,1)S(1)} %collective-permute-done.24.refs_2_), channel_id=1, source_target_pairs={{0,1},{1,0},{2,3},{3,2},{4,5},{5,4},{6,7},{7,6},{8,9},{9,8},{10,11... | collective-permute-start | bytes 1290248 | tf_op jit(solution)/shard_map/ppermute | solution.py:304
  90.3 11.7 %collective-permute-start.6 = (bf16[560,112]{1,0:T(8,128)(2,1)S(1)}, bf16[560,112]{1,0:T(8,128)(2,1)S(1)}, u32[]{:S(2)}, u32[]{:S(2)}) collective-permute-start(bf16[560,112]{1,0:T(8,128)(2,1)S(1)} %get-tuple-element.23), channel_id=1, source_target_pairs={{0,12},{1,13},{2,14},{3,15},{16,28},{17,29},{18,30},{19,31}} | collective-permute-start | bytes 376328 | tf_op jit(solution)/shard_map/ppermute | solution.py:307
  102.0 19.6 %collective-permute-start.16 = (bf16[96,2240]{1,0:T(8,128)(2,1)S(1)}, bf16[96,2240]{1,0:T(8,128)(2,1)}, u32[]{:S(2)}, u32[]{:S(2)}) collective-permute-start(bf16[96,2240]{1,0:T(8,128)(2,1)S(1)} %collective-permute-done.15.refs_2_), channel_id=1, source_target_pairs={{0,1},{1,0},{2,3},{3,2},{4,5},{5,4},{6,7},{7,6},{8,9},{9,8},{10,11... | collective-permute-start | bytes 1290248 | tf_op jit(solution)/shard_map/ppermute | solution.py:304
  102.0 0.9 copy-start.28
  105.1 0.7 copy-start.14
  105.8 0.8 copy-start.8
  106.5 12.0 %collective-permute-start.7 = (bf16[2,560,128]{2,1,0:T(8,128)(2,1)}, bf16[2,560,128]{2,1,0:T(8,128)(2,1)}, u32[]{:S(2)}, u32[]{:S(2)}) collective-permute-start(bf16[2,560,128]{2,1,0:T(8,128)(2,1)} %get-tuple-element.28), channel_id=1, source_target_pairs={{0,1},{1,0},{2,3},{3,2},{4,5},{5,4},{6,7},{7,6},{8,9},{9,8},{10,11... | collective-permute-start | bytes 860168 | tf_op jit(solution)/shard_map/ppermute | solution.py:304
  107.0 0.8 copy-start.10
  107.9 13.8 %collective-permute-start.8 = (bf16[2,560,128]{2,1,0:T(8,128)(2,1)}, bf16[2,560,128]{2,1,0:T(8,128)(2,1)}, u32[]{:S(2)}, u32[]{:S(2)}) collective-permute-start(bf16[2,560,128]{2,1,0:T(8,128)(2,1)} %get-tuple-element.29), channel_id=1, source_target_pairs={{0,2},{1,3},{2,0},{3,1},{4,6},{5,7},{6,4},{7,5},{8,10},{9,11},{10,... | collective-permute-start | bytes 860168 | tf_op jit(solution)/shard_map/ppermute | solution.py:304
  109.3 0.8 copy-start.12
  110.1 12.0 %collective-permute-start.9 = (bf16[2,560,128]{2,1,0:T(8,128)(2,1)}, bf16[2,560,128]{2,1,0:T(8,128)(2,1)}, u32[]{:S(2)}, u32[]{:S(2)}) collective-permute-start(bf16[2,560,128]{2,1,0:T(8,128)(2,1)} %get-tuple-element.30), channel_id=1, source_target_pairs={{0,3},{1,2},{2,1},{3,0},{4,7},{5,6},{6,5},{7,4},{8,11},{9,10},{10,... | collective-permute-start | bytes 860168 | tf_op jit(solution)/shard_map/ppermute | solution.py:304
  110.1 11.5 %collective-permute-start.13 = (bf16[48,2240]{1,0:T(8,128)(2,1)}, bf16[48,2240]{1,0:T(8,128)(2,1)}, u32[]{:S(2)}, u32[]{:S(2)}) collective-permute-start(bf16[48,2240]{1,0:T(8,128)(2,1)} %collective-permute-done.12.refs_0_), channel_id=1, source_target_pairs={{0,1},{1,0},{2,3},{3,2},{4,5},{5,4},{6,7},{7,6},{8,9},{9,8},{10,11... | collective-permute-start | bytes 645128 | tf_op jit(solution)/shard_map/ppermute | solution.py:304
  110.9 1.0 copy-start.7
  111.9 1.0 copy-start.9
  112.9 1.0 copy-start.13
  113.9 1.7 %copy-start.5 = (bf16[96,2240]{1,0:T(8,128)(2,1)S(1)}, bf16[96,2240]{1,0:T(8,128)(2,1)}, u32[]{:S(2)}) copy-start(bf16[96,2240]{1,0:T(8,128)(2,1)} %copy-done.4) | copy-start | bytes 1290244
  113.9 1.7 %copy-start.11 = (bf16[96,2240]{1,0:T(8,128)(2,1)S(1)}, bf16[96,2240]{1,0:T(8,128)(2,1)}, u32[]{:S(2)}) copy-start(bf16[96,2240]{1,0:T(8,128)(2,1)} %copy-done.10) | copy-start | bytes 1290244
  113.9 1.7 %copy-start.17 = (bf16[48,2240]{1,0:T(8,128)(2,1)S(1)}, bf16[48,2240]{1,0:T(8,128)(2,1)}, u32[]{:S(2)}) copy-start(bf16[48,2240]{1,0:T(8,128)(2,1)} %copy-done.16) | copy-start | bytes 645124
  113.9 1.7 %copy-start.19 = (bf16[48,2240]{1,0:T(8,128)(2,1)S(1)}, bf16[48,2240]{1,0:T(8,128)(2,1)}, u32[]{:S(2)}) copy-start(bf16[48,2240]{1,0:T(8,128)(2,1)} %copy-done.18) | copy-start | bytes 645124
  113.9 1.7 %copy-start.21 = (bf16[48,2240]{1,0:T(8,128)(2,1)S(1)}, bf16[48,2240]{1,0:T(8,128)(2,1)}, u32[]{:S(2)}) copy-start(bf16[48,2240]{1,0:T(8,128)(2,1)} %copy-done.20) | copy-start | bytes 645124
  113.9 1.7 %copy-start.23 = (bf16[48,2240]{1,0:T(8,128)(2,1)S(1)}, bf16[48,2240]{1,0:T(8,128)(2,1)}, u32[]{:S(2)}) copy-start(bf16[48,2240]{1,0:T(8,128)(2,1)} %copy-done.22) | copy-start | bytes 645124
  114.0 1.7 %copy-start.25 = (bf16[48,2240]{1,0:T(8,128)(2,1)S(1)}, bf16[48,2240]{1,0:T(8,128)(2,1)}, u32[]{:S(2)}) copy-start(bf16[48,2240]{1,0:T(8,128)(2,1)} %copy-done.24) | copy-start | bytes 645124
  114.0 1.7 %copy-start.27 = (bf16[48,2240]{1,0:T(8,128)(2,1)S(1)}, bf16[48,2240]{1,0:T(8,128)(2,1)}, u32[]{:S(2)}) copy-start(bf16[48,2240]{1,0:T(8,128)(2,1)} %copy-done.26) | copy-start | bytes 645124
  115.7 2.9 %copy-start.3 = (bf16[560,2240]{1,0:T(8,128)(2,1)S(1)}, bf16[560,2240]{1,0:T(8,128)(2,1)}, u32[]{:S(2)}) copy-start(bf16[560,2240]{1,0:T(8,128)(2,1)} %src.1) | copy-start | bytes 7526404
  115.7 2.9 %copy-start.15 = (bf16[2,560,128]{2,1,0:T(8,128)(2,1)S(1)}, bf16[2,560,128]{2,1,0:T(8,128)(2,1)}, u32[]{:S(2)}) copy-start(bf16[2,560,128]{2,1,0:T(8,128)(2,1)} %copy-done.14) | copy-start | bytes 860164
